TPU v7x, 128 devices: a whole 4x4x4 slice. The times are simulated.
128 devices in a mesh: blk: 32 (over y, z, core), sub: 4 (over x).
Axes of the slice: x: 4, y: 4, z: 4, core: 2. Of those that a mesh axis runs over, the one named last changes fastest.
Arguments:
- pressure: float32 [2, 8, 8, 8, 65536], P(None, None, None, None, ('blk', 'sub')), may hold values from -6 to 6
- right_side: float32 [2, 8, 8, 8, 65536], P(None, None, None, None, ('blk', 'sub')), may hold values from -6 to 6
- geometry: float32 [6, 8, 8, 8, 65536], P(None, None, None, None, ('blk', 'sub')), may hold values from -0.03 to 0.08, as said below
- face_weight: float32 [64, 6, 65536], P(None, None, ('blk', 'sub')), may hold values from 0.004 to 0.02
- face_metric: float32 [64, 6, 65536], P(None, None, ('blk', 'sub')), may hold values from 0.5 to 2
- cross_slots: int32 [5, 128, 576], P(None, ('blk', 'sub')), may hold values from 0 to 511, as said below
- local_pairs: int32 [5, 65536], P(None, ('blk', 'sub')), may hold values from 0 to 511, as said below
- coarse_map: int32 [65536], P(('blk', 'sub')), may hold values from 0 to 255, as said below
- coarse_inverse: float32 [8, 8, 8192], P(None, None, 'blk'), may hold values from -0.12 to 0.48, as said below
Outputs:
- residual: float32 [2, 8, 8, 8, 65536], P(None, None, None, None, ('blk', 'sub'))
- corrected: float32 [2, 8, 8, 8, 65536], P(None, None, None, None, ('blk', 'sub'))
Inputs may be any that keep to these rules, and one draw needn't show every extreme that they name: `cross_slots`: Rows: local element index, face 0 to 5 (low or high end of node axis 1, 2, 3), live flag, owner flag, orientation code 0 to 7. Columns come in 9 blocks of 64, block k for neighbour k of the device grid; block 4 (the device itself) has no live slot. The slot of device d at neighbour k, place c and the slot of neighbour k at column (8 - k) * 64 + c describe the same pair: equal live flags and codes, opposite owner flags. Within a block the live slots come first; every device shares exactly 64 pairs with some neighbour. Every (element, face) of a device appears at most once among its slots, live or not, and its local pairs. `local_pairs`: the columns of device d hold 512 pairs of its own elements; see cross_slots for the faces used. `coarse_map`: each coarse cell of a Morton block holds exactly 8 elements of that block. `geometry`: at each node the 3 x 3 matrix of the six rows is symmetric positive definite. `coarse_inverse`: each block is symmetric.
All inputs are finite; a program needn't handle non-finite values.
Results may differ from a plain program's by a relative error of at most 0.00016.
Values sent between devices are 32-bit elements; how exact they have to be, the bound alone decides.
A program may use at most 128 MiB of HBM per device.

v0:
```python
import jax
import jax.numpy as jnp
import numpy as np
from jax import lax
from jax.sharding import PartitionSpec as P

precise = lax.Precision.HIGHEST


def extended(cells, sides, width):
    for axis, dim in sides:
        count = lax.axis_size(axis)
        head = lax.slice_in_dim(cells, 0, width, axis=dim)
        tail = lax.slice_in_dim(cells, cells.shape[dim] - width, cells.shape[dim], axis=dim)
        cells = jnp.concatenate(
            [
                lax.ppermute(tail, axis, [(i, (i + 1) % count) for i in range(count)]),
                cells,
                lax.ppermute(head, axis, [((i + 1) % count, i) for i in range(count)]),
            ],
            axis=dim,
        )
    return cells


def node_points():
    positive = [0.2092992179024789, 0.5917001814331423, 0.8717401485096066, 1.0]
    return np.array(sorted([-entry_value for entry_value in positive] + positive))


def derivative_matrix(node_count):
    points = node_points()
    weights = np.array(
        [
            1.0
            / np.prod(
                [
                    points[row_index] - points[col_index]
                    for col_index in range(node_count)
                    if col_index != row_index
                ]
            )
            for row_index in range(node_count)
        ]
    )
    matrix = np.zeros((node_count, node_count))
    for row_index in range(node_count):
        for col_index in range(node_count):
            if row_index != col_index:
                matrix[row_index, col_index] = (
                    weights[col_index]
                    / weights[row_index]
                    / (points[row_index] - points[col_index])
                )
        matrix[row_index, row_index] = -np.sum(matrix[row_index])
    return matrix


def edge_matrix(node_count):
    derivative = derivative_matrix(node_count)
    edge_rows = np.zeros((4, node_count))
    edge_rows[0, 0] = 1.0
    edge_rows[1] = -derivative[0]
    edge_rows[2, node_count - 1] = 1.0
    edge_rows[3] = derivative[node_count - 1]
    return edge_rows


def prolong_matrix():
    points = node_points()
    return np.stack([(1.0 - points) / 2.0, (1.0 + points) / 2.0], axis=1)


def orient_tables(node_count):
    forward = np.zeros((8, node_count * node_count), np.int32)
    for orient_code in range(8):
        for first_axis in range(node_count):
            for second_axis in range(node_count):
                if orient_code & 4:
                    source_one, source_two = (second_axis, first_axis)
                else:
                    source_one, source_two = (first_axis, second_axis)
                if orient_code & 1:
                    source_one = node_count - 1 - source_one
                if orient_code & 2:
                    source_two = node_count - 1 - source_two
                forward[orient_code, first_axis * node_count + second_axis] = (
                    source_one * node_count + source_two
                )
    inverse = np.argsort(forward, axis=1).astype(np.int32)
    return (forward, inverse)


def perm_matrices(table):
    face_size = table.shape[1]
    identity = np.eye(face_size, dtype=np.float32)
    return jnp.asarray(identity[table].reshape(8 * face_size, face_size), jnp.float32)


def reorient(traces, orient_codes, perm_tables):
    shape_all = traces.shape
    face_size = shape_all[-2]
    slot_total = shape_all[-1]
    flattened = traces.reshape(-1, face_size, slot_total)
    groups = flattened.shape[0]
    tiled = jnp.broadcast_to(perm_tables, (groups,) + perm_tables.shape)
    product = lax.dot_general(tiled, flattened, (((2,), (1,)), ((0,), (0,))), precision=precise)
    product = product.reshape(groups, 8, face_size, slot_total)
    code_mask = (orient_codes[None, :] == jnp.arange(8, dtype=jnp.int32)[:, None]).astype(
        jnp.float32
    )
    return jnp.sum(product * code_mask[None, :, None, :], axis=1).reshape(shape_all)


def face_flux(first_side, second_side, orient_codes, node_count):
    forward, inverse = orient_tables(node_count)
    forward_perm = perm_matrices(forward)
    inverse_perm = perm_matrices(inverse)
    first_value, first_slope, first_weight, first_metric = first_side
    second_value = reorient(second_side[0], orient_codes, forward_perm)
    second_slope = reorient(second_side[1], orient_codes, forward_perm)
    second_weight = reorient(second_side[2], orient_codes, forward_perm)
    second_metric = reorient(second_side[3], orient_codes, forward_perm)
    penalty = node_count * (node_count + 1) / 2.0
    jump_value = first_value - second_value
    weight = 0.5 * (first_weight + second_weight)
    penalty_term = penalty * 0.5 * (first_metric + second_metric)
    normal_term = weight * (penalty_term * jump_value - 0.5 * (first_slope - second_slope))
    symmetric_term = -0.5 * weight * jump_value
    return (
        normal_term,
        symmetric_term * first_metric,
        -reorient(normal_term, orient_codes, inverse_perm),
        -reorient(symmetric_term, orient_codes, inverse_perm) * second_side[3],
    )


def apply_along(small_table, operand, axis):
    shape_all = operand.shape
    before = int(np.prod(shape_all[:axis]))
    shaped = operand.reshape(before, shape_all[axis], -1)
    tiled = jnp.broadcast_to(small_table, (before,) + small_table.shape)
    product = lax.dot_general(tiled, shaped, (((2,), (1,)), ((0,), (0,))), precision=precise)
    return product.reshape(shape_all[:axis] + (small_table.shape[0],) + shape_all[axis + 1 :])


def volume_term(fields, geometry, derivative):
    slope_first = apply_along(derivative, fields, 1)
    slope_second = apply_along(derivative, fields, 2)
    slope_third = apply_along(derivative, fields, 3)
    flux_first = geometry[0] * slope_first + geometry[3] * slope_second + geometry[4] * slope_third
    flux_second = geometry[3] * slope_first + geometry[1] * slope_second + geometry[5] * slope_third
    flux_third = geometry[4] * slope_first + geometry[5] * slope_second + geometry[2] * slope_third
    transposed = derivative.T
    result = apply_along(transposed, flux_first, 1)
    result = result + apply_along(transposed, flux_second, 2)
    return result + apply_along(transposed, flux_third, 3)


def edge_values(fields, edge_np, axis):
    slices = [
        lax.index_in_dim(fields, node_index, axis, keepdims=False)
        for node_index in range(fields.shape[axis])
    ]
    collected = []
    for row_index in range(4):
        running = 0.0
        for node_index, layer_slice in enumerate(slices):
            factor = float(edge_np[row_index, node_index])
            if factor != 0.0:
                running = running + factor * layer_slice
        collected.append(running)
    return collected


def face_tables(fields, face_metric, edge_np):
    field_count = fields.shape[0]
    elem_count = fields.shape[-1]
    face_size = fields.shape[1] * fields.shape[1]
    values = []
    slopes = []
    for axis_number in range(3):
        collected = edge_values(fields, edge_np, 1 + axis_number)
        shaped = [entry.reshape(field_count, face_size, elem_count) for entry in collected]
        values += [shaped[0], shaped[2]]
        slopes += [shaped[1], shaped[3]]
    value_all = jnp.stack(values, axis=2)
    slope_all = jnp.stack(slopes, axis=2) * face_metric
    return (
        value_all.reshape(field_count * face_size, 6 * elem_count),
        slope_all.reshape(field_count * face_size, 6 * elem_count),
    )


def lift_faces(value_grid, lift_grid, edge_np, node_count):
    field_count = value_grid.shape[0]
    elem_count = value_grid.shape[-1]
    result = 0.0
    for axis_number in range(3):
        face_rows = [
            value_grid[:, :, 2 * axis_number],
            lift_grid[:, :, 2 * axis_number],
            value_grid[:, :, 2 * axis_number + 1],
            lift_grid[:, :, 2 * axis_number + 1],
        ]
        face_rows = [
            entry.reshape(field_count, node_count, node_count, elem_count) for entry in face_rows
        ]
        node_terms = []
        for node_index in range(node_count):
            running = 0.0
            for row_index in range(4):
                factor = float(edge_np[row_index, node_index])
                if factor != 0.0:
                    running = running + factor * face_rows[row_index]
            node_terms.append(running)
        result = result + jnp.stack(node_terms, axis=1 + axis_number)
    return result


def on_device(
    pressure,
    right_side,
    geometry,
    face_weight,
    face_metric,
    cross_slots,
    local_pairs,
    coarse_map,
    coarse_inverse,
):
    node_count = pressure.shape[1]
    elem_count = pressure.shape[-1]
    face_size = node_count * node_count
    derivative = jnp.asarray(derivative_matrix(node_count), jnp.float32)
    edge_np = edge_matrix(node_count)
    slot_table = cross_slots[:, 0, :]
    slot_total = slot_table.shape[1]
    cross_index = slot_table[1] * elem_count + slot_table[0]
    live_mask = slot_table[2].astype(jnp.float32)
    owned_mask = slot_table[3].astype(jnp.float32)
    orient_codes = slot_table[4]
    local_first = local_pairs[1] * elem_count + local_pairs[0]
    local_second = local_pairs[3] * elem_count + local_pairs[2]
    all_index = jnp.concatenate([cross_index, local_first, local_second])
    selector = (jnp.arange(6 * elem_count, dtype=jnp.int32)[:, None] == all_index[None, :]).astype(
        jnp.float32
    )
    weight_flat = face_weight.reshape(face_size, 6 * elem_count)
    metric_flat = face_metric.reshape(face_size, 6 * elem_count)

    def split_rows(matrix, field_count):
        field_rows = field_count * face_size
        columns = matrix.shape[1]
        return (
            matrix[0:field_rows].reshape(field_count, face_size, columns),
            matrix[field_rows : 2 * field_rows].reshape(field_count, face_size, columns),
            matrix[2 * field_rows : 2 * field_rows + face_size],
            matrix[2 * field_rows + face_size : 2 * field_rows + 2 * face_size],
        )

    def apply_operator(fields):
        field_count = fields.shape[0]
        field_rows = field_count * face_size
        volume = volume_term(fields, geometry, derivative)
        value_rows, slope_rows = face_tables(fields, face_metric, edge_np)
        table_all = jnp.concatenate([value_rows, slope_rows, weight_flat, metric_flat], axis=0)
        picked = jnp.dot(table_all, selector, precision=precise)
        own_block = picked[:, 0:slot_total]
        row_total = own_block.shape[0]
        padded = extended(
            own_block.reshape(row_total, 3, 3, slot_total // 9), (("blk", 1), ("sub", 2)), 1
        )
        received = padded[:, 0::2, 0::2].reshape(row_total, slot_total)
        own_traces = split_rows(own_block, field_count)
        peer_traces = split_rows(received, field_count)
        first_value, first_lift, second_value, second_lift = face_flux(
            own_traces, peer_traces, orient_codes, node_count
        )
        sent_back = jnp.concatenate(
            [
                second_value.reshape(field_rows, slot_total),
                second_lift.reshape(field_rows, slot_total),
            ],
            axis=0,
        )
        back_padded = extended(
            sent_back.reshape(2 * field_rows, 3, 3, slot_total // 9), (("blk", 1), ("sub", 2)), 1
        )
        returned = back_padded[:, 0::2, 0::2].reshape(2 * field_rows, slot_total)
        own_part = live_mask * owned_mask
        other_part = live_mask * (1.0 - owned_mask)
        cross_value = (
            first_value * own_part
            + returned[0:field_rows].reshape(field_count, face_size, slot_total) * other_part
        )
        cross_lift = (
            first_lift * own_part
            + returned[field_rows : 2 * field_rows].reshape(field_count, face_size, slot_total)
            * other_part
        )
        first_local = split_rows(picked[:, slot_total : slot_total + elem_count], field_count)
        second_local = split_rows(picked[:, slot_total + elem_count :], field_count)
        local_value_one, local_lift_one, local_value_two, local_lift_two = face_flux(
            first_local, second_local, local_pairs[4], node_count
        )
        value_cols = jnp.concatenate([cross_value, local_value_one, local_value_two], axis=2)
        lift_cols = jnp.concatenate([cross_lift, local_lift_one, local_lift_two], axis=2)
        column_total = value_cols.shape[2]
        contrib = jnp.concatenate(
            [
                value_cols.reshape(field_rows, column_total),
                lift_cols.reshape(field_rows, column_total),
            ],
            axis=0,
        )
        deposited = lax.dot_general(contrib, selector, (((1,), (1,)), ((), ())), precision=precise)
        value_grid = deposited[0:field_rows].reshape(field_count, face_size, 6, elem_count)
        lift_grid = deposited[field_rows : 2 * field_rows].reshape(
            field_count, face_size, 6, elem_count
        )
        return volume + lift_faces(value_grid, lift_grid, edge_np, node_count)

    operated = jnp.concatenate(
        [apply_operator(pressure[0:1]), apply_operator(pressure[1:2])], axis=0
    )
    residual = right_side - operated
    prolong = jnp.asarray(prolong_matrix(), jnp.float32)
    prolong_rows = prolong.T
    field_total = residual.shape[0]
    restricted = apply_along(prolong_rows, residual, 1)
    restricted = apply_along(prolong_rows, restricted, 2)
    restricted = apply_along(prolong_rows, restricted, 3).reshape(field_total, 8, elem_count)
    row_cells = coarse_inverse.shape[-1]
    one_hot = (coarse_map[:, None] == jnp.arange(row_cells, dtype=jnp.int32)[None, :]).astype(
        jnp.float32
    )
    cell_sums = jnp.einsum("fae,ec->fac", restricted, one_hot, precision=precise)
    totals = lax.psum(cell_sums, "sub")
    correction = jnp.einsum("ijc,fjc->fic", coarse_inverse, totals, precision=precise)
    spread = lax.dot_general(correction, one_hot, (((2,), (1,)), ((), ())), precision=precise)
    spread = spread.reshape(field_total, 2, 2, 2, elem_count)
    grown = apply_along(prolong, spread, 1)
    grown = apply_along(prolong, grown, 2)
    grown = apply_along(prolong, grown, 3)
    corrected = pressure + grown
    return (residual, corrected)


def solution(mesh):
    return jax.shard_map(
        on_device,
        mesh=mesh,
        in_specs=(
            P(None, None, None, None, ("blk", "sub")),
            P(None, None, None, None, ("blk", "sub")),
            P(None, None, None, None, ("blk", "sub")),
            P(None, None, ("blk", "sub")),
            P(None, None, ("blk", "sub")),
            P(None, ("blk", "sub"), None),
            P(None, ("blk", "sub")),
            P(("blk", "sub")),
            P(None, None, "blk"),
        ),
        out_specs=(
            P(None, None, None, None, ("blk", "sub")),
            P(None, None, None, None, ("blk", "sub")),
        ),
        check_vma=False,
    )
```

profile of v0, /device:TPU:0, one launch (start us, length us, event | category | flops | bytes accessed | tf_op | source)
XLA Modules:
  0.0 472.1 jit_solution(11285577279841709263)
XLA Ops:
  2.0 9.3 %fusion.151 = (f32[1,8,8,1,512]{4,3,2,1,0:T(1,128)S(1)}, f32[1,8,8,1,512]{4,3,2,1,0:T(1,128)S(1)}, f32[1,8,8,1,512]{4,3,2,1,0:T(1,128)S(1)}, f32[1,8,8,1,512]{4,...) fusion(f32[2,8,8,8,512]{4,3,2,1,0:T(8,128)} %param.19), kind=kLoop, calls=%fused_computation.395 | loop fusion | bytes 4194304 | tf_op jit(solution)/shard_map/slice | solution.py:162
  23.5 2.7 stack.20
  27.7 18.2 %fusion.3 = f32[256,1600]{0,1:T(8,128)S(1)} fusion(s32[1600]{0:T(1024)S(1)} %concatenate.71, f32[64,3072]{1,0:T(8,128)} %bitcast.489, f32[64,3072]{1,0:T(8,128)} %bitcast.491, f32[64,3072]{1,0:T(8,128)} %bitcast.493, f32[64,3072]{1,0:T(8,128)} %bitcast.486), kind=kOutput, calls=%fused_computation.4 | convolution fusion | flops 15106768896 | bytes 4790528 | tf_op jit(solution)/shard_map/dot_general | solution.py:268
  46.8 6.0 %collective-permute-start.1 = (f32[256,1,3,64]{0,3,2,1:T(8,128)}, f32[256,1,3,64]{0,3,2,1:T(8,128)}, u32[]{:S(2)}, u32[]{:S(2)}) collective-permute-start(f32[256,1,3,64]{0,3,2,1:T(8,128)} %get-tuple-element.146), channel_id=1, source_target_pairs={{4,0},{8,4},{12,8},{16,12},{20,16},{24,20},{28,24},{32,28},{36,32}... | collective-permute-start | bytes 589832 | tf_op jit(solution)/shard_map/ppermute | solution.py:19
  56.6 2.9 stack.25
  60.9 17.9 %fusion.1 = f32[256,1600]{0,1:T(8,128)S(1)} fusion(s32[1600]{0:T(1024)S(1)} %concatenate.71, f32[64,3072]{1,0:T(8,128)S(1)} %bitcast.490, f32[64,3072]{1,0:T(8,128)S(1)} %bitcast.492, f32[64,3072]{1,0:T(8,128)} %bitcast.494, f32[64,3072]{1,0:T(8,128)S(1)} %bitcast.487), kind=kOutput, calls=%fused_computation.2 | convolution fusion | flops 15106768896 | bytes 4790528 | tf_op jit(solution)/shard_map/dot_general | solution.py:268
  79.7 5.1 %collective-permute-start.9 = (f32[256,1,3,64]{0,3,2,1:T(8,128)}, f32[256,1,3,64]{0,3,2,1:T(8,128)}, u32[]{:S(2)}, u32[]{:S(2)}) collective-permute-start(f32[256,1,3,64]{0,3,2,1:T(8,128)} %get-tuple-element.155), channel_id=1, source_target_pairs={{4,0},{8,4},{12,8},{16,12},{20,16},{24,20},{28,24},{32,28},{36,32}... | collective-permute-start | bytes 589832 | tf_op jit(solution)/shard_map/ppermute | solution.py:19
  88.6 2.5 reshape.4718
  92.3 2.4 fusion.154
  109.5 4.7 fusion.150
  122.9 10.0 %multiply_add_fusion.1 = (f32[1,8,8,8,512]{4,1,3,2,0:T(8,128)S(1)}, f32[1,8,8,8,512]{4,1,3,2,0:T(8,128)S(1)}, f32[1,8,8,8,512]{4,1,3,2,0:T(8,128)}, f32[1,8,8,8,512]{4,1,3,2,0:T(8,128)}, f32[1,8,8,8,512]{4,1,3,2,0:T(8,128)}) fusion(f32[1,8,8,8,512]{4,3,2,1,0:T(8,128)S(1)} %get-tuple-element.24, f32[1,8,8,8,512]{4,3,2,1,0:T(8,128)S(1)} %bitcast.440, ...), kind=kOutput, calls=%fused_computation.88 | convolution fusion | flops 30408704 | bytes 16777472 | tf_op jit(solution)/shard_map/dot_general | solution.py:143
  136.3 2.4 reshape.4723
  138.7 3.2 fusion.114
  142.0 2.0 fusion.125
  150.8 2.0 multiply_bitcast_fusion.4
  152.8 2.6 fusion.43
  159.1 2.6 fusion.42
  165.1 1.9 copy.621
  167.0 2.0 fusion.116
  170.6 2.4 reshape.4698
  173.0 3.2 fusion.127
  183.0 2.0 multiply_bitcast_fusion.5
  185.1 2.6 fusion.37
  189.5 1.9 multiply_bitcast_fusion.3
  191.3 2.6 fusion.36
  198.7 2.8 collective-permute-start.3
  204.0 3.4 collective-permute-start.11
  207.5 2.0 collective-permute-done.3
  209.5 3.6 collective-permute-done.2
  219.6 2.8 fusion.22
  224.2 2.6 fusion.25
  229.3 2.2 fusion.157
  235.1 2.8 fusion.21
  256.0 2.8 fusion.28
  260.6 2.6 fusion.31
  265.6 2.2 fusion.160
  271.4 2.8 fusion.27
  281.6 1.9 pad_maximum_fusion.25
  283.5 5.0 %collective-permute-start.13 = (f32[128,1,3,64]{0,3,2,1:T(8,128)}, f32[128,1,3,64]{0,3,2,1:T(8,128)}, u32[]{:S(2)}, u32[]{:S(2)}) collective-permute-start(f32[128,1,3,64]{0,3,2,1:T(8,128)} %get-tuple-element.148), channel_id=1, source_target_pairs={{4,0},{8,4},{12,8},{16,12},{20,16},{24,20},{28,24},{32,28},{36,32}... | collective-permute-start | bytes 294920 | tf_op jit(solution)/shard_map/ppermute | solution.py:19
  298.3 2.8 copy.1040
  304.6 2.2 copy.748
  313.4 3.1 collective-permute-done.14
  320.1 11.2 %fusion = f32[128,3072]{1,0:T(8,128)S(1)} fusion(s32[1600]{0:T(1024)S(1)} %copy-done.123, f32[64,1600]{0,1:T(8,128)S(1)} %maximum_bitcast_fusion.3, f32[64,1600]{0,1:T(8,128)S(1)} %maximum_bitcast_fusion.2), kind=kOutput, calls=%fused_computation.1 | convolution fusion | flops 7554867200 | bytes 2398464 | tf_op jit(solution)/shard_map/dot_general | solution.py:317
  332.6 2.5 reshape.4739
  335.1 6.7 %multiply_add_fusion.11 = (f32[1,64,1,512]{3,2,1,0:T(1,128)}, f32[1,64,1,512]{3,2,1,0:T(1,128)}, f32[1,64,1,512]{3,2,1,0:T(1,128)}, f32[1,64,1,512]{3,2,1,0:T(1,...) fusion(f32[1,64,6,512]{3,2,1,0:T(8,128)} %reshape.4739), kind=kLoop, calls=%fused_computation.297 | loop fusion | flops 884736 | bytes 1966080 | tf_op jit(solution)/shard_map/add | solution.py:215
  341.9 2.6 multiply_add_fusion.10
  344.6 11.4 %fusion.2 = f32[128,3072]{1,0:T(8,128)S(1)} fusion(s32[1600]{0:T(1024)S(1)} %copy-done.123, f32[64,1600]{0,1:T(8,128)S(1)} %maximum_bitcast_fusion.1, f32[64,1600]{0,1:T(8,128)S(1)} %maximum_bitcast_fusion), kind=kOutput, calls=%fused_computation.3 | convolution fusion | flops 7554867200 | bytes 2398464 | tf_op jit(solution)/shard_map/dot_general | solution.py:317
  357.3 2.5 reshape.4716
  359.9 6.8 %multiply_add_fusion.29 = (f32[1,64,1,512]{3,2,1,0:T(1,128)}, f32[1,64,1,512]{3,2,1,0:T(1,128)}, f32[1,64,1,512]{3,2,1,0:T(1,128)}, f32[1,64,1,512]{3,2,1,0:T(1,...) fusion(f32[1,64,6,512]{3,2,1,0:T(8,128)} %reshape.4716), kind=kLoop, calls=%fused_computation.318 | loop fusion | flops 884736 | bytes 1966080 | tf_op jit(solution)/shard_map/add | solution.py:215
  366.7 2.6 multiply_add_fusion.28
  369.3 2.5 reshape.4738
  371.9 7.4 %fusion.100 = (f32[1,64,1,512]{3,2,1,0:T(1,128)S(1)}, f32[1,64,1,512]{3,2,1,0:T(1,128)S(1)}, f32[1,64,1,512]{3,2,1,0:T(1,128)S(1)}, f32[1,64,1,512]{3,2,1,0:T(1,...) fusion(f32[1,64,6,512]{3,2,1,0:T(8,128)} %reshape.4738, f32[1,64,6,512]{3,2,1,0:T(8,128)} %reshape.4739), kind=kLoop, calls=%fused_computation.191 | loop fusion | flops 786432 | bytes 2359296 | tf_op jit(solution)/shard_map/add | solution.py:215
  390.2 2.5 reshape.4715
  392.8 7.9 %fusion.106 = (f32[1,64,1,512]{3,2,1,0:T(1,128)S(1)}, f32[1,64,1,512]{3,2,1,0:T(1,128)S(1)}, f32[1,64,1,512]{3,2,1,0:T(1,128)S(1)}, f32[1,64,1,512]{3,2,1,0:T(1,...) fusion(f32[1,64,6,512]{3,2,1,0:T(8,128)} %reshape.4715, f32[1,64,6,512]{3,2,1,0:T(8,128)} %reshape.4716), kind=kLoop, calls=%fused_computation.203 | loop fusion | flops 786432 | bytes 2359296 | tf_op jit(solution)/shard_map/add | solution.py:215
  409.8 3.8 stack.22
  413.7 10.0 %fusion.19 = f32[1,8,8,8,512]{4,1,3,2,0:T(8,128)} fusion(f32[8,8,1,1]{1,0,3,2:T(8,128)S(1)} %copy-done.114, f32[8,8,8,512]{3,2,1,0:T(8,128)} %bitcast.458, f32[8,8,8,512]{3,2,1,0:T(8,128)} %copy.1040, f32[8,8,8,512]{3,0,2,1:T(8,128)} %copy-done.55, f32[8,8,8,512]{3,0,2,1:T(8,128)} %stack.22, f32[8,8,8,512]{3,0,2,1:T(8,128)} %copy_dynamic-update-slice_fusion.24, ...), kind=kOutput, calls=%fused_computation.42 | convolution fusion | flops 27787264 | bytes 12583168 | tf_op jit(solution)/shard_map/dot_general | solution.py:143
  423.7 3.8 stack.27
  427.4 9.6 %fusion.16 = f32[1,8,8,8,512]{4,1,3,2,0:T(8,128)S(1)} fusion(f32[8,8,1,1]{1,0,3,2:T(8,128)S(1)} %copy-done.114, f32[8,8,8,512]{3,2,1,0:T(8,128)} %bitcast.457, f32[8,8,8,512]{3,2,1,0:T(8,128)} %copy.1039, f32[8,8,8,512]{3,0,2,1:T(8,128)} %copy-done.54, f32[8,8,8,512]{3,0,2,1:T(8,128)} %stack.27, f32[8,8,8,512]{3,0,2,1:T(8,128)} %copy-done.52, ...), kind=kOutput, calls=%fused_computation.37 | convolution fusion | flops 27787264 | bytes 12583168 | tf_op jit(solution)/shard_map/dot_general | solution.py:143
  437.0 2.0 maximum_subtract_fusion
  439.0 2.5 copy.750
  441.6 2.7 fusion.142
  444.2 2.4 reshape_reshape.18
  449.0 14.5 %psum.7 = f32[2,8,256]{2,1,0:T(8,128)S(1)} all-reduce(f32[2,8,256]{2,1,0:T(8,128)S(1)} %fusion.75), channel_id=1, replica_groups=mesh['blk'=32,'sub'=4] {'sub'}, use_global_device_ids=true, to_apply=%region_24.0 | all-reduce | flops 4096 | bytes 32768 | tf_op jit(solution)/shard_map/psum | solution.py:339
  467.8 2.2 fusion.122
  (489 shorter events, 186.0 us)
Async XLA Ops:
  2.0 9.4 %copy-start = (f32[2,8,8,8,512]{4,3,2,1,0:T(8,128)S(1)}, f32[2,8,8,8,512]{4,3,2,1,0:T(8,128)}, u32[]{:S(2)}) copy-start(f32[2,8,8,8,512]{4,3,2,1,0:T(8,128)} %param.19) | copy-start | bytes 6291460
  27.7 32.3 %copy-start.122 = (s32[1600]{0:T(1024)}, s32[1600]{0:T(1024)S(1)}, u32[]{:S(2)}) copy-start(s32[1600]{0:T(1024)S(1)} %concatenate.71) | copy-start | bytes 19204
  45.9 7.9 %copy-start.2 = (f32[256,1600]{0,1:T(8,128)}, f32[256,1600]{0,1:T(8,128)S(1)}, u32[]{:S(2)}) copy-start(f32[256,1600]{0,1:T(8,128)S(1)} %fusion.3) | copy-start | bytes 4915204
  45.9 6.9 %copy-start.45 = (f32[6,8,8,512]{3,2,1,0:T(8,128)S(1)}, f32[6,8,8,512]{3,2,1,0:T(8,128)}, u32[]{:S(2)}) copy-start(f32[6,8,8,512]{3,2,1,0:T(8,128)} %get-tuple-element.133) | copy-start | bytes 2359300
  45.9 8.1 %copy-start.24 = (f32[256,576]{0,1:T(8,128)}, f32[256,576]{0,1:T(8,128)S(1)}, u32[]{:S(2)}) copy-start(f32[256,576]{0,1:T(8,128)S(1)} %slice.715) | copy-start | bytes 1769476
  46.0 7.8 %copy-start.87 = (f32[1,64,1,512]{3,1,2,0:T(8,128)S(1)}, f32[1,64,1,512]{3,1,2,0:T(8,128)}, u32[]{:S(2)}) copy-start(f32[1,64,1,512]{3,1,2,0:T(8,128)} %get-tuple-element.46) | copy-start | bytes 393220
  46.0 7.9 %copy-start.85 = (f32[1,64,1,512]{3,1,2,0:T(8,128)S(1)}, f32[1,64,1,512]{3,1,2,0:T(8,128)}, u32[]{:S(2)}) copy-start(f32[1,64,1,512]{3,1,2,0:T(8,128)} %get-tuple-element.45) | copy-start | bytes 393220
  46.0 8.1 %copy-start.88 = (f32[1,64,1,512]{3,1,2,0:T(8,128)S(1)}, f32[1,64,1,512]{3,1,2,0:T(8,128)}, u32[]{:S(2)}) copy-start(f32[1,64,1,512]{3,1,2,0:T(8,128)} %get-tuple-element.42) | copy-start | bytes 393220
  46.8 7.5 %copy-start.86 = (f32[1,64,1,512]{3,1,2,0:T(8,128)S(1)}, f32[1,64,1,512]{3,1,2,0:T(8,128)}, u32[]{:S(2)}) copy-start(f32[1,64,1,512]{3,1,2,0:T(8,128)} %get-tuple-element.41) | copy-start | bytes 393220
  46.8 150.7 %collective-permute-start.1 = (f32[256,1,3,64]{0,3,2,1:T(8,128)}, f32[256,1,3,64]{0,3,2,1:T(8,128)}, u32[]{:S(2)}, u32[]{:S(2)}) collective-permute-start(f32[256,1,3,64]{0,3,2,1:T(8,128)} %get-tuple-element.146), channel_id=1, source_target_pairs={{4,0},{8,4},{12,8},{16,12},{20,16},{24,20},{28,24},{32,28},{36,32}... | collective-permute-start | bytes 589832 | tf_op jit(solution)/shard_map/ppermute | solution.py:19
  52.8 144.7 %collective-permute-start = (f32[256,1,3,64]{0,3,2,1:T(8,128)}, f32[256,1,3,64]{0,3,2,1:T(8,128)}, u32[]{:S(2)}, u32[]{:S(2)}) collective-permute-start(f32[256,1,3,64]{0,3,2,1:T(8,128)} %get-tuple-element.145), channel_id=1, source_target_pairs={{0,4},{4,8},{8,12},{12,16},{16,20},{20,24},{24,28},{28,32},{32,36}... | collective-permute-start | bytes 589832 | tf_op jit(solution)/shard_map/ppermute | solution.py:17
  78.7 7.3 %copy-start.5 = (f32[256,1600]{0,1:T(8,128)}, f32[256,1600]{0,1:T(8,128)S(1)}, u32[]{:S(2)}) copy-start(f32[256,1600]{0,1:T(8,128)S(1)} %fusion.1) | copy-start | bytes 4915204
  79.7 122.5 %collective-permute-start.9 = (f32[256,1,3,64]{0,3,2,1:T(8,128)}, f32[256,1,3,64]{0,3,2,1:T(8,128)}, u32[]{:S(2)}, u32[]{:S(2)}) collective-permute-start(f32[256,1,3,64]{0,3,2,1:T(8,128)} %get-tuple-element.155), channel_id=1, source_target_pairs={{4,0},{8,4},{12,8},{16,12},{20,16},{24,20},{28,24},{32,28},{36,32}... | collective-permute-start | bytes 589832 | tf_op jit(solution)/shard_map/ppermute | solution.py:19
  84.8 117.4 %collective-permute-start.8 = (f32[256,1,3,64]{0,3,2,1:T(8,128)}, f32[256,1,3,64]{0,3,2,1:T(8,128)}, u32[]{:S(2)}, u32[]{:S(2)}) collective-permute-start(f32[256,1,3,64]{0,3,2,1:T(8,128)} %get-tuple-element.154), channel_id=1, source_target_pairs={{0,4},{4,8},{8,12},{12,16},{16,20},{20,24},{24,28},{28,32},{32,36}... | collective-permute-start | bytes 589832 | tf_op jit(solution)/shard_map/ppermute | solution.py:17
  94.7 6.9 %copy-start.3 = (f32[256,1600]{0,1:T(8,128)S(1)}, f32[256,1600]{0,1:T(8,128)}, u32[]{:S(2)}) copy-start(f32[256,1600]{0,1:T(8,128)} %copy-done.2) | copy-start | bytes 4915204
  114.2 7.7 %copy-start.8 = (f32[1,8,8,8,512]{4,3,2,1,0:T(8,128)}, f32[1,8,8,8,512]{4,3,2,1,0:T(8,128)S(1)}, u32[]{:S(2)}) copy-start(f32[1,8,8,8,512]{4,3,2,1,0:T(8,128)S(1)} %get-tuple-element.26) | copy-start | bytes 3145732
  120.9 12.1 %copy-start.18 = (f32[1,8,8,8,512]{4,3,2,1,0:T(8,128)}, f32[1,8,8,8,512]{4,3,2,1,0:T(8,128)S(1)}, u32[]{:S(2)}) copy-start(f32[1,8,8,8,512]{4,3,2,1,0:T(8,128)S(1)} %get-tuple-element.168) | copy-start | bytes 3145732
  120.9 12.1 %copy-start.19 = (f32[1,8,8,8,512]{4,3,2,1,0:T(8,128)}, f32[1,8,8,8,512]{4,3,2,1,0:T(8,128)S(1)}, u32[]{:S(2)}) copy-start(f32[1,8,8,8,512]{4,3,2,1,0:T(8,128)S(1)} %get-tuple-element.169) | copy-start | bytes 3145732
  121.9 11.0 %copy-start.17 = (f32[1,8,8,8,512]{4,1,3,2,0:T(8,128)}, f32[1,8,8,8,512]{4,1,3,2,0:T(8,128)S(1)}, u32[]{:S(2)}) copy-start(f32[1,8,8,8,512]{4,1,3,2,0:T(8,128)S(1)} %convolution_bitcast_fusion.1) | copy-start | bytes 3145732
  152.8 14.2 %copy-start.57 = (f32[64,512]{1,0:T(8,128)}, f32[64,512]{1,0:T(8,128)S(1)}, u32[]{:S(2)}) copy-start(f32[64,512]{1,0:T(8,128)S(1)} %get-tuple-element.137) | copy-start | bytes 393220
  185.1 13.6 %copy-start.58 = (f32[64,512]{1,0:T(8,128)}, f32[64,512]{1,0:T(8,128)S(1)}, u32[]{:S(2)}) copy-start(f32[64,512]{1,0:T(8,128)S(1)} %get-tuple-element.136) | copy-start | bytes 393220
  197.4 15.7 %copy-start.25 = (f32[256,576]{0,1:T(8,128)S(1)}, f32[256,576]{0,1:T(8,128)}, u32[]{:S(2)}) copy-start(f32[256,576]{0,1:T(8,128)} %copy-done.24) | copy-start | bytes 1769476
  198.7 10.8 %collective-permute-start.3 = (f32[256,5,1,64]{0,3,2,1:T(8,128)S(1)}, f32[256,5,1,64]{0,3,2,1:T(8,128)S(1)}, u32[]{:S(2)}, u32[]{:S(2)}) collective-permute-start(f32[256,5,1,64]{0,3,2,1:T(8,128)S(1)} %get-tuple-element.127), channel_id=1, source_target_pairs={{1,0},{2,1},{3,2},{0,3},{5,4},{6,5},{7,6},{4,7},{9,8},{10,9},{11,1... | collective-permute-start | bytes 983048 | tf_op jit(solution)/shard_map/ppermute | solution.py:19
  201.5 11.6 %collective-permute-start.2 = (f32[256,5,1,64]{0,3,2,1:T(8,128)S(1)}, f32[256,5,1,64]{0,3,2,1:T(8,128)S(1)}, u32[]{:S(2)}, u32[]{:S(2)}) collective-permute-start(f32[256,5,1,64]{0,3,2,1:T(8,128)S(1)} %get-tuple-element.126), channel_id=1, source_target_pairs={{0,1},{1,2},{2,3},{3,0},{4,5},{5,6},{6,7},{7,4},{8,9},{9,10},{10,1... | collective-permute-start | bytes 983048 | tf_op jit(solution)/shard_map/ppermute | solution.py:17
  204.0 45.1 %collective-permute-start.11 = (f32[256,5,1,64]{0,3,2,1:T(8,128)}, f32[256,5,1,64]{0,3,2,1:T(8,128)}, u32[]{:S(2)}, u32[]{:S(2)}) collective-permute-start(f32[256,5,1,64]{0,3,2,1:T(8,128)} %get-tuple-element.129), channel_id=1, source_target_pairs={{1,0},{2,1},{3,2},{0,3},{5,4},{6,5},{7,6},{4,7},{9,8},{10,9},{11,1... | collective-permute-start | bytes 983048 | tf_op jit(solution)/shard_map/ppermute | solution.py:19
  207.5 41.7 %collective-permute-start.10 = (f32[256,5,1,64]{0,3,2,1:T(8,128)}, f32[256,5,1,64]{0,3,2,1:T(8,128)}, u32[]{:S(2)}, u32[]{:S(2)}) collective-permute-start(f32[256,5,1,64]{0,3,2,1:T(8,128)} %get-tuple-element.128), channel_id=1, source_target_pairs={{0,1},{1,2},{2,3},{3,0},{4,5},{5,6},{6,7},{7,4},{8,9},{9,10},{10,1... | collective-permute-start | bytes 983048 | tf_op jit(solution)/shard_map/ppermute | solution.py:17
  247.1 41.5 %collective-permute-start.5 = (f32[128,1,3,64]{0,3,2,1:T(8,128)}, f32[128,1,3,64]{0,3,2,1:T(8,128)S(1)}, u32[]{:S(2)}, u32[]{:S(2)}) collective-permute-start(f32[128,1,3,64]{0,3,2,1:T(8,128)} %get-tuple-element.139), channel_id=1, source_target_pairs={{4,0},{8,4},{12,8},{16,12},{20,16},{24,20},{28,24},{32,28},{36,32}... | collective-permute-start | bytes 294920 | tf_op jit(solution)/shard_map/ppermute | solution.py:19
  248.8 39.8 %collective-permute-start.4 = (f32[128,1,3,64]{0,3,2,1:T(8,128)}, f32[128,1,3,64]{0,3,2,1:T(8,128)}, u32[]{:S(2)}, u32[]{:S(2)}) collective-permute-start(f32[128,1,3,64]{0,3,2,1:T(8,128)} %get-tuple-element.138), channel_id=1, source_target_pairs={{0,4},{4,8},{8,12},{12,16},{16,20},{20,24},{24,28},{28,32},{32,36}... | collective-permute-start | bytes 294920 | tf_op jit(solution)/shard_map/ppermute | solution.py:17
  279.2 9.4 %copy-start.32 = (f32[64,3,3,64]{0,3,2,1:T(8,128)S(1)}, f32[64,3,3,64]{0,3,2,1:T(8,128)}, u32[]{:S(2)}) copy-start(f32[64,3,3,64]{0,3,2,1:T(8,128)} %get-tuple-element.141) | copy-start | bytes 442372
  281.6 11.6 %copy-start.38 = (f32[8,8,4096]{2,1,0:T(8,128)S(1)}, f32[8,8,4096]{2,1,0:T(8,128)}, u32[]{:S(2)}) copy-start(f32[8,8,4096]{2,1,0:T(8,128)} %fusion.125) | copy-start | bytes 3145732
  283.5 23.2 %collective-permute-start.13 = (f32[128,1,3,64]{0,3,2,1:T(8,128)}, f32[128,1,3,64]{0,3,2,1:T(8,128)}, u32[]{:S(2)}, u32[]{:S(2)}) collective-permute-start(f32[128,1,3,64]{0,3,2,1:T(8,128)} %get-tuple-element.148), channel_id=1, source_target_pairs={{4,0},{8,4},{12,8},{16,12},{20,16},{24,20},{28,24},{32,28},{36,32}... | collective-permute-start | bytes 294920 | tf_op jit(solution)/shard_map/ppermute | solution.py:19
  288.6 18.2 %collective-permute-start.12 = (f32[128,1,3,64]{0,3,2,1:T(8,128)}, f32[128,1,3,64]{0,3,2,1:T(8,128)}, u32[]{:S(2)}, u32[]{:S(2)}) collective-permute-start(f32[128,1,3,64]{0,3,2,1:T(8,128)} %get-tuple-element.147), channel_id=1, source_target_pairs={{0,4},{4,8},{8,12},{12,16},{16,20},{20,24},{24,28},{28,32},{32,36}... | collective-permute-start | bytes 294920 | tf_op jit(solution)/shard_map/ppermute | solution.py:17
  290.4 19.8 %collective-permute-start.7 = (f32[128,5,1,64]{0,3,2,1:T(8,128)}, f32[128,5,1,64]{0,3,2,1:T(8,128)}, u32[]{:S(2)}, u32[]{:S(2)}) collective-permute-start(f32[128,5,1,64]{0,3,2,1:T(8,128)} %get-tuple-element.131), channel_id=1, source_target_pairs={{1,0},{2,1},{3,2},{0,3},{5,4},{6,5},{7,6},{4,7},{9,8},{10,9},{11,1... | collective-permute-start | bytes 491528 | tf_op jit(solution)/shard_map/ppermute | solution.py:19
  291.0 19.3 %collective-permute-start.6 = (f32[128,5,1,64]{0,3,2,1:T(8,128)}, f32[128,5,1,64]{0,3,2,1:T(8,128)}, u32[]{:S(2)}, u32[]{:S(2)}) collective-permute-start(f32[128,5,1,64]{0,3,2,1:T(8,128)} %get-tuple-element.130), channel_id=1, source_target_pairs={{0,1},{1,2},{2,3},{3,0},{4,5},{5,6},{6,7},{7,4},{8,9},{9,10},{10,1... | collective-permute-start | bytes 491528 | tf_op jit(solution)/shard_map/ppermute | solution.py:17
  308.0 5.4 %collective-permute-start.15 = (f32[128,5,1,64]{0,3,2,1:T(8,128)S(1)}, f32[128,5,1,64]{0,3,2,1:T(8,128)S(1)}, u32[]{:S(2)}, u32[]{:S(2)}) collective-permute-start(f32[128,5,1,64]{0,3,2,1:T(8,128)S(1)} %get-tuple-element.135), channel_id=1, source_target_pairs={{1,0},{2,1},{3,2},{0,3},{5,4},{6,5},{7,6},{4,7},{9,8},{10,9},{11,1... | collective-permute-start | bytes 491528 | tf_op jit(solution)/shard_map/ppermute | solution.py:19
  309.9 6.7 %collective-permute-start.14 = (f32[128,5,1,64]{0,3,2,1:T(8,128)S(1)}, f32[128,5,1,64]{0,3,2,1:T(8,128)S(1)}, u32[]{:S(2)}, u32[]{:S(2)}) collective-permute-start(f32[128,5,1,64]{0,3,2,1:T(8,128)S(1)} %get-tuple-element.134), channel_id=1, source_target_pairs={{0,1},{1,2},{2,3},{3,0},{4,5},{5,6},{6,7},{7,4},{8,9},{9,10},{10,1... | collective-permute-start | bytes 491528 | tf_op jit(solution)/shard_map/ppermute | solution.py:17
  335.1 6.8 %copy-start.21 = (f32[1,64,6,512]{3,2,1,0:T(8,128)S(1)}, f32[1,64,6,512]{3,2,1,0:T(8,128)}, u32[]{:S(2)}) copy-start(f32[1,64,6,512]{3,2,1,0:T(8,128)} %reshape.4739) | copy-start | bytes 2359300
  335.1 9.4 %copy-start.56 = (f32[64,576]{0,1:T(8,128)S(1)}, f32[64,576]{0,1:T(8,128)}, u32[]{:S(2)}) copy-start(f32[64,576]{0,1:T(8,128)} %get-tuple-element.164) | copy-start | bytes 442372
  335.1 9.4 %copy-start.60 = (f32[1,64,512]{1,2,0:T(8,128)S(1)}, f32[1,64,512]{1,2,0:T(8,128)}, u32[]{:S(2)}) copy-start(f32[1,64,512]{1,2,0:T(8,128)} %multiply_bitcast_fusion.3) | copy-start | bytes 393220
  335.1 9.4 %copy-start.64 = (f32[1,64,512]{1,2,0:T(8,128)S(1)}, f32[1,64,512]{1,2,0:T(8,128)}, u32[]{:S(2)}) copy-start(f32[1,64,512]{1,2,0:T(8,128)} %copy.663) | copy-start | bytes 393220
  359.9 6.8 %copy-start.20 = (f32[1,64,6,512]{3,2,1,0:T(8,128)S(1)}, f32[1,64,6,512]{3,2,1,0:T(8,128)}, u32[]{:S(2)}) copy-start(f32[1,64,6,512]{3,2,1,0:T(8,128)} %reshape.4716) | copy-start | bytes 2359300
  371.8 8.3 %copy-start.112 = (f32[1,64,1,512]{3,2,1,0:T(1,128)S(1)}, f32[1,64,1,512]{3,2,1,0:T(1,128)}, u32[]{:S(2)}) copy-start(f32[1,64,1,512]{3,2,1,0:T(1,128)} %get-tuple-element.123) | copy-start | bytes 393220
  371.8 8.9 %copy-start.111 = (f32[1,64,1,512]{3,2,1,0:T(1,128)S(1)}, f32[1,64,1,512]{3,2,1,0:T(1,128)}, u32[]{:S(2)}) copy-start(f32[1,64,1,512]{3,2,1,0:T(1,128)} %get-tuple-element.118) | copy-start | bytes 393220
  371.8 9.6 %copy-start.110 = (f32[1,64,1,512]{3,2,1,0:T(1,128)S(1)}, f32[1,64,1,512]{3,2,1,0:T(1,128)}, u32[]{:S(2)}) copy-start(f32[1,64,1,512]{3,2,1,0:T(1,128)} %get-tuple-element.119) | copy-start | bytes 393220
  371.8 10.3 %copy-start.109 = (f32[1,64,1,512]{3,2,1,0:T(1,128)S(1)}, f32[1,64,1,512]{3,2,1,0:T(1,128)}, u32[]{:S(2)}) copy-start(f32[1,64,1,512]{3,2,1,0:T(1,128)} %get-tuple-element.120) | copy-start | bytes 393220
  371.9 10.9 %copy-start.108 = (f32[1,64,1,512]{3,2,1,0:T(1,128)S(1)}, f32[1,64,1,512]{3,2,1,0:T(1,128)}, u32[]{:S(2)}) copy-start(f32[1,64,1,512]{3,2,1,0:T(1,128)} %get-tuple-element.121) | copy-start | bytes 393220
  371.9 11.6 %copy-start.107 = (f32[1,64,1,512]{3,2,1,0:T(1,128)S(1)}, f32[1,64,1,512]{3,2,1,0:T(1,128)}, u32[]{:S(2)}) copy-start(f32[1,64,1,512]{3,2,1,0:T(1,128)} %get-tuple-element.122) | copy-start | bytes 393220
  379.3 7.0 %copy-start.96 = (f32[1,64,1,512]{3,2,1,0:T(1,128)S(1)}, f32[1,64,1,512]{3,2,1,0:T(1,128)}, u32[]{:S(2)}) copy-start(f32[1,64,1,512]{3,2,1,0:T(1,128)} %get-tuple-element.114) | copy-start | bytes 393220
  379.4 7.6 %copy-start.95 = (f32[1,64,1,512]{3,2,1,0:T(1,128)S(1)}, f32[1,64,1,512]{3,2,1,0:T(1,128)}, u32[]{:S(2)}) copy-start(f32[1,64,1,512]{3,2,1,0:T(1,128)} %get-tuple-element.115) | copy-start | bytes 393220
  380.1 7.5 %copy-start.94 = (f32[1,64,1,512]{3,2,1,0:T(1,128)S(1)}, f32[1,64,1,512]{3,2,1,0:T(1,128)}, u32[]{:S(2)}) copy-start(f32[1,64,1,512]{3,2,1,0:T(1,128)} %get-tuple-element.116) | copy-start | bytes 393220
  380.8 7.5 %copy-start.99 = (f32[1,64,1,512]{3,2,1,0:T(1,128)S(1)}, f32[1,64,1,512]{3,2,1,0:T(1,128)}, u32[]{:S(2)}) copy-start(f32[1,64,1,512]{3,2,1,0:T(1,128)} %get-tuple-element.117) | copy-start | bytes 393220
  381.4 7.5 %copy-start.93 = (f32[1,64,1,512]{3,2,1,0:T(1,128)S(1)}, f32[1,64,1,512]{3,2,1,0:T(1,128)}, u32[]{:S(2)}) copy-start(f32[1,64,1,512]{3,2,1,0:T(1,128)} %get-tuple-element.108) | copy-start | bytes 393220
  392.8 8.0 %copy-start.106 = (f32[1,64,1,512]{3,2,1,0:T(1,128)S(1)}, f32[1,64,1,512]{3,2,1,0:T(1,128)}, u32[]{:S(2)}) copy-start(f32[1,64,1,512]{3,2,1,0:T(1,128)} %get-tuple-element.105) | copy-start | bytes 393220
  392.8 8.1 %copy-start.105 = (f32[1,64,1,512]{3,2,1,0:T(1,128)S(1)}, f32[1,64,1,512]{3,2,1,0:T(1,128)}, u32[]{:S(2)}) copy-start(f32[1,64,1,512]{3,2,1,0:T(1,128)} %get-tuple-element.100) | copy-start | bytes 393220
  392.8 8.1 %copy-start.104 = (f32[1,64,1,512]{3,2,1,0:T(1,128)S(1)}, f32[1,64,1,512]{3,2,1,0:T(1,128)}, u32[]{:S(2)}) copy-start(f32[1,64,1,512]{3,2,1,0:T(1,128)} %get-tuple-element.101) | copy-start | bytes 393220
  392.8 8.1 %copy-start.103 = (f32[1,64,1,512]{3,2,1,0:T(1,128)S(1)}, f32[1,64,1,512]{3,2,1,0:T(1,128)}, u32[]{:S(2)}) copy-start(f32[1,64,1,512]{3,2,1,0:T(1,128)} %get-tuple-element.102) | copy-start | bytes 393220
  392.8 8.2 %copy-start.101 = (f32[1,64,1,512]{3,2,1,0:T(1,128)S(1)}, f32[1,64,1,512]{3,2,1,0:T(1,128)}, u32[]{:S(2)}) copy-start(f32[1,64,1,512]{3,2,1,0:T(1,128)} %get-tuple-element.103) | copy-start | bytes 393220
  392.8 8.2 %copy-start.100 = (f32[1,64,1,512]{3,2,1,0:T(1,128)S(1)}, f32[1,64,1,512]{3,2,1,0:T(1,128)}, u32[]{:S(2)}) copy-start(f32[1,64,1,512]{3,2,1,0:T(1,128)} %get-tuple-element.104) | copy-start | bytes 393220
  406.9 6.8 %copy-start.114 = (f32[8,8,1,1]{1,0,3,2:T(8,128)S(1)}, f32[8,8,1,1]{1,0,3,2:T(8,128)}, u32[]{:S(2)}) copy-start(f32[8,8,1,1]{1,0,3,2:T(8,128)} %constant.55) | copy-start | bytes 772
  413.6 10.0 %copy-start.84 = (f32[1,64,1,512]{3,2,1,0:T(1,128)S(1)}, f32[1,64,1,512]{3,2,1,0:T(1,128)}, u32[]{:S(2)}) copy-start(f32[1,64,1,512]{3,2,1,0:T(1,128)} %get-tuple-element.109) | copy-start | bytes 393220
  427.4 9.6 %copy-start.41 = (f32[1,8,8,8,512]{4,1,3,2,0:T(8,128)S(1)}, f32[1,8,8,8,512]{4,1,3,2,0:T(8,128)}, u32[]{:S(2)}) copy-start(f32[1,8,8,8,512]{4,1,3,2,0:T(8,128)} %fusion.19) | copy-start | bytes 3145732
  427.4 9.6 %copy-start.50 = (f32[2,8,8,8,512]{4,3,2,1,0:T(8,128)S(1)}, f32[2,8,8,8,512]{4,3,2,1,0:T(8,128)}, u32[]{:S(2)}) copy-start(f32[2,8,8,8,512]{4,3,2,1,0:T(8,128)} %param.20) | copy-start | bytes 6291460
  444.2 19.5 %copy-start.37 = (f32[8,8,256]{1,0,2:T(8,128)S(1)}, f32[8,8,256]{1,0,2:T(8,128)}, u32[]{:S(2)}) copy-start(f32[8,8,256]{1,0,2:T(8,128)} %copy.748) | copy-start | bytes 196612
  446.6 19.6 %copy-start.120 = (f32[8,2]{0,1:T(2,128)S(1)}, f32[8,2]{0,1:T(2,128)}, u32[]{:S(2)}) copy-start(f32[8,2]{0,1:T(2,128)} %constant.49.clone) | copy-start | bytes 196
  (80 other events, 225.5 us)
where the time goes:
time: 480 us; the launch traced here: 472 us
  local copies, waits for them, and re-layouts  168 us (35%)
  matrix products  165 us (34%)
  other arithmetic  82.6 us (17%)
  starting transfers between devices  28.7 us (6%)
  blocking collectives  14.5 us (3%)
  waiting for transfers between devices  10.4 us (2%)
    dot_general x18, matrix products, apply_along(): lax.dot_general(tiled, shaped, (((2,), (1,)), ((0,), (0,))), precision=pr...  53 us
    dot_general x24, matrix products, reorient(): lax.dot_general(tiled, flattened, (((2,), (1,)), ((0,), (0,))), precision...  50.4 us
    unnamed x330, local copies, waits for them, and re-layouts  48.4 us
    dot_general x2, matrix products, apply_operator(): picked = jnp.dot(table_all, selector, precision=precise)  36 us
    add x6, other arithmetic, lift_faces(): running = running + factor * face_rows[row_index]  34.1 us
    ppermute x8, starting transfers between devices, extended(): lax.ppermute(head, axis, [((i + 1) % count, i) for i in range(count)])  26.5 us
    dot_general x2, matrix products, apply_operator(): lax.dot_general(contrib, selector, (((1,), (1,)), ((), ())), precision=pr...  22.6 us
    reduce_sum x12, local copies, waits for them, and re-layouts, reorient(): jnp.sum(product * code_mask[None, :, None, :], axis=1).reshape(shape_all)  21.3 us
  transfers between devices with their start and end apart: 16, of which 4 were waited for; matrix products, arithmetic and copies ran while one was open for 48% of the time, Pallas kernels for 0%

commit v1 on v0

v1 whole, which is shorter than its diff:
```python
import functools

import jax
import jax.numpy as jnp
import numpy as np
from jax import lax
from jax.experimental import pallas as pl
from jax.experimental.pallas import tpu as pltpu
from jax.sharding import PartitionSpec as P

NODES = 8
FACE = NODES * NODES
BRICK = NODES * FACE
LANES = 128
MESH = pl.DeviceIdType.MESH
VMEM = pltpu.MemorySpace.VMEM
SMEM = pltpu.MemorySpace.SMEM


def node_points():
    positive = [0.2092992179024789, 0.5917001814331423, 0.8717401485096066, 1.0]
    return np.array(sorted([-entry for entry in positive] + positive))


def derivative_matrix():
    points = node_points()
    count = len(points)
    weights = np.array(
        [
            1.0 / np.prod([points[row] - points[col] for col in range(count) if col != row])
            for row in range(count)
        ]
    )
    matrix = np.zeros((count, count))
    for row in range(count):
        for col in range(count):
            if row != col:
                matrix[row, col] = weights[col] / weights[row] / (points[row] - points[col])
        matrix[row, row] = -np.sum(matrix[row])
    return matrix


DERIV = derivative_matrix()
POINTS = node_points()
MODES = np.stack([(1.0 - POINTS) / 2.0, (1.0 + POINTS) / 2.0], axis=1)


def split_constant(matrix):
    high = matrix.astype(jnp.bfloat16)
    low = (matrix - high.astype(np.float64)).astype(jnp.bfloat16)
    return np.concatenate([high, low, high], axis=1)


def forward_table():
    eye = np.eye(NODES)
    return split_constant(np.concatenate([np.kron(DERIV, eye), np.kron(eye, DERIV)], axis=0))


def backward_table():
    eye = np.eye(NODES)
    return split_constant(np.concatenate([np.kron(DERIV.T, eye), np.kron(eye, DERIV.T)], axis=1))


def lift_table():
    eye = np.eye(NODES)
    rows = [eye[:, :1], -DERIV[:1].T, eye[:, -1:], DERIV[-1:].T]
    second = [np.kron(row, eye) for row in rows]
    third = [np.kron(eye, row) for row in rows]
    return split_constant(np.concatenate(second + third, axis=1))


def split_rows(values):
    high = values.astype(jnp.bfloat16)
    low = (values - high.astype(jnp.float32)).astype(jnp.bfloat16)
    return jnp.concatenate([high, high, low], axis=0)


def product(table, values):
    return lax.dot_general(
        table, split_rows(values), (((1,), (0,)), ((), ())), preferred_element_type=jnp.float32
    )


def even_odd(matrix, layers):
    half = NODES // 2
    sums = [layers[k] + layers[NODES - 1 - k] for k in range(half)]
    gaps = [layers[k] - layers[NODES - 1 - k] for k in range(half)]
    result = [None] * NODES
    for row in range(half):
        even = None
        odd = None
        for k in range(half):
            first = float((matrix[row, k] + matrix[row, NODES - 1 - k]) / 2)
            second = float((matrix[row, k] - matrix[row, NODES - 1 - k]) / 2)
            even = first * sums[k] if even is None else even + first * sums[k]
            odd = second * gaps[k] if odd is None else odd + second * gaps[k]
        result[row] = odd + even
        result[NODES - 1 - row] = odd - even
    return result


def weighted(coefficients, layers):
    total = None
    for factor, layer in zip(coefficients, layers):
        term = float(factor) * layer
        total = term if total is None else total + term
    return total


def pack_kernel(slots, p_ref, fw_ref, fm_ref, t_ref, send_ref):
    step = pl.program_id(0)
    elems = t_ref.shape[0] // 6
    fields = p_ref.shape[0] // BRICK
    base = step * LANES
    for axis in range(3):
        values = []
        slopes = []
        for field in range(fields):
            start = field * BRICK
            layers = []
            for k in range(NODES):
                if axis == 0:
                    layers.append(p_ref[start + k * FACE : start + (k + 1) * FACE, :])
                elif axis == 1:
                    rows = [
                        p_ref[start + i * FACE + k * NODES : start + i * FACE + (k + 1) * NODES, :]
                        for i in range(NODES)
                    ]
                    layers.append(jnp.concatenate(rows, axis=0))
                else:
                    layers.append(p_ref[pl.ds(start + k, FACE, stride=NODES), :])
            values.append((layers[0], layers[-1]))
            slopes.append((weighted(-DERIV[0], layers), weighted(DERIV[-1], layers)))
        for side in range(2):
            face = 2 * axis + side
            metric = fm_ref[face]
            rows = pl.ds(pl.multiple_of(face * elems + base, LANES), LANES)
            value = jnp.concatenate([entry[side] for entry in values], axis=0)
            slope = jnp.concatenate([entry[side] * metric for entry in slopes], axis=0)
            t_ref[rows, 0:LANES] = value.T
            t_ref[rows, LANES : 2 * LANES] = slope.T
            t_ref[rows, 2 * LANES :] = jnp.concatenate([fw_ref[face], metric], axis=0).T

    @pl.when(step == pl.num_programs(0) - 1)
    def _():
        def move(c, carry):
            row = slots[1, 0, c] * elems + slots[0, 0, c]
            send_ref[pl.ds(c, 1), :] = t_ref[pl.ds(row, 1), :]
            return carry

        lax.fori_loop(0, send_ref.shape[0], move, 0, unroll=8)


def exchange_kernel(n_blk, n_sub, send_ref, recv_ref, send_sem, recv_sem):
    place = lax.axis_index("blk")
    sub = lax.axis_index("sub")
    width = send_ref.shape[0] // 9

    def peer(k):
        return (
            lax.rem(place + (k // 3 - 1) + n_blk, n_blk),
            lax.rem(sub + (k % 3 - 1) + n_sub, n_sub),
        )

    others = [k for k in (0, 2, 6, 8, 1, 7, 3, 5)]
    barrier = pltpu.get_barrier_semaphore()
    for k in others:
        pl.semaphore_signal(barrier, inc=1, device_id=peer(k), device_id_type=MESH)
    pl.semaphore_wait(barrier, len(others))
    copies = []
    for k in others:
        copies.append(
            pltpu.make_async_remote_copy(
                src_ref=send_ref.at[pl.ds(k * width, width)],
                dst_ref=recv_ref.at[pl.ds((8 - k) * width, width)],
                send_sem=send_sem.at[k],
                recv_sem=recv_sem.at[8 - k],
                device_id=peer(k),
                device_id_type=MESH,
            )
        )
        copies[-1].start()
    recv_ref[4 * width : 5 * width, :] = jnp.zeros((width, recv_ref.shape[1]), jnp.float32)
    for copy in copies:
        copy.wait()


def volume_kernel(p_ref, g_ref, fwd_ref, bwd_ref, out_ref, s_ref):
    fields = p_ref.shape[0]

    def first(n, carry):
        f = n // NODES
        rows = pl.ds(pl.multiple_of((n % NODES) * NODES, NODES), NODES)
        layers = [p_ref[f, k, rows, :] for k in range(NODES)]
        for k, value in enumerate(even_odd(DERIV, layers)):
            s_ref[f, k, rows, :] = value
        return carry

    lax.fori_loop(0, fields * NODES, first, 0)

    def middle(i, carry):
        for f in range(fields):
            both = product(fwd_ref[...], p_ref[f, i])
            s1 = s_ref[f, i]
            s2 = both[:FACE]
            s3 = both[FACE:]
            q1 = g_ref[0, i] * s1 + g_ref[3, i] * s2 + g_ref[4, i] * s3
            q2 = g_ref[3, i] * s1 + g_ref[1, i] * s2 + g_ref[5, i] * s3
            q3 = g_ref[4, i] * s1 + g_ref[5, i] * s2 + g_ref[2, i] * s3
            s_ref[f, i] = q1
            out_ref[f, i] = product(bwd_ref[...], jnp.concatenate([q2, q3], axis=0))
        return carry

    lax.fori_loop(0, NODES, middle, 0)

    def last(n, carry):
        f = n // NODES
        rows = pl.ds(pl.multiple_of((n % NODES) * NODES, NODES), NODES)
        layers = [s_ref[f, k, rows, :] for k in range(NODES)]
        for k, value in enumerate(even_odd(DERIV.T, layers)):
            out_ref[f, k, rows, :] += value
        return carry

    lax.fori_loop(0, fields * NODES, last, 0)


def inverse_code(code):
    swapped = 4 + 2 * (code & 1) + ((code >> 1) & 1)
    return jnp.where((code & 4) != 0, swapped, code)


def lane_pick(values, index):
    return jnp.take_along_axis(values, index, axis=1, mode="promise_in_bounds")


def pair_flux(own, peer, code):
    lane = lax.broadcasted_iota(jnp.int32, code.shape, 1)
    node = lane & (FACE - 1)
    swapped = ((node & (NODES - 1)) << 3) | (node >> 3)
    source = jnp.where((code & 4) != 0, swapped, node)
    source = source ^ ((code & 1) * 56) ^ (((code >> 1) & 1) * 7)
    both = source | (lane & FACE)
    v1 = own[:, 0:LANES]
    g1 = own[:, LANES : 2 * LANES]
    wm1 = own[:, 2 * LANES :]
    v2 = lane_pick(peer[:, 0:LANES], both)
    g2 = lane_pick(peer[:, LANES : 2 * LANES], both)
    wm2 = peer[:, 2 * LANES :]
    w2 = lane_pick(wm2, source)
    m2 = lane_pick(wm2, source + FACE)
    w1 = lane_pick(wm1, node)
    m1 = lane_pick(wm1, node + FACE)
    penalty = NODES * (NODES + 1) / 2.0
    jump = v1 - v2
    weight = 0.5 * (w1 + w2)
    tau = (penalty * 0.5) * (m1 + m2)
    value = weight * (tau * jump - 0.5 * (g1 - g2))
    lift = (-0.5 * weight * jump) * m1
    return value, lift


def combine_kernel(
    slots, pairs, slots_v, pairs_v, own_ref, recv_ref, t_ref, vol_ref, rhs_ref, lift_ref, modes_ref,
    cells_ref, res_ref, sums_ref, vt, lt, lb, vb, hb, cb, pad, fv, fl, cs,
):
    elems = t_ref.shape[0] // 6
    slot_total = own_ref.shape[0]
    pair_total = lb.shape[0] // 2
    width = slot_total // 9
    fields = 2

    def clear(n, carry):
        rows = pl.ds(pl.multiple_of(n * FACE, FACE), FACE)
        zero = jnp.zeros((FACE, LANES), jnp.float32)
        vt[rows, :] = zero
        lt[rows, :] = zero
        return carry

    lax.fori_loop(0, vt.shape[0] // FACE, clear, 0)

    def gather(c, carry):
        first = pairs[1, c] * elems + pairs[0, c]
        second = pairs[3, c] * elems + pairs[2, c]
        lb[pl.ds(c, 1), :] = t_ref[pl.ds(first, 1), :]
        lb[pl.ds(c + pair_total, 1), :] = t_ref[pl.ds(second, 1), :]
        return carry

    lax.fori_loop(0, pair_total, gather, 0, unroll=8)

    raw = slots_v[4]
    code = jnp.where(slots_v[3] != 0, raw, inverse_code(raw)) + 8 * slots_v[2]
    pad[0:1, 0:slot_total] = code.astype(jnp.float32)
    pad[0:1, slot_total:] = jnp.zeros((1, pad.shape[1] - slot_total), jnp.float32)
    for t in range(pad.shape[1] // LANES):
        row = jnp.broadcast_to(pad[0:1, t * LANES : (t + 1) * LANES], (LANES, LANES))
        rows = min(LANES, slot_total - t * LANES)
        cb[t * LANES : t * LANES + rows, :] = row.T.astype(jnp.int32)[:rows]
    local = pairs_v[4:5, :]
    for side, codes in enumerate((local, inverse_code(local))):
        for t in range(pair_total // LANES):
            row = codes[:, t * LANES : (t + 1) * LANES].astype(jnp.float32)
            start = slot_total + side * pair_total + t * LANES
            cb[start : start + LANES, :] = jnp.broadcast_to(row, (LANES, LANES)).T.astype(jnp.int32)

    def cross_flux(n, carry):
        rows = pl.ds(pl.multiple_of(n * 8, 8), 8)
        codes = cb[rows, :]
        value, lift = pair_flux(own_ref[rows, :], recv_ref[rows, :], codes & 7)
        live = codes >= 8
        vb[rows, :] = jnp.where(live, value, 0.0)
        hb[rows, :] = jnp.where(live, lift, 0.0)
        return carry

    lax.fori_loop(0, slot_total // 8, cross_flux, 0, unroll=2)

    def local_flux(n, carry):
        first = pl.ds(pl.multiple_of(n * 8, 8), 8)
        second = pl.ds(pl.multiple_of(n * 8 + pair_total, 8), 8)
        for own, peer in ((first, second), (second, first)):
            rows = pl.ds(pl.multiple_of(own.start + slot_total, 8), 8)
            value, lift = pair_flux(lb[own, :], lb[peer, :], cb[rows, :])
            vb[rows, :] = value
            hb[rows, :] = lift
        return carry

    lax.fori_loop(0, pair_total // 8, local_flux, 0)

    def scatter_cross(c, carry):
        row = slots[1, 0, c] * elems + slots[0, 0, c]
        vt[pl.ds(row, 1), :] = vb[pl.ds(c, 1), :]
        lt[pl.ds(row, 1), :] = hb[pl.ds(c, 1), :]
        return carry

    lax.fori_loop(0, slot_total, scatter_cross, 0, unroll=8)

    def scatter_local(c, carry):
        first = pairs[1, c] * elems + pairs[0, c]
        second = pairs[3, c] * elems + pairs[2, c]
        one = slot_total + c
        two = one + pair_total
        vt[pl.ds(first, 1), :] = vb[pl.ds(one, 1), :]
        lt[pl.ds(first, 1), :] = hb[pl.ds(one, 1), :]
        vt[pl.ds(second, 1), :] = vb[pl.ds(two, 1), :]
        lt[pl.ds(second, 1), :] = hb[pl.ds(two, 1), :]
        return carry

    lax.fori_loop(0, pair_total, scatter_local, 0, unroll=4)

    def turn(face, carry):
        for t in range(elems // LANES):
            rows = pl.ds(pl.multiple_of(face * elems + t * LANES, LANES), LANES)
            cols = slice(t * LANES, (t + 1) * LANES)
            value = vt[rows, :].T
            lift = lt[rows, :].T
            for f in range(fields):
                fv[f, face, :, cols] = value[f * FACE : (f + 1) * FACE]
                fl[f, face, :, cols] = lift[f * FACE : (f + 1) * FACE]
        return carry

    lax.fori_loop(0, 6, turn, 0)

    half = elems // 2

    def finish(n, carry):
        f = n // 2
        cols = pl.ds(pl.multiple_of((n % 2) * half, half), half)
        low_lift = fl[f, 0, :, cols]
        high_lift = fl[f, 1, :, cols]
        coarse = [None, None]
        for i in range(NODES):
            part = slice(i * NODES, (i + 1) * NODES)
            stack = []
            for face in range(2, 6):
                stack += [fv[f, face, part, cols], fl[f, face, part, cols]]
            value = rhs_ref[f, i, :, cols] - vol_ref[f, i, :, cols]
            value = value - product(lift_ref[...], jnp.concatenate(stack, axis=0))
            value = value + float(DERIV[0, i]) * low_lift - float(DERIV[-1, i]) * high_lift
            if i == 0:
                value = value - fv[f, 0, :, cols]
            if i == NODES - 1:
                value = value - fv[f, 1, :, cols]
            res_ref[f, i, :, cols] = value
            for a in range(2):
                if MODES[i, a] != 0.0:
                    term = float(MODES[i, a]) * value
                    coarse[a] = term if coarse[a] is None else coarse[a] + term
        for a in range(2):
            for b in range(2):
                layers = [coarse[a][j * NODES : (j + 1) * NODES] for j in range(NODES)]
                level = weighted(MODES[:, b], layers)
                for c in range(2):
                    column = modes_ref[c * NODES : (c + 1) * NODES, 0:1]
                    row = f * NODES + 4 * a + 2 * b + c
                    cs[pl.ds(row, 1), cols] = jnp.sum(level * column, axis=0, keepdims=True)
        return carry

    lax.fori_loop(0, 2 * fields, finish, 0)

    row_cells = sums_ref.shape[1]
    hot = lax.broadcasted_iota(jnp.int32, (row_cells, elems), 0) == cells_ref[...]
    hot = hot.astype(jnp.float32).astype(jnp.bfloat16)
    coarse = cs[...]
    high = coarse.astype(jnp.bfloat16)
    low = (coarse - high.astype(jnp.float32)).astype(jnp.bfloat16)
    both = lax.dot_general(
        jnp.concatenate([high, low], axis=0),
        hot,
        (((1,), (1,)), ((), ())),
        preferred_element_type=jnp.float32,
    )
    sums_ref[...] = both[: coarse.shape[0]] + both[coarse.shape[0] :]


def reduce_kernel(n_sub, sums_ref, total_ref, box, send_sem, recv_sem):
    place = lax.axis_index("blk")
    sub = lax.axis_index("sub")
    barrier = pltpu.get_barrier_semaphore()
    peers = [(place, lax.rem(sub + step, n_sub)) for step in range(1, n_sub)]
    for peer in peers:
        pl.semaphore_signal(barrier, inc=1, device_id=peer, device_id_type=MESH)
    pl.semaphore_wait(barrier, n_sub - 1)
    copies = []
    for step, peer in enumerate(peers):
        copies.append(
            pltpu.make_async_remote_copy(
                src_ref=sums_ref,
                dst_ref=box.at[step],
                send_sem=send_sem.at[step],
                recv_sem=recv_sem.at[step],
                device_id=peer,
                device_id_type=MESH,
            )
        )
        copies[-1].start()
    for copy in copies:
        copy.wait()
    total = sums_ref[...]
    for step in range(n_sub - 1):
        total = total + box[step]
    total_ref[...] = total


def correct_kernel(total_ref, inverse_ref, cells_ref, modes_ref, p_ref, out_ref):
    fields = p_ref.shape[0]
    elems = p_ref.shape[-1]
    row_cells = total_ref.shape[1]
    rows = []
    for f in range(fields):
        level = None
        for j in range(NODES):
            term = inverse_ref[j] * total_ref[f * NODES + j : f * NODES + j + 1, :]
            level = term if level is None else level + term
        rows.append(level)
    level = jnp.concatenate(rows, axis=0)
    high = level.astype(jnp.bfloat16)
    low = (level - high.astype(jnp.float32)).astype(jnp.bfloat16)
    hot = lax.broadcasted_iota(jnp.int32, (row_cells, elems), 0) == cells_ref[...]
    hot = hot.astype(jnp.float32).astype(jnp.bfloat16)
    spread = lax.dot_general(
        jnp.concatenate([high, low], axis=0),
        hot,
        (((1,), (0,)), ((), ())),
        preferred_element_type=jnp.float32,
    )
    spread = spread[: level.shape[0]] + spread[level.shape[0] :]
    columns = [modes_ref[c * NODES : (c + 1) * NODES, 0:1] for c in range(2)]
    for f in range(fields):
        planes = []
        for a in range(2):
            lines = []
            for b in range(2):
                start = f * NODES + 4 * a + 2 * b
                lines.append(
                    columns[0] * spread[start : start + 1] + columns[1] * spread[start + 1 : start + 2]
                )
            planes.append([weighted(MODES[j], lines) for j in range(NODES)])
        for j in range(NODES):
            part = slice(j * NODES, (j + 1) * NODES)
            for i in range(NODES):
                grown = weighted(MODES[i], [planes[0][j], planes[1][j]])
                out_ref[f, i, part, :] = p_ref[f, i, part, :] + grown


def whole(shape, space=VMEM):
    return pl.BlockSpec(shape, lambda *_: (0,) * len(shape), memory_space=space)


def limits(mib, **extra):
    return pltpu.CompilerParams(vmem_limit_bytes=mib << 20, **extra)


def shaped(*shape):
    return jax.ShapeDtypeStruct(shape, jnp.float32)


def on_device(
    n_blk,
    n_sub,
    pressure,
    right_side,
    geometry,
    face_weight,
    face_metric,
    cross_slots,
    local_pairs,
    coarse_map,
    coarse_inverse,
):
    fields = pressure.shape[0]
    elems = pressure.shape[-1]
    slot_total = cross_slots.shape[2]
    pair_total = local_pairs.shape[1]
    row_cells = coarse_inverse.shape[-1]
    tiles = elems // LANES
    record = 3 * LANES
    slabs = (fields, NODES, FACE, elems)
    flat_p = pressure.reshape(fields * BRICK, elems)
    p = pressure.reshape(slabs)
    weights = jnp.transpose(face_weight, (1, 0, 2))
    metrics = jnp.transpose(face_metric, (1, 0, 2))
    cells = coarse_map.reshape(1, elems)
    modes = jnp.asarray(np.repeat(MODES.T.reshape(2 * NODES, 1), LANES, axis=1), jnp.float32)

    table, send = pl.pallas_call(
        pack_kernel,
        grid=(tiles,),
        in_specs=[
            whole(cross_slots.shape, SMEM),
            pl.BlockSpec((fields * BRICK, LANES), lambda t: (0, t)),
            pl.BlockSpec((6, FACE, LANES), lambda t: (0, 0, t)),
            pl.BlockSpec((6, FACE, LANES), lambda t: (0, 0, t)),
        ],
        out_specs=[whole((6 * elems, record)), whole((slot_total, record))],
        out_shape=[shaped(6 * elems, record), shaped(slot_total, record)],
        compiler_params=limits(32),
        name="pack",
    )(cross_slots, flat_p, weights, metrics)

    received = pl.pallas_call(
        functools.partial(exchange_kernel, n_blk, n_sub),
        in_specs=[pl.BlockSpec(memory_space=VMEM)],
        out_specs=pl.BlockSpec(memory_space=VMEM),
        out_shape=shaped(slot_total, record),
        scratch_shapes=[pltpu.SemaphoreType.DMA((9,)), pltpu.SemaphoreType.DMA((9,))],
        compiler_params=limits(8, collective_id=0, has_side_effects=True),
        name="exchange",
    )(send)

    chunk = min(elems, 256)
    volume = pl.pallas_call(
        volume_kernel,
        grid=(elems // chunk,),
        in_specs=[
            pl.BlockSpec((fields, NODES, FACE, chunk), lambda t: (0, 0, 0, t)),
            pl.BlockSpec((6, NODES, FACE, chunk), lambda t: (0, 0, 0, t)),
            whole((2 * FACE, 3 * FACE)),
            whole((FACE, 6 * FACE)),
        ],
        out_specs=pl.BlockSpec((fields, NODES, FACE, chunk), lambda t: (0, 0, 0, t)),
        out_shape=shaped(*slabs),
        scratch_shapes=[pltpu.VMEM((fields, NODES, FACE, chunk), jnp.float32)],
        compiler_params=limits(32),
        name="volume",
    )(p, geometry.reshape(6, NODES, FACE, elems), jnp.asarray(forward_table()), jnp.asarray(backward_table()))

    pad_width = -(-slot_total // LANES) * LANES
    side_total = slot_total + 2 * pair_total
    residual, sums = pl.pallas_call(
        combine_kernel,
        in_specs=[
            pl.BlockSpec(memory_space=SMEM),
            pl.BlockSpec(memory_space=SMEM),
        ]
        + [pl.BlockSpec(memory_space=VMEM)] * 10,
        out_specs=[pl.BlockSpec(memory_space=VMEM)] * 2,
        out_shape=[shaped(*slabs), shaped(fields * NODES, row_cells)],
        scratch_shapes=[
            pltpu.VMEM((6 * elems, LANES), jnp.float32),
            pltpu.VMEM((6 * elems, LANES), jnp.float32),
            pltpu.VMEM((2 * pair_total, record), jnp.float32),
            pltpu.VMEM((side_total, LANES), jnp.float32),
            pltpu.VMEM((side_total, LANES), jnp.float32),
            pltpu.VMEM((side_total, LANES), jnp.int32),
            pltpu.VMEM((8, pad_width), jnp.float32),
            pltpu.VMEM((fields, 6, FACE, elems), jnp.float32),
            pltpu.VMEM((fields, 6, FACE, elems), jnp.float32),
            pltpu.VMEM((fields * NODES, elems), jnp.float32),
        ],
        compiler_params=limits(48),
        name="combine",
    )(
        cross_slots, local_pairs, cross_slots, local_pairs, send, received, table, volume,
        right_side.reshape(slabs), jnp.asarray(lift_table()), modes, cells,
    )

    totals = pl.pallas_call(
        functools.partial(reduce_kernel, n_sub),
        in_specs=[pl.BlockSpec(memory_space=VMEM)],
        out_specs=pl.BlockSpec(memory_space=VMEM),
        out_shape=shaped(fields * NODES, row_cells),
        scratch_shapes=[
            pltpu.VMEM((n_sub - 1, fields * NODES, row_cells), jnp.float32),
            pltpu.SemaphoreType.DMA((n_sub - 1,)),
            pltpu.SemaphoreType.DMA((n_sub - 1,)),
        ],
        compiler_params=limits(8, collective_id=1, has_side_effects=True),
        name="reduce",
    )(sums)

    corrected = pl.pallas_call(
        correct_kernel,
        grid=(elems // chunk,),
        in_specs=[
            whole((fields * NODES, row_cells)),
            whole((NODES, NODES, row_cells)),
            pl.BlockSpec((1, chunk), lambda t: (0, t)),
            whole((2 * NODES, LANES)),
            pl.BlockSpec((fields, NODES, FACE, chunk), lambda t: (0, 0, 0, t)),
        ],
        out_specs=pl.BlockSpec((fields, NODES, FACE, chunk), lambda t: (0, 0, 0, t)),
        out_shape=shaped(*slabs),
        compiler_params=limits(32),
        name="correct",
    )(totals, coarse_inverse, cells, modes, p)
    return residual.reshape(pressure.shape), corrected.reshape(pressure.shape)


def solution(mesh):
    return jax.shard_map(
        functools.partial(on_device, mesh.shape["blk"], mesh.shape["sub"]),
        mesh=mesh,
        in_specs=(
            P(None, None, None, None, ("blk", "sub")),
            P(None, None, None, None, ("blk", "sub")),
            P(None, None, None, None, ("blk", "sub")),
            P(None, None, ("blk", "sub")),
            P(None, None, ("blk", "sub")),
            P(None, ("blk", "sub"), None),
            P(None, ("blk", "sub")),
            P(("blk", "sub")),
            P(None, None, "blk"),
        ),
        out_specs=(
            P(None, None, None, None, ("blk", "sub")),
            P(None, None, None, None, ("blk", "sub")),
        ),
        check_vma=False,
    )
```

time: 480 us -> 76 us (0.16); the launches traced: 472 us -> 75.7 us
  matrix products: 165 us -> 0 us
  local copies, waits for them, and re-layouts: 168 us -> 8.18 us
  other arithmetic: 82.6 us -> 0 us
  Pallas kernels: 0 us -> 66.7 us
  starting transfers between devices: 28.7 us -> 0 us
  blocking collectives: 14.5 us -> 0 us
  waiting for transfers between devices: 10.4 us -> 0 us
    dot_general x49 -> x0, matrix products: 165 us -> none  [the longest x18 53 us: apply_along(): lax.dot_general(tiled, shaped, (((2,), (1,)), ((0,), (0,))), precision=pr...]
    pallas_call x0 -> x6, Pallas kernels: none -> 66.7 us  [the longest x1 28.9 us: on_device(): pl.pallas_call(combine_kernel, in_specs=[pl.BlockSpec(memory_space=SMEM),...]
    unnamed x330 -> x30, local copies, waits for them, and re-layouts: 48.4 us -> 8.18 us
    add x8 -> x0, other arithmetic: 37 us -> none  [the longest x6 34.1 us: lift_faces(): running = running + factor * face_rows[row_index]]
    ppermute x16 -> x0, starting transfers between devices: 28.7 us -> none  [the longest x8 26.5 us: extended(): lax.ppermute(head, axis, [((i + 1) % count, i) for i in range(count)])]
    another operation x32 -> x0, local copies, waits for them, and re-layouts: 27.9 us -> none  [the longest x18 13.9 us: face_tables(): value_all = jnp.stack(values, axis=2)]
    slice x19 -> x0, local copies, waits for them, and re-layouts: 25 us -> none  [the longest x1 9.34 us: edge_values(): lax.index_in_dim(fields, node_index, axis, keepdims=False)]
    reshape x13 -> x0, local copies, waits for them, and re-layouts: 24.2 us -> none  [the longest x4 8.74 us: apply_along(): shaped = operand.reshape(before, shape_all[axis], -1)]
  transfers between devices with their start and end apart: 16 -> 0, of which waited for: 4 -> 0; matrix products, arithmetic and copies ran while one was open for 48% -> 0% of each run, Pallas kernels for 0% -> 0%
where the time goes in v1:
time: 76 us; the launch traced here: 75.7 us
  Pallas kernels  66.7 us (88%)
  local copies, waits for them, and re-layouts  8.18 us (11%)
  between operations  0.81 us (1%)
    pallas_call x1, Pallas kernels, on_device(): pl.pallas_call(combine_kernel, in_specs=[pl.BlockSpec(memory_space=SMEM),...  28.9 us
    pallas_call x1, Pallas kernels, on_device(): pl.pallas_call(functools.partial(exchange_kernel, n_blk, n_sub), in_specs...  14.4 us
    pallas_call x1, Pallas kernels, on_device(): pl.pallas_call(volume_kernel, grid=(elems // chunk,), in_specs=[pl.BlockS...  9.48 us
    unnamed x30, local copies, waits for them, and re-layouts  8.18 us
    pallas_call x1, Pallas kernels, on_device(): pl.pallas_call(pack_kernel, grid=(tiles,), in_specs=[whole(cross_slots.sh...  6.35 us
    pallas_call x1, Pallas kernels, on_device(): pl.pallas_call(functools.partial(reduce_kernel, n_sub), in_specs=[pl.Bloc...  5.82 us
    pallas_call x1, Pallas kernels, on_device(): pl.pallas_call(correct_kernel, grid=(elems // chunk,), in_specs=[whole((f...  1.81 us

profile of v1, /device:TPU:0, one launch (start us, length us, event | category | flops | bytes accessed | tf_op | source)
XLA Modules:
  0.0 75.7 jit_solution(16922794347373603805)
XLA Ops:
  0.6 0.0 copy-start
  0.6 1.6 %copy-done = f32[2,8,8,8,512]{4,3,2,1,0:T(8,128)S(1)} copy-done((f32[2,8,8,8,512]{4,3,2,1,0:T(8,128)S(1)}, f32[2,8,8,8,512]{4,3,2,1,0:T(8,128)}, u32[]{:S(2)}) %copy-start) | copy-done | bytes 2097176
  2.2 0.0 copy-start.2
  2.2 2.8 %copy-done.2 = f32[6,8,8,8,512]{4,3,2,1,0:T(8,128)S(1)} copy-done((f32[6,8,8,8,512]{4,3,2,1,0:T(8,128)S(1)}, f32[6,8,8,8,512]{4,3,2,1,0:T(8,128)}, u32[]{:S(2)}) %copy-start.2) | copy-done | bytes 6291480
  5.0 0.0 copy-start.10
  5.0 0.8 %copy-done.10 = bf16[128,192]{1,0:T(8,128)(2,1)S(1)} copy-done((bf16[128,192]{1,0:T(8,128)(2,1)S(1)}, bf16[128,192]{1,0:T(8,128)(2,1)}, u32[]{:S(2)}) %copy-start.10) | copy-done | bytes 49176
  5.8 0.0 copy-start.11
  5.9 0.8 %copy-done.11 = bf16[64,384]{1,0:T(8,128)(2,1)S(1)} copy-done((bf16[64,384]{1,0:T(8,128)(2,1)S(1)}, bf16[64,384]{1,0:T(8,128)(2,1)}, u32[]{:S(2)}) %copy-start.11) | copy-done | bytes 49176
  6.6 0.0 copy-start.1
  6.6 0.0 copy-start.5
  6.7 0.0 copy-start.6
  6.7 0.0 copy-start.7
  6.7 9.5 %volume.1.vol_ref = f32[2,8,64,512]{3,2,1,0:T(8,128)S(1)} custom-call(f32[2,8,64,512]{3,2,1,0:T(8,128)S(1)} %bitcast.9, f32[6,8,64,512]{3,2,1,0:T(8,128)S(1)} %bitcast.12, bf16[128,192]{1,0:T(8,128)(2,1)S(1)} %copy-done.10, bf16[64,384]{1,0:T(8,128)(2,1)S(1)} %copy-done.11), custom_call_target="tpu_custom_call" | custom-call | tf_op jit(solution)/shard_map/volume/pallas_call | solution.py:550
  16.1 0.0 copy-done.1
  16.2 0.0 copy-done.5
  16.2 0.0 copy-done.6
  16.2 0.0 copy-done.7
  16.2 0.0 copy-start.4
  16.2 0.0 copy-start.9
  16.2 0.0 copy-start.12
  16.2 0.0 copy-start.13
  16.2 0.0 copy-start.14
  16.2 6.3 %pack.1 = (f32[3072,384]{1,0:T(8,128)S(1)}, f32[576,384]{1,0:T(8,128)S(1)}) custom-call(s32[5,1,576]{2,1,0:T(1,128)S(1)} %copy-done.7, f32[1024,512]{1,0:T(8,128)S(1)} %bitcast.10, f32[6,64,512]{2,1,0:T(8,128)S(1)} %bitcast.14, f32[6,64,512]{2,1,0:T(8,128)S(1)} %bitcast.15), custom_call_target="tpu_custom_call" | custom-call | tf_op jit(solution)/shard_map/pack/pallas_call | solution.py:524
  22.6 0.0 copy-start.3
  22.6 2.1 %copy-done.3 = f32[3072,384]{1,0:T(8,128)} copy-done((f32[3072,384]{1,0:T(8,128)}, f32[3072,384]{1,0:T(8,128)S(1)}, u32[]{:S(2)}) %copy-start.3) | copy-done | bytes 4718616
  24.7 14.4 %exchange.1.recv_ref = f32[576,384]{1,0:T(8,128)S(1)} custom-call(f32[576,384]{1,0:T(8,128)S(1)} %get-tuple-element.6.send_ref.own_ref), custom_call_target="tpu_custom_call" | custom-call | tf_op jit(solution)/shard_map/exchange/pallas_call | solution.py:539
  39.1 0.0 copy-done.4
  39.1 0.0 copy-done.9
  39.2 0.0 copy-done.12
  39.2 0.0 copy-done.13
  39.2 0.0 copy-done.14
  39.2 0.0 copy-start.8
  39.2 28.9 %combine.1 = (f32[2,8,64,512]{3,2,1,0:T(8,128)}, f32[16,256]{1,0:T(8,128)S(1)}) custom-call(s32[5,1,576]{2,1,0:T(1,128)S(1)} %copy-done.7, s32[5,512]{1,0:T(8,128)S(1)} %copy-done.9, s32[5,1,576]{2,1,0:T(1,128)S(1)} %copy-done.7, s32[5,512]{1,0:T(8,128)S(1)} %copy-done.9, f32[576,384]{1,0:T(8,128)S(1)} %get-tuple-element.6.send_ref.own_ref, ...), custom_call_target="tpu_custom_call" | custom-call | tf_op jit(solution)/shard_map/combine/pallas_call | solution.py:568
  68.1 5.8 %reduce.1.total_ref = f32[16,256]{1,0:T(8,128)S(1)} custom-call(f32[16,256]{1,0:T(8,128)S(1)} %get-tuple-element.9.sums_ref), custom_call_target="tpu_custom_call" | custom-call | tf_op jit(solution)/shard_map/reduce/pallas_call | solution.py:596
  73.9 0.0 copy-done.8
  73.9 1.8 %correct.1 = f32[2,8,64,512]{3,2,1,0:T(8,128)} custom-call(f32[16,256]{1,0:T(8,128)S(1)} %reduce.1.total_ref, f32[8,8,256]{2,1,0:T(8,128)S(1)} %copy-done.8, s32[1,512]{1,0:T(1,128)S(1)} %bitcast.17, f32[16,128]{1,0:T(8,128)S(1)} %copy-done.13, f32[2,8,64,512]{3,2,1,0:T(8,128)S(1)} %bitcast.11), custom_call_target="tpu_custom_call" | custom-call | tf_op jit(solution)/shard_map/correct/pallas_call | solution.py:610
Async XLA Ops:
  0.6 1.6 %copy-start = (f32[2,8,8,8,512]{4,3,2,1,0:T(8,128)S(1)}, f32[2,8,8,8,512]{4,3,2,1,0:T(8,128)}, u32[]{:S(2)}) copy-start(f32[2,8,8,8,512]{4,3,2,1,0:T(8,128)} %param.13) | copy-start | bytes 6291460
  2.2 2.8 %copy-start.2 = (f32[6,8,8,8,512]{4,3,2,1,0:T(8,128)S(1)}, f32[6,8,8,8,512]{4,3,2,1,0:T(8,128)}, u32[]{:S(2)}) copy-start(f32[6,8,8,8,512]{4,3,2,1,0:T(8,128)} %param.15) | copy-start | bytes 18874372
  5.0 0.8 %copy-start.10 = (bf16[128,192]{1,0:T(8,128)(2,1)S(1)}, bf16[128,192]{1,0:T(8,128)(2,1)}, u32[]{:S(2)}) copy-start(bf16[128,192]{1,0:T(8,128)(2,1)} %constant.9.clone.fwd_ref) | copy-start | bytes 147460
  5.8 0.8 %copy-start.11 = (bf16[64,384]{1,0:T(8,128)(2,1)S(1)}, bf16[64,384]{1,0:T(8,128)(2,1)}, u32[]{:S(2)}) copy-start(bf16[64,384]{1,0:T(8,128)(2,1)} %constant.10.clone.bwd_ref) | copy-start | bytes 147460
  6.6 9.5 %copy-start.1 = (f32[2,8,8,8,512]{4,3,2,1,0:T(8,128)S(1)}, f32[2,8,8,8,512]{4,3,2,1,0:T(8,128)}, u32[]{:S(2)}) copy-start(f32[2,8,8,8,512]{4,3,2,1,0:T(8,128)} %param.13) | copy-start | bytes 6291460
  6.6 9.5 %copy-start.5 = (f32[64,6,512]{2,0,1:T(8,128)S(1)}, f32[64,6,512]{2,0,1:T(8,128)}, u32[]{:S(2)}) copy-start(f32[64,6,512]{2,0,1:T(8,128)} %param.16) | copy-start | bytes 2359300
  6.7 9.5 %copy-start.6 = (f32[64,6,512]{2,0,1:T(8,128)S(1)}, f32[64,6,512]{2,0,1:T(8,128)}, u32[]{:S(2)}) copy-start(f32[64,6,512]{2,0,1:T(8,128)} %param.17) | copy-start | bytes 2359300
  6.7 9.5 %copy-start.7 = (s32[5,1,576]{2,1,0:T(1,128)S(1)}, s32[5,1,576]{2,1,0:T(1,128)}, u32[]{:S(2)}) copy-start(s32[5,1,576]{2,1,0:T(1,128)} %slots_v.1) | copy-start | bytes 34564
  16.2 23.0 %copy-start.4 = (f32[2,8,8,8,512]{4,3,2,1,0:T(8,128)S(1)}, f32[2,8,8,8,512]{4,3,2,1,0:T(8,128)}, u32[]{:S(2)}) copy-start(f32[2,8,8,8,512]{4,3,2,1,0:T(8,128)} %param.14) | copy-start | bytes 6291460
  16.2 22.9 %copy-start.9 = (s32[5,512]{1,0:T(8,128)S(1)}, s32[5,512]{1,0:T(8,128)}, u32[]{:S(2)}) copy-start(s32[5,512]{1,0:T(8,128)} %pairs_v.1) | copy-start | bytes 30724
  16.2 22.9 %copy-start.12 = (bf16[64,192]{1,0:T(8,128)(2,1)S(1)}, bf16[64,192]{1,0:T(8,128)(2,1)}, u32[]{:S(2)}) copy-start(bf16[64,192]{1,0:T(8,128)(2,1)} %constant.11.clone.lift_ref) | copy-start | bytes 73732
  16.2 22.9 %copy-start.13 = (f32[16,128]{1,0:T(8,128)S(1)}, f32[16,128]{1,0:T(8,128)}, u32[]{:S(2)}) copy-start(f32[16,128]{1,0:T(8,128)} %constant.8.clone.modes_ref) | copy-start | bytes 24580
  16.2 22.9 %copy-start.14 = (s32[512]{0:T(512)S(1)}, s32[512]{0:T(512)}, u32[]{:S(2)}) copy-start(s32[512]{0:T(512)} %param.20) | copy-start | bytes 6148
  22.6 2.1 %copy-start.3 = (f32[3072,384]{1,0:T(8,128)}, f32[3072,384]{1,0:T(8,128)S(1)}, u32[]{:S(2)}) copy-start(f32[3072,384]{1,0:T(8,128)S(1)} %get-tuple-element.7.t_ref) | copy-start | bytes 14155780
  39.2 34.7 %copy-start.8 = (f32[8,8,256]{2,1,0:T(8,128)S(1)}, f32[8,8,256]{2,1,0:T(8,128)}, u32[]{:S(2)}) copy-start(f32[8,8,256]{2,1,0:T(8,128)} %inverse_ref.1) | copy-start | bytes 196612

commit v2 on v1

v2 whole, which is shorter than its diff:
```python
import functools

import jax
import jax.numpy as jnp
import numpy as np
from jax import lax
from jax.experimental import pallas as pl
from jax.experimental.pallas import tpu as pltpu
from jax.sharding import PartitionSpec as P

NODES = 8
FACE = NODES * NODES
BRICK = NODES * FACE
LANES = 128
MESH = pl.DeviceIdType.MESH
VMEM = pltpu.MemorySpace.VMEM
SMEM = pltpu.MemorySpace.SMEM


def node_points():
    positive = [0.2092992179024789, 0.5917001814331423, 0.8717401485096066, 1.0]
    return np.array(sorted([-entry for entry in positive] + positive))


def derivative_matrix():
    points = node_points()
    count = len(points)
    weights = np.array(
        [
            1.0 / np.prod([points[row] - points[col] for col in range(count) if col != row])
            for row in range(count)
        ]
    )
    matrix = np.zeros((count, count))
    for row in range(count):
        for col in range(count):
            if row != col:
                matrix[row, col] = weights[col] / weights[row] / (points[row] - points[col])
        matrix[row, row] = -np.sum(matrix[row])
    return matrix


DERIV = derivative_matrix()
POINTS = node_points()
MODES = np.stack([(1.0 - POINTS) / 2.0, (1.0 + POINTS) / 2.0], axis=1)


def split_constant(matrix):
    high = matrix.astype(jnp.bfloat16)
    low = (matrix - high.astype(np.float64)).astype(jnp.bfloat16)
    return np.concatenate([high, low, high], axis=1)


def forward_table():
    eye = np.eye(NODES)
    return split_constant(np.kron(eye, DERIV))


def backward_table():
    eye = np.eye(NODES)
    return split_constant(np.kron(eye, DERIV.T))


def lift_table():
    eye = np.eye(NODES)
    rows = [eye[:, :1], -DERIV[:1].T, eye[:, -1:], DERIV[-1:].T]
    second = [np.kron(row, eye) for row in rows]
    third = [np.kron(eye, row) for row in rows]
    return split_constant(np.concatenate(second + third, axis=1))


def split_rows(values):
    high = values.astype(jnp.bfloat16)
    low = (values - high.astype(jnp.float32)).astype(jnp.bfloat16)
    return jnp.concatenate([high, high, low], axis=0)


def product(table, values):
    return lax.dot_general(
        table, split_rows(values), (((1,), (0,)), ((), ())), preferred_element_type=jnp.float32
    )


def even_odd(matrix, layers):
    half = NODES // 2
    sums = [layers[k] + layers[NODES - 1 - k] for k in range(half)]
    gaps = [layers[k] - layers[NODES - 1 - k] for k in range(half)]
    result = [None] * NODES
    for row in range(half):
        even = None
        odd = None
        for k in range(half):
            first = float((matrix[row, k] + matrix[row, NODES - 1 - k]) / 2)
            second = float((matrix[row, k] - matrix[row, NODES - 1 - k]) / 2)
            even = first * sums[k] if even is None else even + first * sums[k]
            odd = second * gaps[k] if odd is None else odd + second * gaps[k]
        result[row] = odd + even
        result[NODES - 1 - row] = odd - even
    return result


def weighted(coefficients, layers):
    total = None
    for factor, layer in zip(coefficients, layers):
        term = float(factor) * layer
        total = term if total is None else total + term
    return total


def inverse_code(code):
    swapped = 4 + 2 * (code & 1) + ((code >> 1) & 1)
    return jnp.where((code & 4) != 0, swapped, code)


def lane_pick(values, index):
    return jnp.take_along_axis(values, index, axis=1, mode="promise_in_bounds")


def pair_flux(own, peer, code):
    v1, g1, wm1 = own
    v2, g2, wm2 = peer
    lane = lax.broadcasted_iota(jnp.int32, code.shape, 1)
    node = lane & (FACE - 1)
    swapped = ((node & (NODES - 1)) << 3) | (node >> 3)
    source = jnp.where((code & 4) != 0, swapped, node)
    source = source ^ ((code & 1) * 56) ^ (((code >> 1) & 1) * 7)
    both = source | (lane & FACE)
    v2 = lane_pick(v2, both)
    g2 = lane_pick(g2, both)
    w2 = lane_pick(wm2, source)
    m2 = lane_pick(wm2, source + FACE)
    w1 = lane_pick(wm1, node)
    m1 = lane_pick(wm1, node + FACE)
    penalty = NODES * (NODES + 1) / 2.0
    jump = v1 - v2
    weight = 0.5 * (w1 + w2)
    tau = (penalty * 0.5) * (m1 + m2)
    value = weight * (tau * jump - 0.5 * (g1 - g2))
    lift = (-0.5 * weight * jump) * m1
    return value, lift


def row_numbers(slots, pairs, elems, staged, rows, sem):
    staged[0][...] = slots[1] * elems + slots[0]
    staged[1][...] = pairs[1:2] * elems + pairs[0:1]
    staged[2][...] = pairs[3:4] * elems + pairs[2:3]
    return [pltpu.make_async_copy(staged[n], rows[n], sem.at[n]) for n in range(3)]


def code_rows(slots, pairs, pad, cb):
    slot_total = slots.shape[2]
    pair_total = pairs.shape[1]
    raw = slots[4]
    code = jnp.where(slots[3] != 0, raw, inverse_code(raw)) + 8 * slots[2]
    pad[0:1, 0:slot_total] = code.astype(jnp.float32)
    pad[0:1, slot_total:] = jnp.zeros((1, pad.shape[1] - slot_total), jnp.float32)
    for t in range(pad.shape[1] // LANES):
        row = jnp.broadcast_to(pad[0:1, t * LANES : (t + 1) * LANES], (LANES, LANES))
        count = min(LANES, slot_total - t * LANES)
        cb[t * LANES : t * LANES + count, :] = row.T.astype(jnp.int32)[:count]
    local = pairs[4:5, :]
    for side, codes in enumerate((local, inverse_code(local))):
        for t in range(pair_total // LANES):
            row = codes[:, t * LANES : (t + 1) * LANES].astype(jnp.float32)
            start = slot_total + side * pair_total + t * LANES
            cb[start : start + LANES, :] = jnp.broadcast_to(row, (LANES, LANES)).T.astype(jnp.int32)


def aligned(start, size):
    return pl.ds(pl.multiple_of(start, size), size)


def trace_tile(t, elems, p_s, fw_s, fm_s, tables):
    fields = p_s.shape[1] // BRICK
    for axis in range(3):
        values = []
        slopes = []
        for field in range(fields):
            start = field * BRICK
            layers = []
            for k in range(NODES):
                if axis == 0:
                    layers.append(p_s[t, start + k * FACE : start + (k + 1) * FACE, :])
                elif axis == 1:
                    rows = [
                        p_s[t, start + i * FACE + k * NODES : start + i * FACE + (k + 1) * NODES, :]
                        for i in range(NODES)
                    ]
                    layers.append(jnp.concatenate(rows, axis=0))
                else:
                    layers.append(p_s[t, pl.ds(start + k, FACE, stride=NODES), :])
            values.append((layers[0], layers[-1]))
            slopes.append((weighted(-DERIV[0], layers), weighted(DERIV[-1], layers)))
        for side in range(2):
            face = 2 * axis + side
            metric = fm_s[t, face]
            rows = aligned(face * elems + t * LANES, LANES)
            value = jnp.concatenate([entry[side] for entry in values], axis=0)
            slope = jnp.concatenate([entry[side] * metric for entry in slopes], axis=0)
            tables[0][rows, :] = value.T
            tables[1][rows, :] = slope.T
            tables[2][rows, :] = jnp.concatenate([fw_s[t, face], metric], axis=0).T


def volume_half(h, p_s, g_s, fwd, bwd, out, s_ref):
    fields = p_s.shape[1] // BRICK
    tiles = (2 * h, 2 * h + 1)

    def wide(ref, rows):
        return jnp.concatenate([ref[tiles[0], rows, :], ref[tiles[1], rows, :]], axis=1)

    def first(n, carry):
        f = n // NODES
        r = n % NODES
        where = [aligned(f * BRICK + k * FACE + r * NODES, NODES) for k in range(NODES)]
        for q, value in enumerate(even_odd(DERIV, [wide(p_s, rows) for rows in where])):
            s_ref[where[q], :] = value
        return carry

    lax.fori_loop(0, fields * NODES, first, 0, unroll=4)

    def middle(i, carry):
        g = [wide(g_s, aligned(n * BRICK + i * FACE, FACE)) for n in range(6)]
        for f in range(fields):
            rows = aligned(f * BRICK + i * FACE, FACE)
            x = wide(p_s, rows)
            s3 = product(fwd[...], x)
            s2 = jnp.concatenate(
                even_odd(DERIV, [x[j * NODES : (j + 1) * NODES] for j in range(NODES)]), axis=0
            )
            s1 = s_ref[rows, :]
            q1 = g[0] * s1 + g[3] * s2 + g[4] * s3
            q2 = g[3] * s1 + g[1] * s2 + g[5] * s3
            q3 = g[4] * s1 + g[5] * s2 + g[2] * s3
            s_ref[rows, :] = q1
            r2 = jnp.concatenate(
                even_odd(DERIV.T, [q2[j * NODES : (j + 1) * NODES] for j in range(NODES)]), axis=0
            )
            r23 = product(bwd[...], q3) + r2
            out[tiles[0], rows, :] = r23[:, :LANES]
            out[tiles[1], rows, :] = r23[:, LANES:]
        return carry

    lax.fori_loop(0, NODES, middle, 0, unroll=4)

    def last(n, carry):
        f = n // NODES
        r = n % NODES
        where = [aligned(f * BRICK + k * FACE + r * NODES, NODES) for k in range(NODES)]
        for q, value in enumerate(even_odd(DERIV.T, [s_ref[rows, :] for rows in where])):
            out[tiles[0], where[q], :] += value[:, :LANES]
            out[tiles[1], where[q], :] += value[:, LANES:]
        return carry

    lax.fori_loop(0, fields * NODES, last, 0, unroll=4)


def front_kernel(
    n_blk, n_sub,
    slots, pairs, p_hbm, fw_hbm, fm_hbm, g_hbm, fwd, bwd,
    vol, vb, hb,
    p_s, fw_s, fm_s, g_s, s_ref, tv, tg, tw, la, lb, lc, cb, pad, send, recv,
    st0, st1, st2, rw0, rw1, rw2,
    load_sem, geo_sem, row_sem, send_sem, recv_sem,
):
    elems = tv.shape[0] // 6
    tiles = elems // LANES
    slot_total = slots.shape[2]
    pair_total = pairs.shape[1]
    width = slot_total // 9
    tables = (tv, tg, tw)
    locals_ = (la, lb, lc)
    place = lax.axis_index("blk")
    sub = lax.axis_index("sub")

    def peer(k):
        return (
            lax.rem(place + (k // 3 - 1) + n_blk, n_blk),
            lax.rem(sub + (k % 3 - 1) + n_sub, n_sub),
        )

    others = [0, 2, 6, 8, 1, 7, 3, 5]
    loads = []
    for t in range(tiles):
        cols = pl.ds(t * LANES, LANES)
        loads.append(
            [
                pltpu.make_async_copy(p_hbm.at[:, cols], p_s.at[t], load_sem.at[t, 0]),
                pltpu.make_async_copy(fw_hbm.at[:, :, cols], fw_s.at[t], load_sem.at[t, 1]),
                pltpu.make_async_copy(fm_hbm.at[:, :, cols], fm_s.at[t], load_sem.at[t, 2]),
            ]
        )
        for copy in loads[-1]:
            copy.start()
    geo = []
    for t in range(tiles):
        cols = pl.ds(t * LANES, LANES)
        geo.append(pltpu.make_async_copy(g_hbm.at[:, cols], g_s.at[t], geo_sem.at[t]))
        geo[-1].start()
    barrier = pltpu.get_barrier_semaphore()
    for k in others:
        pl.semaphore_signal(barrier, inc=1, device_id=peer(k), device_id_type=MESH)
    numbers = row_numbers(slots, pairs, elems, (st0, st1, st2), (rw0, rw1, rw2), row_sem)
    for copy in numbers:
        copy.start()
    code_rows(slots, pairs, pad, cb)
    for t in range(tiles):
        for copy in loads[t]:
            copy.wait()
        trace_tile(t, elems, p_s, fw_s, fm_s, tables)
    for copy in numbers:
        copy.wait()
    pl.semaphore_wait(barrier, len(others))
    copies = []
    for k in others:

        def gather(n, carry, k=k):
            base = n * 16
            rows = [rw0[0, k * width + base + u] for u in range(16)]
            for j in range(3):
                found = [tables[j][pl.ds(row, 1), :] for row in rows]
                for u in range(16):
                    send[k, j, pl.ds(base + u, 1), :] = found[u]
            return carry

        lax.fori_loop(0, width // 16, gather, 0)
        copies.append(
            pltpu.make_async_remote_copy(
                src_ref=send.at[k],
                dst_ref=recv.at[8 - k],
                send_sem=send_sem.at[k],
                recv_sem=recv_sem.at[8 - k],
                device_id=peer(k),
                device_id_type=MESH,
            )
        )
        copies[-1].start()

    for side, numbers in enumerate((rw1, rw2)):

        def gather_local(n, carry, side=side, numbers=numbers):
            base = n * 16
            rows = [numbers[0, base + u] for u in range(16)]
            for j in range(3):
                found = [tables[j][pl.ds(row, 1), :] for row in rows]
                for u in range(16):
                    locals_[j][pl.ds(side * pair_total + base + u, 1), :] = found[u]
            return carry

        lax.fori_loop(0, pair_total // 16, gather_local, 0)

    def local_flux(n, carry):
        own = aligned(n * LANES, LANES)
        other = aligned((n * LANES + pair_total) % (2 * pair_total), LANES)
        rows = aligned(n * LANES + slot_total, FACE)
        rows = pl.ds(rows.start, LANES)
        value, lift = pair_flux(
            [table[own, :] for table in locals_], [table[other, :] for table in locals_], cb[rows, :]
        )
        vb[rows, :] = value
        hb[rows, :] = lift
        return carry

    lax.fori_loop(0, 2 * pair_total // LANES, local_flux, 0)
    for copy in geo:
        copy.wait()

    def volume(h, carry):
        volume_half(h, p_s, g_s, fwd, bwd, vol, s_ref)
        return carry

    lax.fori_loop(0, tiles // 2, volume, 0)
    for copy in copies:
        copy.wait()

    def cross_flux(n, carry):
        for shift in (0, 5):
            k = n + shift
            rows = aligned(k * width, FACE)
            codes = cb[rows, :]
            value, lift = pair_flux(
                [send[k, j] for j in range(3)], [recv[k, j] for j in range(3)], codes & 7
            )
            live = codes >= 8
            vb[rows, :] = jnp.where(live, value, 0.0)
            hb[rows, :] = jnp.where(live, lift, 0.0)
        return carry

    lax.fori_loop(0, 4, cross_flux, 0)
    vb[4 * width : 5 * width, :] = jnp.zeros((width, LANES), jnp.float32)
    hb[4 * width : 5 * width, :] = jnp.zeros((width, LANES), jnp.float32)


def combine_kernel(
    slots, pairs, vb, hb, vol, rhs, lift_ref, modes, cells,
    res, sums,
    vt, lt, fv, fl, cs, st0, st1, st2, rw0, rw1, rw2, row_sem,
):
    elems = vt.shape[0] // 6
    tiles = elems // LANES
    slot_total = slots.shape[2]
    pair_total = pairs.shape[1]
    fields = 2
    numbers = row_numbers(slots, pairs, elems, (st0, st1, st2), (rw0, rw1, rw2), row_sem)
    for copy in numbers:
        copy.start()

    def clear(n, carry):
        rows = aligned(n * LANES, LANES)
        zero = jnp.zeros((LANES, LANES), jnp.float32)
        vt[rows, :] = zero
        lt[rows, :] = zero
        return carry

    lax.fori_loop(0, vt.shape[0] // LANES, clear, 0)
    for copy in numbers:
        copy.wait()
    for start, count, numbers in (
        (0, slot_total, rw0),
        (slot_total, pair_total, rw1),
        (slot_total + pair_total, pair_total, rw2),
    ):

        def scatter(n, carry, start=start, numbers=numbers):
            base = n * 16
            rows = [numbers[0, base + u] for u in range(16)]
            for source, table in ((vb, vt), (hb, lt)):
                found = [source[pl.ds(start + base + u, 1), :] for u in range(16)]
                for u in range(16):
                    table[pl.ds(rows[u], 1), :] = found[u]
            return carry

        lax.fori_loop(0, count // 16, scatter, 0)

    for face in range(6):
        for t in range(tiles):
            rows = slice(face * elems + t * LANES, face * elems + (t + 1) * LANES)
            value = vt[rows, :].T
            lift = lt[rows, :].T
            for f in range(fields):
                fv[t, f, face] = value[f * FACE : (f + 1) * FACE]
                fl[t, f, face] = lift[f * FACE : (f + 1) * FACE]

    half = 2 * LANES

    def finish(n, carry):
        f = n // (tiles // 2)
        h = n % (tiles // 2)
        cols = aligned(h * half, half)

        def wide(ref, *where):
            return jnp.concatenate([ref[2 * h, *where], ref[2 * h + 1, *where]], axis=-1)

        low_lift = wide(fl, f, 0)
        high_lift = wide(fl, f, 1)
        coarse = [None, None]
        for i in range(NODES):
            part = slice(i * NODES, (i + 1) * NODES)
            stack = []
            for face in range(2, 6):
                stack += [wide(fv, f, face, part), wide(fl, f, face, part)]
            rows = aligned(f * BRICK + i * FACE, FACE)
            value = rhs[f, i, :, cols] - wide(vol, rows)
            value = value - product(lift_ref[...], jnp.concatenate(stack, axis=0))
            value = value + float(DERIV[0, i]) * low_lift - float(DERIV[-1, i]) * high_lift
            if i == 0:
                value = value - wide(fv, f, 0)
            if i == NODES - 1:
                value = value - wide(fv, f, 1)
            res[f, i, :, cols] = value
            for a in range(2):
                if MODES[i, a] != 0.0:
                    term = float(MODES[i, a]) * value
                    coarse[a] = term if coarse[a] is None else coarse[a] + term
        for a in range(2):
            for b in range(2):
                layers = [coarse[a][j * NODES : (j + 1) * NODES] for j in range(NODES)]
                level = weighted(MODES[:, b], layers)
                for c in range(2):
                    column = modes[c * NODES : (c + 1) * NODES, 0:1]
                    row = f * NODES + 4 * a + 2 * b + c
                    cs[pl.ds(row, 1), cols] = jnp.sum(level * column, axis=0, keepdims=True)
        return carry

    lax.fori_loop(0, fields * tiles // 2, finish, 0)

    row_cells = sums.shape[1]
    hot = lax.broadcasted_iota(jnp.int32, (row_cells, elems), 0) == cells[...]
    hot = hot.astype(jnp.float32).astype(jnp.bfloat16)
    coarse = cs[...]
    high = coarse.astype(jnp.bfloat16)
    low = (coarse - high.astype(jnp.float32)).astype(jnp.bfloat16)
    both = lax.dot_general(
        jnp.concatenate([high, low], axis=0),
        hot,
        (((1,), (1,)), ((), ())),
        preferred_element_type=jnp.float32,
    )
    sums[...] = both[: coarse.shape[0]] + both[coarse.shape[0] :]


def reduce_kernel(n_sub, sums_ref, total_ref, box, send_sem, recv_sem):
    place = lax.axis_index("blk")
    sub = lax.axis_index("sub")
    barrier = pltpu.get_barrier_semaphore()
    peers = [(place, lax.rem(sub + step, n_sub)) for step in range(1, n_sub)]
    for peer in peers:
        pl.semaphore_signal(barrier, inc=1, device_id=peer, device_id_type=MESH)
    pl.semaphore_wait(barrier, n_sub - 1)
    copies = []
    for step, peer in enumerate(peers):
        copies.append(
            pltpu.make_async_remote_copy(
                src_ref=sums_ref,
                dst_ref=box.at[step],
                send_sem=send_sem.at[step],
                recv_sem=recv_sem.at[step],
                device_id=peer,
                device_id_type=MESH,
            )
        )
        copies[-1].start()
    for copy in copies:
        copy.wait()
    total = sums_ref[...]
    for step in range(n_sub - 1):
        total = total + box[step]
    total_ref[...] = total


def correct_kernel(total_ref, inverse_ref, cells_ref, modes_ref, p_ref, out_ref):
    fields = p_ref.shape[0]
    elems = p_ref.shape[-1]
    row_cells = total_ref.shape[1]
    rows = []
    for f in range(fields):
        level = None
        for j in range(NODES):
            term = inverse_ref[j] * total_ref[f * NODES + j : f * NODES + j + 1, :]
            level = term if level is None else level + term
        rows.append(level)
    level = jnp.concatenate(rows, axis=0)
    high = level.astype(jnp.bfloat16)
    low = (level - high.astype(jnp.float32)).astype(jnp.bfloat16)
    hot = lax.broadcasted_iota(jnp.int32, (row_cells, elems), 0) == cells_ref[...]
    hot = hot.astype(jnp.float32).astype(jnp.bfloat16)
    spread = lax.dot_general(
        jnp.concatenate([high, low], axis=0),
        hot,
        (((1,), (0,)), ((), ())),
        preferred_element_type=jnp.float32,
    )
    spread = spread[: level.shape[0]] + spread[level.shape[0] :]
    columns = [modes_ref[c * NODES : (c + 1) * NODES, 0:1] for c in range(2)]
    for f in range(fields):
        planes = []
        for a in range(2):
            lines = []
            for b in range(2):
                start = f * NODES + 4 * a + 2 * b
                lines.append(
                    columns[0] * spread[start : start + 1] + columns[1] * spread[start + 1 : start + 2]
                )
            planes.append([weighted(MODES[j], lines) for j in range(NODES)])
        for j in range(NODES):
            part = slice(j * NODES, (j + 1) * NODES)
            for i in range(NODES):
                grown = weighted(MODES[i], [planes[0][j], planes[1][j]])
                out_ref[f, i, part, :] = p_ref[f, i, part, :] + grown


def whole(shape, space=VMEM):
    return pl.BlockSpec(shape, lambda *_: (0,) * len(shape), memory_space=space)


def limits(mib, **extra):
    return pltpu.CompilerParams(vmem_limit_bytes=mib << 20, **extra)


def shaped(*shape):
    return jax.ShapeDtypeStruct(shape, jnp.float32)


def on_device(
    n_blk,
    n_sub,
    pressure,
    right_side,
    geometry,
    face_weight,
    face_metric,
    cross_slots,
    local_pairs,
    coarse_map,
    coarse_inverse,
):
    fields = pressure.shape[0]
    elems = pressure.shape[-1]
    slot_total = cross_slots.shape[2]
    pair_total = local_pairs.shape[1]
    row_cells = coarse_inverse.shape[-1]
    tiles = elems // LANES
    width = slot_total // 9
    slabs = (fields, NODES, FACE, elems)
    rows = fields * BRICK
    p = pressure.reshape(slabs)
    weights = jnp.transpose(face_weight, (1, 0, 2))
    metrics = jnp.transpose(face_metric, (1, 0, 2))
    cells = coarse_map.reshape(1, elems)
    modes = jnp.asarray(np.repeat(MODES.T.reshape(2 * NODES, 1), LANES, axis=1), jnp.float32)
    pad_width = -(-slot_total // LANES) * LANES
    side_total = slot_total + 2 * pair_total
    f32 = jnp.float32
    i32 = jnp.int32
    inside = pl.BlockSpec(memory_space=VMEM)
    outside = pl.BlockSpec(memory_space=pltpu.MemorySpace.HBM)
    number_scratch = [
        pltpu.VMEM((1, slot_total), i32),
        pltpu.VMEM((1, pair_total), i32),
        pltpu.VMEM((1, pair_total), i32),
        pltpu.SMEM((1, slot_total), i32),
        pltpu.SMEM((1, pair_total), i32),
        pltpu.SMEM((1, pair_total), i32),
    ]
    dma = pltpu.SemaphoreType.DMA

    volume, values, lifts = pl.pallas_call(
        functools.partial(front_kernel, n_blk, n_sub),
        in_specs=[inside] * 2 + [outside] * 4 + [inside] * 2,
        out_specs=[inside] * 3,
        out_shape=[shaped(tiles, rows, LANES), shaped(side_total, LANES), shaped(side_total, LANES)],
        scratch_shapes=[
            pltpu.VMEM((tiles, rows, LANES), f32),
            pltpu.VMEM((tiles, 6, FACE, LANES), f32),
            pltpu.VMEM((tiles, 6, FACE, LANES), f32),
            pltpu.VMEM((tiles, 6 * BRICK, LANES), f32),
            pltpu.VMEM((rows, 2 * LANES), f32),
        ]
        + [pltpu.VMEM((6 * elems, LANES), f32)] * 3
        + [pltpu.VMEM((2 * pair_total, LANES), f32)] * 3
        + [
            pltpu.VMEM((side_total, LANES), i32),
            pltpu.VMEM((8, pad_width), f32),
            pltpu.VMEM((9, 3, width, LANES), f32),
            pltpu.VMEM((9, 3, width, LANES), f32),
        ]
        + number_scratch
        + [dma((tiles, 3)), dma((tiles,)), dma((3,)), dma((9,)), dma((9,))],
        compiler_params=limits(36, collective_id=0, has_side_effects=True),
        name="front",
    )(
        cross_slots,
        local_pairs,
        pressure.reshape(rows, elems),
        weights,
        metrics,
        geometry.reshape(6 * BRICK, elems),
        jnp.asarray(forward_table()),
        jnp.asarray(backward_table()),
    )

    residual, sums = pl.pallas_call(
        combine_kernel,
        in_specs=[inside] * 9,
        out_specs=[inside] * 2,
        out_shape=[shaped(*slabs), shaped(fields * NODES, row_cells)],
        scratch_shapes=[
            pltpu.VMEM((6 * elems, LANES), f32),
            pltpu.VMEM((6 * elems, LANES), f32),
            pltpu.VMEM((tiles, fields, 6, FACE, LANES), f32),
            pltpu.VMEM((tiles, fields, 6, FACE, LANES), f32),
            pltpu.VMEM((fields * NODES, elems), f32),
        ]
        + number_scratch
        + [dma((3,))],
        compiler_params=limits(32),
        name="combine",
    )(
        cross_slots,
        local_pairs,
        values,
        lifts,
        volume,
        right_side.reshape(slabs),
        jnp.asarray(lift_table()),
        modes,
        cells,
    )

    totals = pl.pallas_call(
        functools.partial(reduce_kernel, n_sub),
        in_specs=[inside],
        out_specs=inside,
        out_shape=shaped(fields * NODES, row_cells),
        scratch_shapes=[
            pltpu.VMEM((n_sub - 1, fields * NODES, row_cells), f32),
            dma((n_sub - 1,)),
            dma((n_sub - 1,)),
        ],
        compiler_params=limits(8, collective_id=1, has_side_effects=True),
        name="reduce",
    )(sums)

    chunk = min(elems, 256)
    corrected = pl.pallas_call(
        correct_kernel,
        grid=(elems // chunk,),
        in_specs=[
            whole((fields * NODES, row_cells)),
            whole((NODES, NODES, row_cells)),
            pl.BlockSpec((1, chunk), lambda t: (0, t)),
            whole((2 * NODES, LANES)),
            pl.BlockSpec((fields, NODES, FACE, chunk), lambda t: (0, 0, 0, t)),
        ],
        out_specs=pl.BlockSpec((fields, NODES, FACE, chunk), lambda t: (0, 0, 0, t)),
        out_shape=shaped(*slabs),
        compiler_params=limits(32),
        name="correct",
    )(totals, coarse_inverse, cells, modes, p)
    return residual.reshape(pressure.shape), corrected.reshape(pressure.shape)


def solution(mesh):
    return jax.shard_map(
        functools.partial(on_device, mesh.shape["blk"], mesh.shape["sub"]),
        mesh=mesh,
        in_specs=(
            P(None, None, None, None, ("blk", "sub")),
            P(None, None, None, None, ("blk", "sub")),
            P(None, None, None, None, ("blk", "sub")),
            P(None, None, ("blk", "sub")),
            P(None, None, ("blk", "sub")),
            P(None, ("blk", "sub"), None),
            P(None, ("blk", "sub")),
            P(("blk", "sub")),
            P(None, None, "blk"),
        ),
        out_specs=(
            P(None, None, None, None, ("blk", "sub")),
            P(None, None, None, None, ("blk", "sub")),
        ),
        check_vma=False,
    )
```

time: 76 us -> 46.6 us (0.61)
  Pallas kernels: 66.7 us -> 35.8 us
  local copies, waits for them, and re-layouts: 8.18 us -> 9.6 us
    pallas_call x5 -> x3, Pallas kernels: 64.9 us -> 34 us  [the longest x1 21.8 us: on_device(): pl.pallas_call(functools.partial(front_kernel, n_blk, n_sub), in_specs=[i...]
    unnamed x30 -> x28, local copies, waits for them, and re-layouts: 8.18 us -> 9.6 us
where the time goes in v2:
time: 46.6 us; the launch traced here: 46.1 us
  Pallas kernels  35.8 us (77%)
  local copies, waits for them, and re-layouts  9.6 us (21%)
  between operations  0.74 us (2%)
    pallas_call x1, Pallas kernels, on_device(): pl.pallas_call(functools.partial(front_kernel, n_blk, n_sub), in_specs=[i...  21.8 us
    unnamed x28, local copies, waits for them, and re-layouts  9.6 us
    pallas_call x1, Pallas kernels, on_device(): pl.pallas_call(combine_kernel, in_specs=[inside] * 9, out_specs=[inside]...  6.59 us
    pallas_call x1, Pallas kernels, on_device(): pl.pallas_call(functools.partial(reduce_kernel, n_sub), in_specs=[inside]...  5.58 us
    pallas_call x1, Pallas kernels, on_device(): pl.pallas_call(correct_kernel, grid=(elems // chunk,), in_specs=[whole((f...  1.81 us

profile of v2, /device:TPU:0, one launch (start us, length us, event | category | flops | bytes accessed | tf_op | source)
XLA Modules:
  0.0 46.1 jit_solution(7570074954875828186)
XLA Ops:
  0.6 0.0 copy-start
  0.6 1.6 %copy-done = f32[2,8,8,8,512]{4,3,2,1,0:T(8,128)S(1)} copy-done((f32[2,8,8,8,512]{4,3,2,1,0:T(8,128)S(1)}, f32[2,8,8,8,512]{4,3,2,1,0:T(8,128)}, u32[]{:S(2)}) %copy-start) | copy-done | bytes 2097176
  2.2 0.0 copy-start.2
  2.2 2.8 %copy-done.2 = f32[6,8,8,8,512]{4,3,2,1,0:T(8,128)S(1)} copy-done((f32[6,8,8,8,512]{4,3,2,1,0:T(8,128)S(1)}, f32[6,8,8,8,512]{4,3,2,1,0:T(8,128)}, u32[]{:S(2)}) %copy-start.2) | copy-done | bytes 6291480
  5.0 0.0 copy-start.4
  5.0 1.1 %copy-done.4 = f32[64,6,512]{2,0,1:T(8,128)S(1)} copy-done((f32[64,6,512]{2,0,1:T(8,128)S(1)}, f32[64,6,512]{2,0,1:T(8,128)}, u32[]{:S(2)}) %copy-start.4) | copy-done | bytes 786456
  6.1 0.0 copy-start.5
  6.1 1.1 %copy-done.5 = f32[64,6,512]{2,0,1:T(8,128)S(1)} copy-done((f32[64,6,512]{2,0,1:T(8,128)S(1)}, f32[64,6,512]{2,0,1:T(8,128)}, u32[]{:S(2)}) %copy-start.5) | copy-done | bytes 786456
  7.3 0.0 copy-start.7
  7.3 0.7 %copy-done.7 = s32[5,512]{1,0:T(8,128)S(1)} copy-done((s32[5,512]{1,0:T(8,128)S(1)}, s32[5,512]{1,0:T(8,128)}, u32[]{:S(2)}) %copy-start.7) | copy-done | bytes 10264
  8.0 0.0 copy-start.8
  8.0 0.7 %copy-done.8 = s32[5,1,576]{2,1,0:T(1,128)S(1)} copy-done((s32[5,1,576]{2,1,0:T(1,128)S(1)}, s32[5,1,576]{2,1,0:T(1,128)}, u32[]{:S(2)}) %copy-start.8) | copy-done | bytes 11544
  8.7 0.0 copy-start.9
  8.7 0.8 %copy-done.9 = bf16[64,192]{1,0:T(8,128)(2,1)S(1)} copy-done((bf16[64,192]{1,0:T(8,128)(2,1)S(1)}, bf16[64,192]{1,0:T(8,128)(2,1)}, u32[]{:S(2)}) %copy-start.9) | copy-done | bytes 24600
  9.5 0.0 copy-start.11
  9.5 0.8 %copy-done.11 = bf16[64,192]{1,0:T(8,128)(2,1)S(1)} copy-done((bf16[64,192]{1,0:T(8,128)(2,1)S(1)}, bf16[64,192]{1,0:T(8,128)(2,1)}, u32[]{:S(2)}) %copy-start.11) | copy-done | bytes 24600
  10.2 0.0 copy-start.3
  10.2 0.0 copy-start.10
  10.2 0.0 copy-start.12
  10.2 0.0 copy-start.13
  10.2 21.8 %front.1 = (f32[4,1024,128]{2,1,0:T(8,128)S(1)}, f32[1600,128]{1,0:T(8,128)S(1)}, f32[1600,128]{1,0:T(8,128)S(1)}) custom-call(s32[5,1,576]{2,1,0:T(1,128)S(1)} %copy-done.8, s32[5,512]{1,0:T(8,128)S(1)} %copy-done.7, f32[1024,512]{1,0:T(8,128)S(1)} %bitcast.9, f32[6,64,512]{2,1,0:T(8,128)S(1)} %bitcast.13, f32[6,64,512]{2,1,0:T(8,128)S(1)} %bitcast.14, ...), custom_call_target="tpu_custom_call" | custom-call | tf_op jit(solution)/shard_map/front/pallas_call | solution.py:627
  32.1 0.0 copy-done.3
  32.1 0.0 copy-done.10
  32.1 0.0 copy-done.12
  32.1 0.0 copy-done.13
  32.1 0.0 copy-start.1
  32.1 0.0 copy-start.6
  32.1 6.6 %combine.1 = (f32[2,8,64,512]{3,2,1,0:T(8,128)}, f32[16,256]{1,0:T(8,128)S(1)}) custom-call(s32[5,1,576]{2,1,0:T(1,128)S(1)} %copy-done.8, s32[5,512]{1,0:T(8,128)S(1)} %copy-done.7, f32[1600,128]{1,0:T(8,128)S(1)} %get-tuple-element.7.vb, f32[1600,128]{1,0:T(8,128)S(1)} %get-tuple-element.8.hb, f32[4,1024,128]{2,1,0:T(8,128)S(1)} %get-tuple-element.9.vol, ...), custom_call_target="tpu_custom_call" | custom-call | tf_op jit(solution)/shard_map/combine/pallas_call | solution.py:662
  38.7 5.6 %reduce.1.total_ref = f32[16,256]{1,0:T(8,128)S(1)} custom-call(f32[16,256]{1,0:T(8,128)S(1)} %get-tuple-element.11.sums_ref), custom_call_target="tpu_custom_call" | custom-call | tf_op jit(solution)/shard_map/reduce/pallas_call | solution.py:690
  44.3 0.0 copy-done.1
  44.3 0.0 copy-done.6
  44.3 1.8 %correct.1 = f32[2,8,64,512]{3,2,1,0:T(8,128)} custom-call(f32[16,256]{1,0:T(8,128)S(1)} %reduce.1.total_ref, f32[8,8,256]{2,1,0:T(8,128)S(1)} %copy-done.6, s32[1,512]{1,0:T(1,128)S(1)} %bitcast.16, f32[16,128]{1,0:T(8,128)S(1)} %copy-done.12, f32[2,8,64,512]{3,2,1,0:T(8,128)S(1)} %bitcast.10), custom_call_target="tpu_custom_call" | custom-call | tf_op jit(solution)/shard_map/correct/pallas_call | solution.py:705
Async XLA Ops:
  0.6 1.6 %copy-start = (f32[2,8,8,8,512]{4,3,2,1,0:T(8,128)S(1)}, f32[2,8,8,8,512]{4,3,2,1,0:T(8,128)}, u32[]{:S(2)}) copy-start(f32[2,8,8,8,512]{4,3,2,1,0:T(8,128)} %param.13) | copy-start | bytes 6291460
  2.2 2.8 %copy-start.2 = (f32[6,8,8,8,512]{4,3,2,1,0:T(8,128)S(1)}, f32[6,8,8,8,512]{4,3,2,1,0:T(8,128)}, u32[]{:S(2)}) copy-start(f32[6,8,8,8,512]{4,3,2,1,0:T(8,128)} %param.15) | copy-start | bytes 18874372
  5.0 1.1 %copy-start.4 = (f32[64,6,512]{2,0,1:T(8,128)S(1)}, f32[64,6,512]{2,0,1:T(8,128)}, u32[]{:S(2)}) copy-start(f32[64,6,512]{2,0,1:T(8,128)} %param.16) | copy-start | bytes 2359300
  6.1 1.1 %copy-start.5 = (f32[64,6,512]{2,0,1:T(8,128)S(1)}, f32[64,6,512]{2,0,1:T(8,128)}, u32[]{:S(2)}) copy-start(f32[64,6,512]{2,0,1:T(8,128)} %param.17) | copy-start | bytes 2359300
  7.3 0.7 %copy-start.7 = (s32[5,512]{1,0:T(8,128)S(1)}, s32[5,512]{1,0:T(8,128)}, u32[]{:S(2)}) copy-start(s32[5,512]{1,0:T(8,128)} %pairs.3) | copy-start | bytes 30724
  8.0 0.7 %copy-start.8 = (s32[5,1,576]{2,1,0:T(1,128)S(1)}, s32[5,1,576]{2,1,0:T(1,128)}, u32[]{:S(2)}) copy-start(s32[5,1,576]{2,1,0:T(1,128)} %slots.3) | copy-start | bytes 34564
  8.7 0.8 %copy-start.9 = (bf16[64,192]{1,0:T(8,128)(2,1)S(1)}, bf16[64,192]{1,0:T(8,128)(2,1)}, u32[]{:S(2)}) copy-start(bf16[64,192]{1,0:T(8,128)(2,1)} %constant.10.clone.bwd) | copy-start | bytes 73732
  9.5 0.8 %copy-start.11 = (bf16[64,192]{1,0:T(8,128)(2,1)S(1)}, bf16[64,192]{1,0:T(8,128)(2,1)}, u32[]{:S(2)}) copy-start(bf16[64,192]{1,0:T(8,128)(2,1)} %constant.9.clone.fwd) | copy-start | bytes 73732
  10.2 21.8 %copy-start.3 = (f32[2,8,8,8,512]{4,3,2,1,0:T(8,128)S(1)}, f32[2,8,8,8,512]{4,3,2,1,0:T(8,128)}, u32[]{:S(2)}) copy-start(f32[2,8,8,8,512]{4,3,2,1,0:T(8,128)} %param.14) | copy-start | bytes 6291460
  10.2 21.8 %copy-start.10 = (bf16[64,192]{1,0:T(8,128)(2,1)S(1)}, bf16[64,192]{1,0:T(8,128)(2,1)}, u32[]{:S(2)}) copy-start(bf16[64,192]{1,0:T(8,128)(2,1)} %constant.11.clone.lift_ref) | copy-start | bytes 73732
  10.2 21.8 %copy-start.12 = (f32[16,128]{1,0:T(8,128)S(1)}, f32[16,128]{1,0:T(8,128)}, u32[]{:S(2)}) copy-start(f32[16,128]{1,0:T(8,128)} %constant.8.clone.modes.modes_ref) | copy-start | bytes 24580
  10.2 21.9 %copy-start.13 = (s32[512]{0:T(512)S(1)}, s32[512]{0:T(512)}, u32[]{:S(2)}) copy-start(s32[512]{0:T(512)} %param.20) | copy-start | bytes 6148
  32.1 12.2 %copy-start.1 = (f32[2,8,8,8,512]{4,3,2,1,0:T(8,128)S(1)}, f32[2,8,8,8,512]{4,3,2,1,0:T(8,128)}, u32[]{:S(2)}) copy-start(f32[2,8,8,8,512]{4,3,2,1,0:T(8,128)} %param.13) | copy-start | bytes 6291460
  32.1 12.2 %copy-start.6 = (f32[8,8,256]{2,1,0:T(8,128)S(1)}, f32[8,8,256]{2,1,0:T(8,128)}, u32[]{:S(2)}) copy-start(f32[8,8,256]{2,1,0:T(8,128)} %inverse_ref.1) | copy-start | bytes 196612

commit v3 on v2

--- a/solution.py
+++ b/solution.py
@@ -117,26 +117,25 @@
 
 
 def pair_flux(own, peer, code):
-    v1, g1, wm1 = own
-    v2, g2, wm2 = peer
+    wm1, v1, g1 = own
+    wm2, v2, g2 = peer
     lane = lax.broadcasted_iota(jnp.int32, code.shape, 1)
+    low = lane < FACE
     node = lane & (FACE - 1)
     swapped = ((node & (NODES - 1)) << 3) | (node >> 3)
     source = jnp.where((code & 4) != 0, swapped, node)
     source = source ^ ((code & 1) * 56) ^ (((code >> 1) & 1) * 7)
-    both = source | (lane & FACE)
-    v2 = lane_pick(v2, both)
-    g2 = lane_pick(g2, both)
-    w2 = lane_pick(wm2, source)
-    m2 = lane_pick(wm2, source + FACE)
-    w1 = lane_pick(wm1, node)
-    m1 = lane_pick(wm1, node + FACE)
+    source = source | (lane & FACE)
     penalty = NODES * (NODES + 1) / 2.0
-    jump = v1 - v2
-    weight = 0.5 * (w1 + w2)
-    tau = (penalty * 0.5) * (m1 + m2)
-    value = weight * (tau * jump - 0.5 * (g1 - g2))
-    lift = (-0.5 * weight * jump) * m1
+    jump = v1 - lane_pick(v2, source)
+    gap = g1 - lane_pick(g2, source)
+    total = wm1 + lane_pick(wm2, source)
+    turned = pltpu.roll(total, FACE, 1)
+    weight = 0.5 * jnp.where(low, total, turned)
+    tau = (penalty * 0.5) * jnp.where(low, turned, total)
+    metric = jnp.where(low, pltpu.roll(wm1, FACE, 1), wm1)
+    value = weight * (tau * jump - 0.5 * gap)
+    lift = (-0.5 * weight * jump) * metric
     return value, lift
 
 
@@ -170,36 +169,60 @@
     return pl.ds(pl.multiple_of(start, size), size)
 
 
-def trace_tile(t, elems, p_s, fw_s, fm_s, tables):
-    fields = p_s.shape[1] // BRICK
+def node_layers(t, axis, start, p_s):
+    layers = []
+    for k in range(NODES):
+        if axis == 0:
+            layers.append(p_s[t, start + k * FACE : start + (k + 1) * FACE, :])
+        elif axis == 1:
+            rows = [
+                p_s[t, start + i * FACE + k * NODES : start + i * FACE + (k + 1) * NODES, :]
+                for i in range(NODES)
+            ]
+            layers.append(jnp.concatenate(rows, axis=0))
+        else:
+            layers.append(p_s[t, pl.ds(start + k, FACE, stride=NODES), :])
+    return layers
+
+
+def face_rows(face, t, elems):
+    return aligned(face * elems + t * LANES, LANES)
+
+
+def fixed_tile(t, elems, fw_s, fm_s, table):
+    for face in range(6):
+        both = jnp.concatenate([fw_s[t, face], fm_s[t, face]], axis=0)
+        table[face_rows(face, t, elems), :] = both.T
+
+
+def value_tile(t, elems, p_s, table):
     for axis in range(3):
-        values = []
-        slopes = []
-        for field in range(fields):
-            start = field * BRICK
-            layers = []
-            for k in range(NODES):
+        for side in range(2):
+            ends = []
+            for start in range(0, p_s.shape[1], BRICK):
+                k = side * (NODES - 1)
                 if axis == 0:
-                    layers.append(p_s[t, start + k * FACE : start + (k + 1) * FACE, :])
+                    ends.append(p_s[t, start + k * FACE : start + (k + 1) * FACE, :])
                 elif axis == 1:
-                    rows = [
+                    ends += [
                         p_s[t, start + i * FACE + k * NODES : start + i * FACE + (k + 1) * NODES, :]
                         for i in range(NODES)
                     ]
-                    layers.append(jnp.concatenate(rows, axis=0))
                 else:
-                    layers.append(p_s[t, pl.ds(start + k, FACE, stride=NODES), :])
-            values.append((layers[0], layers[-1]))
+                    ends.append(p_s[t, pl.ds(start + k, FACE, stride=NODES), :])
+            table[face_rows(2 * axis + side, t, elems), :] = jnp.concatenate(ends, axis=0).T
+
+
+def slope_tile(t, elems, p_s, fm_s, table):
+    for axis in range(3):
+        slopes = []
+        for start in range(0, p_s.shape[1], BRICK):
+            layers = node_layers(t, axis, start, p_s)
             slopes.append((weighted(-DERIV[0], layers), weighted(DERIV[-1], layers)))
         for side in range(2):
             face = 2 * axis + side
-            metric = fm_s[t, face]
-            rows = aligned(face * elems + t * LANES, LANES)
-            value = jnp.concatenate([entry[side] for entry in values], axis=0)
-            slope = jnp.concatenate([entry[side] * metric for entry in slopes], axis=0)
-            tables[0][rows, :] = value.T
-            tables[1][rows, :] = slope.T
-            tables[2][rows, :] = jnp.concatenate([fw_s[t, face], metric], axis=0).T
+            slope = jnp.concatenate([entry[side] * fm_s[t, face] for entry in slopes], axis=0)
+            table[face_rows(face, t, elems), :] = slope.T
 
 
 def volume_half(h, p_s, g_s, fwd, bwd, out, s_ref):
@@ -257,18 +280,18 @@
 
 def front_kernel(
     n_blk, n_sub,
-    slots, pairs, p_hbm, fw_hbm, fm_hbm, g_hbm, fwd, bwd,
+    slots_hbm, pairs_hbm, p_hbm, fw_hbm, fm_hbm, g_hbm, fwd_hbm, bwd_hbm,
     vol, vb, hb,
-    p_s, fw_s, fm_s, g_s, s_ref, tv, tg, tw, la, lb, lc, cb, pad, send, recv,
+    slots, pairs, fwd, bwd, p_s, fw_s, fm_s, g_s, s_ref, tv, tg, tw, la, lb, lc, cb, pad, send, recv,
     st0, st1, st2, rw0, rw1, rw2,
-    load_sem, geo_sem, row_sem, send_sem, recv_sem,
+    small_sem, load_sem, geo_sem, row_sem, send_sem, recv_sem,
 ):
     elems = tv.shape[0] // 6
     tiles = elems // LANES
     slot_total = slots.shape[2]
     pair_total = pairs.shape[1]
     width = slot_total // 9
-    tables = (tv, tg, tw)
+    tables = (tw, tv, tg)
     locals_ = (la, lb, lc)
     place = lax.axis_index("blk")
     sub = lax.axis_index("sub")
@@ -279,62 +302,86 @@
             lax.rem(sub + (k % 3 - 1) + n_sub, n_sub),
         )
 
-    others = [0, 2, 6, 8, 1, 7, 3, 5]
+    others = [2, 0, 8, 6, 5, 3, 1, 7]
+    small = [
+        pltpu.make_async_copy(source, target, small_sem.at[n])
+        for n, (source, target) in enumerate(
+            ((slots_hbm, slots), (pairs_hbm, pairs), (fwd_hbm, fwd), (bwd_hbm, bwd))
+        )
+    ]
+    for copy in small[:2]:
+        copy.start()
     loads = []
     for t in range(tiles):
         cols = pl.ds(t * LANES, LANES)
         loads.append(
             [
-                pltpu.make_async_copy(p_hbm.at[:, cols], p_s.at[t], load_sem.at[t, 0]),
-                pltpu.make_async_copy(fw_hbm.at[:, :, cols], fw_s.at[t], load_sem.at[t, 1]),
-                pltpu.make_async_copy(fm_hbm.at[:, :, cols], fm_s.at[t], load_sem.at[t, 2]),
+                pltpu.make_async_copy(fw_hbm.at[:, :, cols], fw_s.at[t], load_sem.at[t, 0]),
+                pltpu.make_async_copy(fm_hbm.at[:, :, cols], fm_s.at[t], load_sem.at[t, 1]),
+                pltpu.make_async_copy(p_hbm.at[:, cols], p_s.at[t], load_sem.at[t, 2]),
             ]
         )
-        for copy in loads[-1]:
-            copy.start()
+    for t in range(tiles):
+        loads[t][0].start()
+        loads[t][1].start()
+    for t in range(tiles):
+        loads[t][2].start()
+    barrier = pltpu.get_barrier_semaphore()
+    for k in others:
+        pl.semaphore_signal(barrier, inc=1, device_id=peer(k), device_id_type=MESH)
+    for copy in small[:2]:
+        copy.wait()
+    numbers = row_numbers(slots, pairs, elems, (st0, st1, st2), (rw0, rw1, rw2), row_sem)
+    for copy in numbers:
+        copy.start()
+    for t in range(tiles):
+        loads[t][0].wait()
+        loads[t][1].wait()
+        fixed_tile(t, elems, fw_s, fm_s, tw)
+    for t in range(tiles):
+        loads[t][2].wait()
+        value_tile(t, elems, p_s, tv)
+    for copy in numbers:
+        copy.wait()
+    pl.semaphore_wait(barrier, len(others))
+    copies = []
+    for part, chosen in enumerate(((0, 1), (2,))):
+        if part == 1:
+            for t in range(tiles):
+                slope_tile(t, elems, p_s, fm_s, tg)
+        for k in others:
+
+            def gather(n, carry, k=k, chosen=chosen):
+                base = n * 16
+                rows = [rw0[0, k * width + base + u] for u in range(16)]
+                for j in chosen:
+                    found = [tables[j][pl.ds(row, 1), :] for row in rows]
+                    for u in range(16):
+                        send[k, j, pl.ds(base + u, 1), :] = found[u]
+                return carry
+
+            lax.fori_loop(0, width // 16, gather, 0)
+            piece = pl.ds(chosen[0], len(chosen))
+            copies.append(
+                pltpu.make_async_remote_copy(
+                    src_ref=send.at[k, piece],
+                    dst_ref=recv.at[8 - k, piece],
+                    send_sem=send_sem.at[k, part],
+                    recv_sem=recv_sem.at[8 - k, part],
+                    device_id=peer(k),
+                    device_id_type=MESH,
+                )
+            )
+            copies[-1].start()
+
     geo = []
     for t in range(tiles):
         cols = pl.ds(t * LANES, LANES)
         geo.append(pltpu.make_async_copy(g_hbm.at[:, cols], g_s.at[t], geo_sem.at[t]))
         geo[-1].start()
-    barrier = pltpu.get_barrier_semaphore()
-    for k in others:
-        pl.semaphore_signal(barrier, inc=1, device_id=peer(k), device_id_type=MESH)
-    numbers = row_numbers(slots, pairs, elems, (st0, st1, st2), (rw0, rw1, rw2), row_sem)
-    for copy in numbers:
+    for copy in small[2:]:
         copy.start()
     code_rows(slots, pairs, pad, cb)
-    for t in range(tiles):
-        for copy in loads[t]:
-            copy.wait()
-        trace_tile(t, elems, p_s, fw_s, fm_s, tables)
-    for copy in numbers:
-        copy.wait()
-    pl.semaphore_wait(barrier, len(others))
-    copies = []
-    for k in others:
-
-        def gather(n, carry, k=k):
-            base = n * 16
-            rows = [rw0[0, k * width + base + u] for u in range(16)]
-            for j in range(3):
-                found = [tables[j][pl.ds(row, 1), :] for row in rows]
-                for u in range(16):
-                    send[k, j, pl.ds(base + u, 1), :] = found[u]
-            return carry
-
-        lax.fori_loop(0, width // 16, gather, 0)
-        copies.append(
-            pltpu.make_async_remote_copy(
-                src_ref=send.at[k],
-                dst_ref=recv.at[8 - k],
-                send_sem=send_sem.at[k],
-                recv_sem=recv_sem.at[8 - k],
-                device_id=peer(k),
-                device_id_type=MESH,
-            )
-        )
-        copies[-1].start()
 
     for side, numbers in enumerate((rw1, rw2)):
 
@@ -350,10 +397,9 @@
         lax.fori_loop(0, pair_total // 16, gather_local, 0)
 
     def local_flux(n, carry):
-        own = aligned(n * LANES, LANES)
-        other = aligned((n * LANES + pair_total) % (2 * pair_total), LANES)
-        rows = aligned(n * LANES + slot_total, FACE)
-        rows = pl.ds(rows.start, LANES)
+        own = aligned(n * group, group)
+        other = aligned((n * group + pair_total) % (2 * pair_total), group)
+        rows = pl.ds(pl.multiple_of(n * group + slot_total, FACE), group)
         value, lift = pair_flux(
             [table[own, :] for table in locals_], [table[other, :] for table in locals_], cb[rows, :]
         )
@@ -361,8 +407,9 @@
         hb[rows, :] = lift
         return carry
 
-    lax.fori_loop(0, 2 * pair_total // LANES, local_flux, 0)
-    for copy in geo:
+    group = 2 * LANES
+    lax.fori_loop(0, 2 * pair_total // group, local_flux, 0)
+    for copy in geo + small[2:]:
         copy.wait()
 
     def volume(h, carry):
@@ -374,8 +421,8 @@
         copy.wait()
 
     def cross_flux(n, carry):
-        for shift in (0, 5):
-            k = n + shift
+        for shift in (0, 1, 5, 6):
+            k = 2 * n + shift
             rows = aligned(k * width, FACE)
             codes = cb[rows, :]
             value, lift = pair_flux(
@@ -386,15 +433,15 @@
             hb[rows, :] = jnp.where(live, lift, 0.0)
         return carry
 
-    lax.fori_loop(0, 4, cross_flux, 0)
+    lax.fori_loop(0, 2, cross_flux, 0)
     vb[4 * width : 5 * width, :] = jnp.zeros((width, LANES), jnp.float32)
     hb[4 * width : 5 * width, :] = jnp.zeros((width, LANES), jnp.float32)
 
 
 def combine_kernel(
-    slots, pairs, vb, hb, vol, rhs, lift_ref, modes, cells,
-    res, sums,
-    vt, lt, fv, fl, cs, st0, st1, st2, rw0, rw1, rw2, row_sem,
+    slots, pairs, vb, hb, vol, rhs, lift_ref, modes,
+    res, cs,
+    vt, lt, fv, fl, st0, st1, st2, rw0, rw1, rw2, row_sem,
 ):
     elems = vt.shape[0] // 6
     tiles = elems // LANES
@@ -484,10 +531,18 @@
 
     lax.fori_loop(0, fields * tiles // 2, finish, 0)
 
-    row_cells = sums.shape[1]
-    hot = lax.broadcasted_iota(jnp.int32, (row_cells, elems), 0) == cells[...]
+
+def reduce_kernel(n_sub, coarse_ref, cells, total_ref, sums_ref, box, send_sem, recv_sem):
+    place = lax.axis_index("blk")
+    sub = lax.axis_index("sub")
+    barrier = pltpu.get_barrier_semaphore()
+    peers = [(place, lax.rem(sub + step, n_sub)) for step in range(1, n_sub)]
+    for peer in peers:
+        pl.semaphore_signal(barrier, inc=1, device_id=peer, device_id_type=MESH)
+    row_cells = sums_ref.shape[1]
+    coarse = coarse_ref[...]
+    hot = lax.broadcasted_iota(jnp.int32, (row_cells, coarse.shape[1]), 0) == cells[...]
     hot = hot.astype(jnp.float32).astype(jnp.bfloat16)
-    coarse = cs[...]
     high = coarse.astype(jnp.bfloat16)
     low = (coarse - high.astype(jnp.float32)).astype(jnp.bfloat16)
     both = lax.dot_general(
@@ -496,16 +551,7 @@
         (((1,), (1,)), ((), ())),
         preferred_element_type=jnp.float32,
     )
-    sums[...] = both[: coarse.shape[0]] + both[coarse.shape[0] :]
-
-
-def reduce_kernel(n_sub, sums_ref, total_ref, box, send_sem, recv_sem):
-    place = lax.axis_index("blk")
-    sub = lax.axis_index("sub")
-    barrier = pltpu.get_barrier_semaphore()
-    peers = [(place, lax.rem(sub + step, n_sub)) for step in range(1, n_sub)]
-    for peer in peers:
-        pl.semaphore_signal(barrier, inc=1, device_id=peer, device_id_type=MESH)
+    sums_ref[...] = both[: coarse.shape[0]] + both[coarse.shape[0] :]
     pl.semaphore_wait(barrier, n_sub - 1)
     copies = []
     for step, peer in enumerate(peers):
@@ -626,10 +672,14 @@
 
     volume, values, lifts = pl.pallas_call(
         functools.partial(front_kernel, n_blk, n_sub),
-        in_specs=[inside] * 2 + [outside] * 4 + [inside] * 2,
+        in_specs=[outside] * 8,
         out_specs=[inside] * 3,
         out_shape=[shaped(tiles, rows, LANES), shaped(side_total, LANES), shaped(side_total, LANES)],
         scratch_shapes=[
+            pltpu.VMEM(cross_slots.shape, i32),
+            pltpu.VMEM(local_pairs.shape, i32),
+            pltpu.VMEM((FACE, 3 * FACE), jnp.bfloat16),
+            pltpu.VMEM((FACE, 3 * FACE), jnp.bfloat16),
             pltpu.VMEM((tiles, rows, LANES), f32),
             pltpu.VMEM((tiles, 6, FACE, LANES), f32),
             pltpu.VMEM((tiles, 6, FACE, LANES), f32),
@@ -645,31 +695,35 @@
             pltpu.VMEM((9, 3, width, LANES), f32),
         ]
         + number_scratch
-        + [dma((tiles, 3)), dma((tiles,)), dma((3,)), dma((9,)), dma((9,))],
+        + [dma((4,)), dma((tiles, 3)), dma((tiles,)), dma((3,)), dma((9, 2)), dma((9, 2))],
         compiler_params=limits(36, collective_id=0, has_side_effects=True),
         name="front",
     )(
-        cross_slots,
-        local_pairs,
-        pressure.reshape(rows, elems),
-        weights,
-        metrics,
-        geometry.reshape(6 * BRICK, elems),
-        jnp.asarray(forward_table()),
-        jnp.asarray(backward_table()),
+        *[
+            pltpu.with_memory_space_constraint(value, pltpu.MemorySpace.HBM)
+            for value in (
+                cross_slots,
+                local_pairs,
+                pressure.reshape(rows, elems),
+                weights,
+                metrics,
+                geometry.reshape(6 * BRICK, elems),
+                jnp.asarray(forward_table()),
+                jnp.asarray(backward_table()),
+            )
+        ]
     )
 
-    residual, sums = pl.pallas_call(
+    residual, coarse = pl.pallas_call(
         combine_kernel,
-        in_specs=[inside] * 9,
+        in_specs=[inside] * 8,
         out_specs=[inside] * 2,
-        out_shape=[shaped(*slabs), shaped(fields * NODES, row_cells)],
+        out_shape=[shaped(*slabs), shaped(fields * NODES, elems)],
         scratch_shapes=[
             pltpu.VMEM((6 * elems, LANES), f32),
             pltpu.VMEM((6 * elems, LANES), f32),
             pltpu.VMEM((tiles, fields, 6, FACE, LANES), f32),
             pltpu.VMEM((tiles, fields, 6, FACE, LANES), f32),
-            pltpu.VMEM((fields * NODES, elems), f32),
         ]
         + number_scratch
         + [dma((3,))],
@@ -684,22 +738,22 @@
         right_side.reshape(slabs),
         jnp.asarray(lift_table()),
         modes,
-        cells,
     )
 
     totals = pl.pallas_call(
         functools.partial(reduce_kernel, n_sub),
-        in_specs=[inside],
+        in_specs=[inside] * 2,
         out_specs=inside,
         out_shape=shaped(fields * NODES, row_cells),
         scratch_shapes=[
+            pltpu.VMEM((fields * NODES, row_cells), f32),
             pltpu.VMEM((n_sub - 1, fields * NODES, row_cells), f32),
             dma((n_sub - 1,)),
             dma((n_sub - 1,)),
         ],
         compiler_params=limits(8, collective_id=1, has_side_effects=True),
         name="reduce",
-    )(sums)
+    )(coarse, cells)
 
     chunk = min(elems, 256)
     corrected = pl.pallas_call(

time: 46.6 us -> 37 us (0.79)
  local copies, waits for them, and re-layouts: 9.6 us -> 0.05 us
    unnamed x28 -> x16, local copies, waits for them, and re-layouts: 9.6 us -> 0.05 us
where the time goes in v3:
time: 37 us; the launch traced here: 36.9 us
  Pallas kernels  36.1 us (98%)
  between operations  0.78 us (2%)
    pallas_call x1, Pallas kernels, on_device(): pl.pallas_call(functools.partial(front_kernel, n_blk, n_sub), in_specs=[o...  22.1 us
    pallas_call x1, Pallas kernels, on_device(): pl.pallas_call(combine_kernel, in_specs=[inside] * 8, out_specs=[inside]...  6.62 us
    pallas_call x1, Pallas kernels, on_device(): pl.pallas_call(functools.partial(reduce_kernel, n_sub), in_specs=[inside]...  5.58 us
    pallas_call x1, Pallas kernels, on_device(): pl.pallas_call(correct_kernel, grid=(elems // chunk,), in_specs=[whole((f...  1.81 us

profile of v3, /device:TPU:0, one launch (start us, length us, event | category | flops | bytes accessed | tf_op | source)
XLA Modules:
  0.0 36.9 jit_solution(17157314949654731584)
XLA Ops:
  0.6 0.0 copy-start.1
  0.6 0.0 copy-start.3
  0.7 0.0 copy-start.4
  0.7 0.0 copy-start.5
  0.7 0.0 copy-start.6
  0.7 22.1 %front.1 = (f32[4,1024,128]{2,1,0:T(8,128)S(1)}, f32[1600,128]{1,0:T(8,128)S(1)}, f32[1600,128]{1,0:T(8,128)S(1)}) custom-call(s32[5,1,576]{2,1,0:T(1,128)} %slots.1, s32[5,512]{1,0:T(8,128)} %pairs.1, f32[1024,512]{1,0:T(8,128)} %bitcast.9, f32[6,64,512]{2,1,0:T(8,128)} %bitcast.16, f32[6,64,512]{2,1,0:T(8,128)} %bitcast.17, f32[3072,512]{1,0:T(8,128)} %bitcast.14, ...), custom_call_target="tpu_custom_call" | custom-call | tf_op jit(solution)/shard_map/front/pallas_call | solution.py:673
  22.8 0.0 copy-done.1
  22.8 0.0 copy-done.3
  22.8 0.0 copy-done.4
  22.8 0.0 copy-done.5
  22.8 0.0 copy-done.6
  22.8 0.0 copy-start.7
  22.8 0.0 copy-start
  22.8 0.0 copy-start.2
  22.9 6.6 %combine.1 = (f32[2,8,64,512]{3,2,1,0:T(8,128)}, f32[16,512]{1,0:T(8,128)S(1)}) custom-call(s32[5,1,576]{2,1,0:T(1,128)S(1)} %copy-done.4, s32[5,512]{1,0:T(8,128)S(1)} %copy-done.3, f32[1600,128]{1,0:T(8,128)S(1)} %get-tuple-element.7.vb, f32[1600,128]{1,0:T(8,128)S(1)} %get-tuple-element.8.hb, f32[4,1024,128]{2,1,0:T(8,128)S(1)} %get-tuple-element.9.vol, ...), custom_call_target="tpu_custom_call" | custom-call | tf_op jit(solution)/shard_map/combine/pallas_call | solution.py:717
  29.5 0.0 copy-done.7
  29.5 5.6 %reduce.1.total_ref = f32[16,256]{1,0:T(8,128)S(1)} custom-call(f32[16,512]{1,0:T(8,128)S(1)} %get-tuple-element.11.coarse_ref, s32[1,512]{1,0:T(1,128)S(1)} %bitcast.12), custom_call_target="tpu_custom_call" | custom-call | tf_op jit(solution)/shard_map/reduce/pallas_call | solution.py:743
  35.1 0.0 copy-done
  35.1 0.0 copy-done.2
  35.1 1.8 %correct.1 = f32[2,8,64,512]{3,2,1,0:T(8,128)} custom-call(f32[16,256]{1,0:T(8,128)S(1)} %reduce.1.total_ref, f32[8,8,256]{2,1,0:T(8,128)S(1)} %copy-done.2, s32[1,512]{1,0:T(1,128)S(1)} %bitcast.13, f32[16,128]{1,0:T(8,128)S(1)} %copy-done.6, f32[2,8,64,512]{3,2,1,0:T(8,128)S(1)} %bitcast.10), custom_call_target="tpu_custom_call" | custom-call | tf_op jit(solution)/shard_map/correct/pallas_call | solution.py:759
Async XLA Ops:
  0.6 22.1 %copy-start.1 = (f32[2,8,8,8,512]{4,3,2,1,0:T(8,128)S(1)}, f32[2,8,8,8,512]{4,3,2,1,0:T(8,128)}, u32[]{:S(2)}) copy-start(f32[2,8,8,8,512]{4,3,2,1,0:T(8,128)} %param.14) | copy-start | bytes 6291460
  0.6 22.1 %copy-start.3 = (s32[5,512]{1,0:T(8,128)S(1)}, s32[5,512]{1,0:T(8,128)}, u32[]{:S(2)}) copy-start(s32[5,512]{1,0:T(8,128)} %pairs.1) | copy-start | bytes 30724
  0.7 22.1 %copy-start.4 = (s32[5,1,576]{2,1,0:T(1,128)S(1)}, s32[5,1,576]{2,1,0:T(1,128)}, u32[]{:S(2)}) copy-start(s32[5,1,576]{2,1,0:T(1,128)} %slots.1) | copy-start | bytes 34564
  0.7 22.1 %copy-start.5 = (bf16[64,192]{1,0:T(8,128)(2,1)S(1)}, bf16[64,192]{1,0:T(8,128)(2,1)}, u32[]{:S(2)}) copy-start(bf16[64,192]{1,0:T(8,128)(2,1)} %constant.11.clone.lift_ref) | copy-start | bytes 73732
  0.7 22.1 %copy-start.6 = (f32[16,128]{1,0:T(8,128)S(1)}, f32[16,128]{1,0:T(8,128)}, u32[]{:S(2)}) copy-start(f32[16,128]{1,0:T(8,128)} %constant.8.clone.modes.modes_ref) | copy-start | bytes 24580
  22.8 6.7 %copy-start.7 = (s32[512]{0:T(512)S(1)}, s32[512]{0:T(512)}, u32[]{:S(2)}) copy-start(s32[512]{0:T(512)} %param.20) | copy-start | bytes 6148
  22.8 12.2 %copy-start = (f32[2,8,8,8,512]{4,3,2,1,0:T(8,128)S(1)}, f32[2,8,8,8,512]{4,3,2,1,0:T(8,128)}, u32[]{:S(2)}) copy-start(f32[2,8,8,8,512]{4,3,2,1,0:T(8,128)} %param.13) | copy-start | bytes 6291460
  22.8 12.2 %copy-start.2 = (f32[8,8,256]{2,1,0:T(8,128)S(1)}, f32[8,8,256]{2,1,0:T(8,128)}, u32[]{:S(2)}) copy-start(f32[8,8,256]{2,1,0:T(8,128)} %inverse_ref.1) | copy-start | bytes 196612

commit v4 on v3

--- a/solution.py
+++ b/solution.py
@@ -303,6 +303,9 @@
         )
 
     others = [2, 0, 8, 6, 5, 3, 1, 7]
+    barrier = pltpu.get_barrier_semaphore()
+    for k in others:
+        pl.semaphore_signal(barrier, inc=1, device_id=peer(k), device_id_type=MESH)
     small = [
         pltpu.make_async_copy(source, target, small_sem.at[n])
         for n, (source, target) in enumerate(
@@ -326,9 +329,6 @@
         loads[t][1].start()
     for t in range(tiles):
         loads[t][2].start()
-    barrier = pltpu.get_barrier_semaphore()
-    for k in others:
-        pl.semaphore_signal(barrier, inc=1, device_id=peer(k), device_id_type=MESH)
     for copy in small[:2]:
         copy.wait()
     numbers = row_numbers(slots, pairs, elems, (st0, st1, st2), (rw0, rw1, rw2), row_sem)
@@ -341,39 +341,7 @@
     for t in range(tiles):
         loads[t][2].wait()
         value_tile(t, elems, p_s, tv)
-    for copy in numbers:
-        copy.wait()
-    pl.semaphore_wait(barrier, len(others))
-    copies = []
-    for part, chosen in enumerate(((0, 1), (2,))):
-        if part == 1:
-            for t in range(tiles):
-                slope_tile(t, elems, p_s, fm_s, tg)
-        for k in others:
-
-            def gather(n, carry, k=k, chosen=chosen):
-                base = n * 16
-                rows = [rw0[0, k * width + base + u] for u in range(16)]
-                for j in chosen:
-                    found = [tables[j][pl.ds(row, 1), :] for row in rows]
-                    for u in range(16):
-                        send[k, j, pl.ds(base + u, 1), :] = found[u]
-                return carry
-
-            lax.fori_loop(0, width // 16, gather, 0)
-            piece = pl.ds(chosen[0], len(chosen))
-            copies.append(
-                pltpu.make_async_remote_copy(
-                    src_ref=send.at[k, piece],
-                    dst_ref=recv.at[8 - k, piece],
-                    send_sem=send_sem.at[k, part],
-                    recv_sem=recv_sem.at[8 - k, part],
-                    device_id=peer(k),
-                    device_id_type=MESH,
-                )
-            )
-            copies[-1].start()
-
+        slope_tile(t, elems, p_s, fm_s, tg)
     geo = []
     for t in range(tiles):
         cols = pl.ds(t * LANES, LANES)
@@ -381,6 +349,20 @@
         geo[-1].start()
     for copy in small[2:]:
         copy.start()
+    for copy in numbers:
+        copy.wait()
+    for k in others:
+
+        def gather(n, carry, k=k):
+            base = n * 16
+            rows = [rw0[0, k * width + base + u] for u in range(16)]
+            for j in range(3):
+                found = [tables[j][pl.ds(row, 1), :] for row in rows]
+                for u in range(16):
+                    send[k, j, pl.ds(base + u, 1), :] = found[u]
+            return carry
+
+        lax.fori_loop(0, width // 16, gather, 0)
     code_rows(slots, pairs, pad, cb)
 
     for side, numbers in enumerate((rw1, rw2)):
@@ -395,6 +377,21 @@
             return carry
 
         lax.fori_loop(0, pair_total // 16, gather_local, 0)
+
+    pl.semaphore_wait(barrier, len(others))
+    copies = []
+    for k in others:
+        copies.append(
+            pltpu.make_async_remote_copy(
+                src_ref=send.at[k],
+                dst_ref=recv.at[8 - k],
+                send_sem=send_sem.at[k],
+                recv_sem=recv_sem.at[8 - k],
+                device_id=peer(k),
+                device_id_type=MESH,
+            )
+        )
+        copies[-1].start()
 
     def local_flux(n, carry):
         own = aligned(n * group, group)
@@ -695,7 +692,7 @@
             pltpu.VMEM((9, 3, width, LANES), f32),
         ]
         + number_scratch
-        + [dma((4,)), dma((tiles, 3)), dma((tiles,)), dma((3,)), dma((9, 2)), dma((9, 2))],
+        + [dma((4,)), dma((tiles, 3)), dma((tiles,)), dma((3,)), dma((9,)), dma((9,))],
         compiler_params=limits(36, collective_id=0, has_side_effects=True),
         name="front",
     )(

time: 37 us -> 36.9 us (level)
  no operation moved by 1% of the time
where the time goes in v4:
time: 36.9 us; the launch traced here: 36.8 us
  Pallas kernels  36 us (98%)
  between operations  0.78 us (2%)
    pallas_call x1, Pallas kernels, on_device(): pl.pallas_call(functools.partial(front_kernel, n_blk, n_sub), in_specs=[o...  22 us
    pallas_call x1, Pallas kernels, on_device(): pl.pallas_call(combine_kernel, in_specs=[inside] * 8, out_specs=[inside]...  6.62 us
    pallas_call x1, Pallas kernels, on_device(): pl.pallas_call(functools.partial(reduce_kernel, n_sub), in_specs=[inside]...  5.58 us
    pallas_call x1, Pallas kernels, on_device(): pl.pallas_call(correct_kernel, grid=(elems // chunk,), in_specs=[whole((f...  1.81 us

profile of v4, /device:TPU:0, one launch (start us, length us, event | category | flops | bytes accessed | tf_op | source)
XLA Modules:
  0.0 36.8 jit_solution(7798435123993750756)
XLA Ops:
  0.6 0.0 copy-start.1
  0.6 0.0 copy-start.3
  0.7 0.0 copy-start.4
  0.7 0.0 copy-start.5
  0.7 0.0 copy-start.6
  0.7 22.0 %front.1 = (f32[4,1024,128]{2,1,0:T(8,128)S(1)}, f32[1600,128]{1,0:T(8,128)S(1)}, f32[1600,128]{1,0:T(8,128)S(1)}) custom-call(s32[5,1,576]{2,1,0:T(1,128)} %slots.1, s32[5,512]{1,0:T(8,128)} %pairs.1, f32[1024,512]{1,0:T(8,128)} %bitcast.9, f32[6,64,512]{2,1,0:T(8,128)} %bitcast.16, f32[6,64,512]{2,1,0:T(8,128)} %bitcast.17, f32[3072,512]{1,0:T(8,128)} %bitcast.14, ...), custom_call_target="tpu_custom_call" | custom-call | tf_op jit(solution)/shard_map/front/pallas_call | solution.py:670
  22.7 0.0 copy-done.1
  22.7 0.0 copy-done.3
  22.7 0.0 copy-done.4
  22.7 0.0 copy-done.5
  22.7 0.0 copy-done.6
  22.7 0.0 copy-start.7
  22.7 0.0 copy-start
  22.7 0.0 copy-start.2
  22.8 6.6 %combine.1 = (f32[2,8,64,512]{3,2,1,0:T(8,128)}, f32[16,512]{1,0:T(8,128)S(1)}) custom-call(s32[5,1,576]{2,1,0:T(1,128)S(1)} %copy-done.4, s32[5,512]{1,0:T(8,128)S(1)} %copy-done.3, f32[1600,128]{1,0:T(8,128)S(1)} %get-tuple-element.7.vb, f32[1600,128]{1,0:T(8,128)S(1)} %get-tuple-element.8.hb, f32[4,1024,128]{2,1,0:T(8,128)S(1)} %get-tuple-element.9.vol, ...), custom_call_target="tpu_custom_call" | custom-call | tf_op jit(solution)/shard_map/combine/pallas_call | solution.py:714
  29.4 0.0 copy-done.7
  29.4 5.6 %reduce.1.total_ref = f32[16,256]{1,0:T(8,128)S(1)} custom-call(f32[16,512]{1,0:T(8,128)S(1)} %get-tuple-element.11.coarse_ref, s32[1,512]{1,0:T(1,128)S(1)} %bitcast.12), custom_call_target="tpu_custom_call" | custom-call | tf_op jit(solution)/shard_map/reduce/pallas_call | solution.py:740
  35.0 0.0 copy-done
  35.0 0.0 copy-done.2
  35.0 1.8 %correct.1 = f32[2,8,64,512]{3,2,1,0:T(8,128)} custom-call(f32[16,256]{1,0:T(8,128)S(1)} %reduce.1.total_ref, f32[8,8,256]{2,1,0:T(8,128)S(1)} %copy-done.2, s32[1,512]{1,0:T(1,128)S(1)} %bitcast.13, f32[16,128]{1,0:T(8,128)S(1)} %copy-done.6, f32[2,8,64,512]{3,2,1,0:T(8,128)S(1)} %bitcast.10), custom_call_target="tpu_custom_call" | custom-call | tf_op jit(solution)/shard_map/correct/pallas_call | solution.py:756
Async XLA Ops:
  0.6 22.0 %copy-start.1 = (f32[2,8,8,8,512]{4,3,2,1,0:T(8,128)S(1)}, f32[2,8,8,8,512]{4,3,2,1,0:T(8,128)}, u32[]{:S(2)}) copy-start(f32[2,8,8,8,512]{4,3,2,1,0:T(8,128)} %param.14) | copy-start | bytes 6291460
  0.6 22.0 %copy-start.3 = (s32[5,512]{1,0:T(8,128)S(1)}, s32[5,512]{1,0:T(8,128)}, u32[]{:S(2)}) copy-start(s32[5,512]{1,0:T(8,128)} %pairs.1) | copy-start | bytes 30724
  0.7 22.0 %copy-start.4 = (s32[5,1,576]{2,1,0:T(1,128)S(1)}, s32[5,1,576]{2,1,0:T(1,128)}, u32[]{:S(2)}) copy-start(s32[5,1,576]{2,1,0:T(1,128)} %slots.1) | copy-start | bytes 34564
  0.7 22.0 %copy-start.5 = (bf16[64,192]{1,0:T(8,128)(2,1)S(1)}, bf16[64,192]{1,0:T(8,128)(2,1)}, u32[]{:S(2)}) copy-start(bf16[64,192]{1,0:T(8,128)(2,1)} %constant.11.clone.lift_ref) | copy-start | bytes 73732
  0.7 22.0 %copy-start.6 = (f32[16,128]{1,0:T(8,128)S(1)}, f32[16,128]{1,0:T(8,128)}, u32[]{:S(2)}) copy-start(f32[16,128]{1,0:T(8,128)} %constant.8.clone.modes.modes_ref) | copy-start | bytes 24580
  22.7 6.7 %copy-start.7 = (s32[512]{0:T(512)S(1)}, s32[512]{0:T(512)}, u32[]{:S(2)}) copy-start(s32[512]{0:T(512)} %param.20) | copy-start | bytes 6148
  22.7 12.2 %copy-start = (f32[2,8,8,8,512]{4,3,2,1,0:T(8,128)S(1)}, f32[2,8,8,8,512]{4,3,2,1,0:T(8,128)}, u32[]{:S(2)}) copy-start(f32[2,8,8,8,512]{4,3,2,1,0:T(8,128)} %param.13) | copy-start | bytes 6291460
  22.7 12.2 %copy-start.2 = (f32[8,8,256]{2,1,0:T(8,128)S(1)}, f32[8,8,256]{2,1,0:T(8,128)}, u32[]{:S(2)}) copy-start(f32[8,8,256]{2,1,0:T(8,128)} %inverse_ref.1) | copy-start | bytes 196612

commit v5 on v4

--- a/solution.py
+++ b/solution.py
@@ -107,25 +107,38 @@
     return total
 
 
-def inverse_code(code):
-    swapped = 4 + 2 * (code & 1) + ((code >> 1) & 1)
-    return jnp.where((code & 4) != 0, swapped, code)
+def turn_code(code, inverse):
+    first = code & 1
+    second = (code >> 1) & 1
+    swap = (code >> 2) & 1
+    if inverse:
+        first, second = (
+            jnp.where(swap != 0, second, first),
+            jnp.where(swap != 0, first, second),
+        )
+    return first * 56 + second * 7 + swap * 128
 
 
 def lane_pick(values, index):
     return jnp.take_along_axis(values, index, axis=1, mode="promise_in_bounds")
 
 
-def pair_flux(own, peer, code):
+def lane_source(turn):
+    lane = lax.broadcasted_iota(jnp.int32, turn.shape, 1)
+    swapped = ((lane & 7) << 3) | ((lane >> 3) & 7) | (lane & FACE)
+    return (jnp.where((turn & 128) != 0, swapped, lane) ^ turn) & (LANES - 1)
+
+
+def spread_metric(both):
+    low = lax.broadcasted_iota(jnp.int32, both.shape, 1) < FACE
+    return jnp.where(low, pltpu.roll(both, FACE, 1), both)
+
+
+def pair_flux(own, peer, turn):
     wm1, v1, g1 = own
     wm2, v2, g2 = peer
-    lane = lax.broadcasted_iota(jnp.int32, code.shape, 1)
-    low = lane < FACE
-    node = lane & (FACE - 1)
-    swapped = ((node & (NODES - 1)) << 3) | (node >> 3)
-    source = jnp.where((code & 4) != 0, swapped, node)
-    source = source ^ ((code & 1) * 56) ^ (((code >> 1) & 1) * 7)
-    source = source | (lane & FACE)
+    source = lane_source(turn)
+    low = lax.broadcasted_iota(jnp.int32, turn.shape, 1) < FACE
     penalty = NODES * (NODES + 1) / 2.0
     jump = v1 - lane_pick(v2, source)
     gap = g1 - lane_pick(g2, source)
@@ -133,10 +146,7 @@
     turned = pltpu.roll(total, FACE, 1)
     weight = 0.5 * jnp.where(low, total, turned)
     tau = (penalty * 0.5) * jnp.where(low, turned, total)
-    metric = jnp.where(low, pltpu.roll(wm1, FACE, 1), wm1)
-    value = weight * (tau * jump - 0.5 * gap)
-    lift = (-0.5 * weight * jump) * metric
-    return value, lift
+    return weight * (tau * jump - 0.5 * gap), -0.5 * weight * jump
 
 
 def row_numbers(slots, pairs, elems, staged, rows, sem):
@@ -150,7 +160,7 @@
     slot_total = slots.shape[2]
     pair_total = pairs.shape[1]
     raw = slots[4]
-    code = jnp.where(slots[3] != 0, raw, inverse_code(raw)) + 8 * slots[2]
+    code = jnp.where(slots[3] != 0, turn_code(raw, False), turn_code(raw, True)) + 256 * slots[2]
     pad[0:1, 0:slot_total] = code.astype(jnp.float32)
     pad[0:1, slot_total:] = jnp.zeros((1, pad.shape[1] - slot_total), jnp.float32)
     for t in range(pad.shape[1] // LANES):
@@ -158,7 +168,7 @@
         count = min(LANES, slot_total - t * LANES)
         cb[t * LANES : t * LANES + count, :] = row.T.astype(jnp.int32)[:count]
     local = pairs[4:5, :]
-    for side, codes in enumerate((local, inverse_code(local))):
+    for side, codes in enumerate((turn_code(local, False), turn_code(local, True))):
         for t in range(pair_total // LANES):
             row = codes[:, t * LANES : (t + 1) * LANES].astype(jnp.float32)
             start = slot_total + side * pair_total + t * LANES
@@ -315,8 +325,10 @@
     for copy in small[:2]:
         copy.start()
     loads = []
+    geo = []
     for t in range(tiles):
         cols = pl.ds(t * LANES, LANES)
+        geo.append(pltpu.make_async_copy(g_hbm.at[:, cols], g_s.at[t], geo_sem.at[t]))
         loads.append(
             [
                 pltpu.make_async_copy(fw_hbm.at[:, :, cols], fw_s.at[t], load_sem.at[t, 0]),
@@ -340,17 +352,15 @@
         fixed_tile(t, elems, fw_s, fm_s, tw)
     for t in range(tiles):
         loads[t][2].wait()
+        if t == tiles - 1:
+            for copy in geo + small[2:]:
+                copy.start()
         value_tile(t, elems, p_s, tv)
         slope_tile(t, elems, p_s, fm_s, tg)
-    geo = []
-    for t in range(tiles):
-        cols = pl.ds(t * LANES, LANES)
-        geo.append(pltpu.make_async_copy(g_hbm.at[:, cols], g_s.at[t], geo_sem.at[t]))
-        geo[-1].start()
-    for copy in small[2:]:
-        copy.start()
     for copy in numbers:
         copy.wait()
+    pl.semaphore_wait(barrier, len(others))
+    copies = []
     for k in others:
 
         def gather(n, carry, k=k):
@@ -363,24 +373,6 @@
             return carry
 
         lax.fori_loop(0, width // 16, gather, 0)
-    code_rows(slots, pairs, pad, cb)
-
-    for side, numbers in enumerate((rw1, rw2)):
-
-        def gather_local(n, carry, side=side, numbers=numbers):
-            base = n * 16
-            rows = [numbers[0, base + u] for u in range(16)]
-            for j in range(3):
-                found = [tables[j][pl.ds(row, 1), :] for row in rows]
-                for u in range(16):
-                    locals_[j][pl.ds(side * pair_total + base + u, 1), :] = found[u]
-            return carry
-
-        lax.fori_loop(0, pair_total // 16, gather_local, 0)
-
-    pl.semaphore_wait(barrier, len(others))
-    copies = []
-    for k in others:
         copies.append(
             pltpu.make_async_remote_copy(
                 src_ref=send.at[k],
@@ -392,20 +384,39 @@
             )
         )
         copies[-1].start()
+    code_rows(slots, pairs, pad, cb)
+
+    for side, numbers in enumerate((rw1, rw2)):
+
+        def gather_local(n, carry, side=side, numbers=numbers):
+            base = n * 16
+            rows = [numbers[0, base + u] for u in range(16)]
+            for j in range(3):
+                found = [tables[j][pl.ds(row, 1), :] for row in rows]
+                for u in range(16):
+                    locals_[j][pl.ds(side * pair_total + base + u, 1), :] = found[u]
+            return carry
+
+        lax.fori_loop(0, pair_total // 16, gather_local, 0)
+
+    group = min(pair_total, 2 * LANES)
 
     def local_flux(n, carry):
-        own = aligned(n * group, group)
-        other = aligned((n * group + pair_total) % (2 * pair_total), group)
+        one = aligned(n * group, group)
+        two = aligned(n * group + pair_total, group)
         rows = pl.ds(pl.multiple_of(n * group + slot_total, FACE), group)
-        value, lift = pair_flux(
-            [table[own, :] for table in locals_], [table[other, :] for table in locals_], cb[rows, :]
-        )
+        peers = pl.ds(pl.multiple_of(n * group + slot_total + pair_total, FACE), group)
+        first = [table[one, :] for table in locals_]
+        second = [table[two, :] for table in locals_]
+        value, lift = pair_flux(first, second, cb[rows, :])
         vb[rows, :] = value
-        hb[rows, :] = lift
+        hb[rows, :] = lift * spread_metric(first[0])
+        back = lane_source(cb[peers, :])
+        vb[peers, :] = -lane_pick(value, back)
+        hb[peers, :] = -lane_pick(lift, back) * spread_metric(second[0])
         return carry
 
-    group = 2 * LANES
-    lax.fori_loop(0, 2 * pair_total // group, local_flux, 0)
+    lax.fori_loop(0, pair_total // group, local_flux, 0)
     for copy in geo + small[2:]:
         copy.wait()
 
@@ -421,13 +432,12 @@
         for shift in (0, 1, 5, 6):
             k = 2 * n + shift
             rows = aligned(k * width, FACE)
-            codes = cb[rows, :]
-            value, lift = pair_flux(
-                [send[k, j] for j in range(3)], [recv[k, j] for j in range(3)], codes & 7
-            )
-            live = codes >= 8
+            turn = cb[rows, :]
+            own = [send[k, j] for j in range(3)]
+            value, lift = pair_flux(own, [recv[k, j] for j in range(3)], turn)
+            live = turn >= 256
             vb[rows, :] = jnp.where(live, value, 0.0)
-            hb[rows, :] = jnp.where(live, lift, 0.0)
+            hb[rows, :] = jnp.where(live, lift * spread_metric(own[0]), 0.0)
         return carry
 
     lax.fori_loop(0, 2, cross_flux, 0)

time: 36.9 us -> 35 us (0.949)
  Pallas kernels: 36 us -> 34 us
    pallas_call x1, Pallas kernels: 22 us -> 20 us  [on_device(): pl.pallas_call(functools.partial(front_kernel, n_blk, n_sub), in_specs=[o...]
where the time goes in v5:
time: 35 us; the launch traced here: 34.9 us
  Pallas kernels  34 us (97%)
  between operations  0.78 us (2%)
    pallas_call x1, Pallas kernels, on_device(): pl.pallas_call(functools.partial(front_kernel, n_blk, n_sub), in_specs=[o...  20 us
    pallas_call x1, Pallas kernels, on_device(): pl.pallas_call(combine_kernel, in_specs=[inside] * 8, out_specs=[inside]...  6.62 us
    pallas_call x1, Pallas kernels, on_device(): pl.pallas_call(functools.partial(reduce_kernel, n_sub), in_specs=[inside]...  5.58 us
    pallas_call x1, Pallas kernels, on_device(): pl.pallas_call(correct_kernel, grid=(elems // chunk,), in_specs=[whole((f...  1.81 us

profile of v5, /device:TPU:0, one launch (start us, length us, event | category | flops | bytes accessed | tf_op | source)
XLA Modules:
  0.0 34.9 jit_solution(18082520332161095816)
XLA Ops:
  0.6 0.0 copy-start.1
  0.6 0.0 copy-start.3
  0.7 0.0 copy-start.4
  0.7 0.0 copy-start.5
  0.7 0.0 copy-start.6
  0.7 20.0 %front.1 = (f32[4,1024,128]{2,1,0:T(8,128)S(1)}, f32[1600,128]{1,0:T(8,128)S(1)}, f32[1600,128]{1,0:T(8,128)S(1)}) custom-call(s32[5,1,576]{2,1,0:T(1,128)} %slots.1, s32[5,512]{1,0:T(8,128)} %pairs.1, f32[1024,512]{1,0:T(8,128)} %bitcast.9, f32[6,64,512]{2,1,0:T(8,128)} %bitcast.16, f32[6,64,512]{2,1,0:T(8,128)} %bitcast.17, f32[3072,512]{1,0:T(8,128)} %bitcast.14, ...), custom_call_target="tpu_custom_call" | custom-call | tf_op jit(solution)/shard_map/front/pallas_call | solution.py:680
  20.7 0.0 copy-done.1
  20.7 0.0 copy-done.3
  20.7 0.0 copy-done.4
  20.8 0.0 copy-done.5
  20.8 0.0 copy-done.6
  20.8 0.0 copy-start.7
  20.8 0.0 copy-start
  20.8 0.0 copy-start.2
  20.8 6.6 %combine.1 = (f32[2,8,64,512]{3,2,1,0:T(8,128)}, f32[16,512]{1,0:T(8,128)S(1)}) custom-call(s32[5,1,576]{2,1,0:T(1,128)S(1)} %copy-done.4, s32[5,512]{1,0:T(8,128)S(1)} %copy-done.3, f32[1600,128]{1,0:T(8,128)S(1)} %get-tuple-element.7.vb, f32[1600,128]{1,0:T(8,128)S(1)} %get-tuple-element.8.hb, f32[4,1024,128]{2,1,0:T(8,128)S(1)} %get-tuple-element.9.vol, ...), custom_call_target="tpu_custom_call" | custom-call | tf_op jit(solution)/shard_map/combine/pallas_call | solution.py:724
  27.4 0.0 copy-done.7
  27.4 5.6 %reduce.1.total_ref = f32[16,256]{1,0:T(8,128)S(1)} custom-call(f32[16,512]{1,0:T(8,128)S(1)} %get-tuple-element.11.coarse_ref, s32[1,512]{1,0:T(1,128)S(1)} %bitcast.12), custom_call_target="tpu_custom_call" | custom-call | tf_op jit(solution)/shard_map/reduce/pallas_call | solution.py:750
  33.0 0.0 copy-done
  33.0 0.0 copy-done.2
  33.1 1.8 %correct.1 = f32[2,8,64,512]{3,2,1,0:T(8,128)} custom-call(f32[16,256]{1,0:T(8,128)S(1)} %reduce.1.total_ref, f32[8,8,256]{2,1,0:T(8,128)S(1)} %copy-done.2, s32[1,512]{1,0:T(1,128)S(1)} %bitcast.13, f32[16,128]{1,0:T(8,128)S(1)} %copy-done.6, f32[2,8,64,512]{3,2,1,0:T(8,128)S(1)} %bitcast.10), custom_call_target="tpu_custom_call" | custom-call | tf_op jit(solution)/shard_map/correct/pallas_call | solution.py:766
Async XLA Ops:
  0.6 20.1 %copy-start.1 = (f32[2,8,8,8,512]{4,3,2,1,0:T(8,128)S(1)}, f32[2,8,8,8,512]{4,3,2,1,0:T(8,128)}, u32[]{:S(2)}) copy-start(f32[2,8,8,8,512]{4,3,2,1,0:T(8,128)} %param.14) | copy-start | bytes 6291460
  0.6 20.1 %copy-start.3 = (s32[5,512]{1,0:T(8,128)S(1)}, s32[5,512]{1,0:T(8,128)}, u32[]{:S(2)}) copy-start(s32[5,512]{1,0:T(8,128)} %pairs.1) | copy-start | bytes 30724
  0.7 20.1 %copy-start.4 = (s32[5,1,576]{2,1,0:T(1,128)S(1)}, s32[5,1,576]{2,1,0:T(1,128)}, u32[]{:S(2)}) copy-start(s32[5,1,576]{2,1,0:T(1,128)} %slots.1) | copy-start | bytes 34564
  0.7 20.1 %copy-start.5 = (bf16[64,192]{1,0:T(8,128)(2,1)S(1)}, bf16[64,192]{1,0:T(8,128)(2,1)}, u32[]{:S(2)}) copy-start(bf16[64,192]{1,0:T(8,128)(2,1)} %constant.11.clone.lift_ref) | copy-start | bytes 73732
  0.7 20.1 %copy-start.6 = (f32[16,128]{1,0:T(8,128)S(1)}, f32[16,128]{1,0:T(8,128)}, u32[]{:S(2)}) copy-start(f32[16,128]{1,0:T(8,128)} %constant.8.clone.modes.modes_ref) | copy-start | bytes 24580
  20.8 6.7 %copy-start.7 = (s32[512]{0:T(512)S(1)}, s32[512]{0:T(512)}, u32[]{:S(2)}) copy-start(s32[512]{0:T(512)} %param.20) | copy-start | bytes 6148
  20.8 12.2 %copy-start = (f32[2,8,8,8,512]{4,3,2,1,0:T(8,128)S(1)}, f32[2,8,8,8,512]{4,3,2,1,0:T(8,128)}, u32[]{:S(2)}) copy-start(f32[2,8,8,8,512]{4,3,2,1,0:T(8,128)} %param.13) | copy-start | bytes 6291460
  20.8 12.2 %copy-start.2 = (f32[8,8,256]{2,1,0:T(8,128)S(1)}, f32[8,8,256]{2,1,0:T(8,128)}, u32[]{:S(2)}) copy-start(f32[8,8,256]{2,1,0:T(8,128)} %inverse_ref.1) | copy-start | bytes 196612

commit v6 on v5

--- a/solution.py
+++ b/solution.py
@@ -235,7 +235,7 @@
             table[face_rows(face, t, elems), :] = slope.T
 
 
-def volume_half(h, p_s, g_s, fwd, bwd, out, s_ref):
+def volume_half(h, p_s, g_s, rhs_s, fwd, bwd, out, z, s_ref):
     fields = p_s.shape[1] // BRICK
     tiles = (2 * h, 2 * h + 1)
 
@@ -280,9 +280,16 @@
         f = n // NODES
         r = n % NODES
         where = [aligned(f * BRICK + k * FACE + r * NODES, NODES) for k in range(NODES)]
+        left = []
         for q, value in enumerate(even_odd(DERIV.T, [s_ref[rows, :] for rows in where])):
-            out[tiles[0], where[q], :] += value[:, :LANES]
-            out[tiles[1], where[q], :] += value[:, LANES:]
+            left.append(wide(rhs_s, where[q]) - (wide(out, where[q]) + value))
+            out[tiles[0], where[q], :] = left[q][:, :LANES]
+            out[tiles[1], where[q], :] = left[q][:, LANES:]
+        for a in range(2):
+            rows = aligned((2 * f + a) * FACE + r * NODES, NODES)
+            level = weighted(MODES[:, a], left)
+            z[tiles[0], rows, :] = level[:, :LANES]
+            z[tiles[1], rows, :] = level[:, LANES:]
         return carry
 
     lax.fori_loop(0, fields * NODES, last, 0, unroll=4)
@@ -290,9 +297,9 @@
 
 def front_kernel(
     n_blk, n_sub,
-    slots_hbm, pairs_hbm, p_hbm, fw_hbm, fm_hbm, g_hbm, fwd_hbm, bwd_hbm,
-    vol, vb, hb,
-    slots, pairs, fwd, bwd, p_s, fw_s, fm_s, g_s, s_ref, tv, tg, tw, la, lb, lc, cb, pad, send, recv,
+    slots_hbm, pairs_hbm, p_hbm, fw_hbm, fm_hbm, g_hbm, rhs_hbm, fwd_hbm, bwd_hbm,
+    rest, z, vb, hb,
+    slots, pairs, fwd, bwd, p_s, fw_s, fm_s, g_s, rhs_s, s_ref, tv, tg, tw, la, lb, lc, cb, pad, send, recv,
     st0, st1, st2, rw0, rw1, rw2,
     small_sem, load_sem, geo_sem, row_sem, send_sem, recv_sem,
 ):
@@ -328,7 +335,8 @@
     geo = []
     for t in range(tiles):
         cols = pl.ds(t * LANES, LANES)
-        geo.append(pltpu.make_async_copy(g_hbm.at[:, cols], g_s.at[t], geo_sem.at[t]))
+        geo.append(pltpu.make_async_copy(g_hbm.at[:, cols], g_s.at[t], geo_sem.at[t, 0]))
+        geo.append(pltpu.make_async_copy(rhs_hbm.at[:, cols], rhs_s.at[t], geo_sem.at[t, 1]))
         loads.append(
             [
                 pltpu.make_async_copy(fw_hbm.at[:, :, cols], fw_s.at[t], load_sem.at[t, 0]),
@@ -421,7 +429,7 @@
         copy.wait()
 
     def volume(h, carry):
-        volume_half(h, p_s, g_s, fwd, bwd, vol, s_ref)
+        volume_half(h, p_s, g_s, rhs_s, fwd, bwd, rest, z, s_ref)
         return carry
 
     lax.fori_loop(0, tiles // 2, volume, 0)
@@ -445,16 +453,10 @@
     hb[4 * width : 5 * width, :] = jnp.zeros((width, LANES), jnp.float32)
 
 
-def combine_kernel(
-    slots, pairs, vb, hb, vol, rhs, lift_ref, modes,
-    res, cs,
-    vt, lt, fv, fl, st0, st1, st2, rw0, rw1, rw2, row_sem,
-):
+def scatter_kernel(slots, pairs, vb, hb, vt, lt, st0, st1, st2, rw0, rw1, rw2, row_sem):
     elems = vt.shape[0] // 6
-    tiles = elems // LANES
     slot_total = slots.shape[2]
     pair_total = pairs.shape[1]
-    fields = 2
     numbers = row_numbers(slots, pairs, elems, (st0, st1, st2), (rw0, rw1, rw2), row_sem)
     for copy in numbers:
         copy.start()
@@ -486,6 +488,23 @@
 
         lax.fori_loop(0, count // 16, scatter, 0)
 
+
+def reduce_kernel(
+    n_sub,
+    vt, lt, rest, z, lift_ref, modes, cells,
+    total_ref, res,
+    fv, fl, cs, sums_ref, box, send_sem, recv_sem,
+):
+    elems = vt.shape[0] // 6
+    tiles = elems // LANES
+    fields = fv.shape[1]
+    place = lax.axis_index("blk")
+    sub = lax.axis_index("sub")
+    barrier = pltpu.get_barrier_semaphore()
+    peers = [(place, lax.rem(sub + step, n_sub)) for step in range(1, n_sub)]
+    for peer in peers:
+        pl.semaphore_signal(barrier, inc=1, device_id=peer, device_id_type=MESH)
+
     for face in range(6):
         for t in range(tiles):
             rows = slice(face * elems + t * LANES, face * elems + (t + 1) * LANES)
@@ -496,59 +515,50 @@
                 fl[t, f, face] = lift[f * FACE : (f + 1) * FACE]
 
     half = 2 * LANES
-
-    def finish(n, carry):
+    slopes = (-DERIV[0] @ MODES, DERIV[-1] @ MODES)
+
+    def halves(n):
         f = n // (tiles // 2)
         h = n % (tiles // 2)
-        cols = aligned(h * half, half)
 
         def wide(ref, *where):
             return jnp.concatenate([ref[2 * h, *where], ref[2 * h + 1, *where]], axis=-1)
 
-        low_lift = wide(fl, f, 0)
-        high_lift = wide(fl, f, 1)
-        coarse = [None, None]
-        for i in range(NODES):
-            part = slice(i * NODES, (i + 1) * NODES)
-            stack = []
-            for face in range(2, 6):
-                stack += [wide(fv, f, face, part), wide(fl, f, face, part)]
-            rows = aligned(f * BRICK + i * FACE, FACE)
-            value = rhs[f, i, :, cols] - wide(vol, rows)
-            value = value - product(lift_ref[...], jnp.concatenate(stack, axis=0))
-            value = value + float(DERIV[0, i]) * low_lift - float(DERIV[-1, i]) * high_lift
-            if i == 0:
-                value = value - wide(fv, f, 0)
-            if i == NODES - 1:
-                value = value - wide(fv, f, 1)
-            res[f, i, :, cols] = value
-            for a in range(2):
-                if MODES[i, a] != 0.0:
-                    term = float(MODES[i, a]) * value
-                    coarse[a] = term if coarse[a] is None else coarse[a] + term
+        return f, h, wide
+
+    def groups(layer):
+        return [layer[k * NODES : (k + 1) * NODES] for k in range(NODES)]
+
+    def restrict(n, carry):
+        f, h, wide = halves(n)
+        cols = aligned(h * half, half)
+        faces = []
+        for axis in range(3):
+            v0, l0 = wide(fv, f, 2 * axis), wide(fl, f, 2 * axis)
+            v1, l1 = wide(fv, f, 2 * axis + 1), wide(fl, f, 2 * axis + 1)
+            modes_here = []
+            for m in range(2):
+                level = float(slopes[0][m]) * l0 + float(slopes[1][m]) * l1
+                modes_here.append(level + (v0 if m == 0 else v1))
+            faces.append(modes_here)
         for a in range(2):
+            first = groups(wide(z, aligned((2 * f + a) * FACE, FACE)) - faces[0][a])
+            third = [weighted(MODES[:, a], groups(faces[2][c])) for c in range(2)]
             for b in range(2):
-                layers = [coarse[a][j * NODES : (j + 1) * NODES] for j in range(NODES)]
-                level = weighted(MODES[:, b], layers)
+                level = weighted(MODES[:, b], first) - weighted(MODES[:, a], groups(faces[1][b]))
                 for c in range(2):
                     column = modes[c * NODES : (c + 1) * NODES, 0:1]
+                    other = modes[b * NODES : (b + 1) * NODES, 0:1]
                     row = f * NODES + 4 * a + 2 * b + c
-                    cs[pl.ds(row, 1), cols] = jnp.sum(level * column, axis=0, keepdims=True)
+                    value = level * column - third[c] * other
+                    cs[pl.ds(row, 1), cols] = jnp.sum(value, axis=0, keepdims=True)
         return carry
 
-    lax.fori_loop(0, fields * tiles // 2, finish, 0)
-
-
-def reduce_kernel(n_sub, coarse_ref, cells, total_ref, sums_ref, box, send_sem, recv_sem):
-    place = lax.axis_index("blk")
-    sub = lax.axis_index("sub")
-    barrier = pltpu.get_barrier_semaphore()
-    peers = [(place, lax.rem(sub + step, n_sub)) for step in range(1, n_sub)]
-    for peer in peers:
-        pl.semaphore_signal(barrier, inc=1, device_id=peer, device_id_type=MESH)
+    lax.fori_loop(0, fields * tiles // 2, restrict, 0)
+
     row_cells = sums_ref.shape[1]
-    coarse = coarse_ref[...]
-    hot = lax.broadcasted_iota(jnp.int32, (row_cells, coarse.shape[1]), 0) == cells[...]
+    coarse = cs[...]
+    hot = lax.broadcasted_iota(jnp.int32, (row_cells, elems), 0) == cells[...]
     hot = hot.astype(jnp.float32).astype(jnp.bfloat16)
     high = coarse.astype(jnp.bfloat16)
     low = (coarse - high.astype(jnp.float32)).astype(jnp.bfloat16)
@@ -573,6 +583,28 @@
             )
         )
         copies[-1].start()
+
+    def finish(n, carry):
+        f, h, wide = halves(n)
+        low_lift = wide(fl, f, 0)
+        high_lift = wide(fl, f, 1)
+        for i in range(NODES):
+            part = slice(i * NODES, (i + 1) * NODES)
+            stack = []
+            for face in range(2, 6):
+                stack += [wide(fv, f, face, part), wide(fl, f, face, part)]
+            rows = aligned(f * BRICK + i * FACE, FACE)
+            value = wide(rest, rows) - product(lift_ref[...], jnp.concatenate(stack, axis=0))
+            value = value + float(DERIV[0, i]) * low_lift - float(DERIV[-1, i]) * high_lift
+            if i == 0:
+                value = value - wide(fv, f, 0)
+            if i == NODES - 1:
+                value = value - wide(fv, f, 1)
+            res[2 * h, rows, :] = value[:, :LANES]
+            res[2 * h + 1, rows, :] = value[:, LANES:]
+        return carry
+
+    lax.fori_loop(0, fields * tiles // 2, finish, 0)
     for copy in copies:
         copy.wait()
     total = sums_ref[...]
@@ -581,7 +613,19 @@
     total_ref[...] = total
 
 
-def correct_kernel(total_ref, inverse_ref, cells_ref, modes_ref, p_ref, out_ref):
+def correct_kernel(
+    total_ref, inverse_ref, cells_ref, modes_ref, p_ref, tiled, out_ref, res_hbm, res_sem
+):
+    copies = [
+        pltpu.make_async_copy(tiled.at[t], res_hbm.at[:, pl.ds(t * LANES, LANES)], res_sem.at[t])
+        for t in range(tiled.shape[0])
+    ]
+
+    @pl.when(pl.program_id(0) == 0)
+    def _():
+        for copy in copies:
+            copy.start()
+
     fields = p_ref.shape[0]
     elems = p_ref.shape[-1]
     row_cells = total_ref.shape[1]
@@ -620,6 +664,11 @@
             for i in range(NODES):
                 grown = weighted(MODES[i], [planes[0][j], planes[1][j]])
                 out_ref[f, i, part, :] = p_ref[f, i, part, :] + grown
+
+    @pl.when(pl.program_id(0) == pl.num_programs(0) - 1)
+    def _():
+        for copy in copies:
+            copy.wait()
 
 
 def whole(shape, space=VMEM):
@@ -677,11 +726,16 @@
     ]
     dma = pltpu.SemaphoreType.DMA
 
-    volume, values, lifts = pl.pallas_call(
+    rest, levels, values, lifts = pl.pallas_call(
         functools.partial(front_kernel, n_blk, n_sub),
-        in_specs=[outside] * 8,
-        out_specs=[inside] * 3,
-        out_shape=[shaped(tiles, rows, LANES), shaped(side_total, LANES), shaped(side_total, LANES)],
+        in_specs=[outside] * 9,
+        out_specs=[inside] * 4,
+        out_shape=[
+            shaped(tiles, rows, LANES),
+            shaped(tiles, 2 * fields * FACE, LANES),
+            shaped(side_total, LANES),
+            shaped(side_total, LANES),
+        ],
         scratch_shapes=[
             pltpu.VMEM(cross_slots.shape, i32),
             pltpu.VMEM(local_pairs.shape, i32),
@@ -691,6 +745,7 @@
             pltpu.VMEM((tiles, 6, FACE, LANES), f32),
             pltpu.VMEM((tiles, 6, FACE, LANES), f32),
             pltpu.VMEM((tiles, 6 * BRICK, LANES), f32),
+            pltpu.VMEM((tiles, rows, LANES), f32),
             pltpu.VMEM((rows, 2 * LANES), f32),
         ]
         + [pltpu.VMEM((6 * elems, LANES), f32)] * 3
@@ -702,7 +757,7 @@
             pltpu.VMEM((9, 3, width, LANES), f32),
         ]
         + number_scratch
-        + [dma((4,)), dma((tiles, 3)), dma((tiles,)), dma((3,)), dma((9,)), dma((9,))],
+        + [dma((4,)), dma((tiles, 3)), dma((tiles, 2)), dma((3,)), dma((9,)), dma((9,))],
         compiler_params=limits(36, collective_id=0, has_side_effects=True),
         name="front",
     )(
@@ -715,55 +770,43 @@
                 weights,
                 metrics,
                 geometry.reshape(6 * BRICK, elems),
+                right_side.reshape(rows, elems),
                 jnp.asarray(forward_table()),
                 jnp.asarray(backward_table()),
             )
         ]
     )
 
-    residual, coarse = pl.pallas_call(
-        combine_kernel,
-        in_specs=[inside] * 8,
+    value_table, lift_rows = pl.pallas_call(
+        scatter_kernel,
+        in_specs=[inside] * 4,
         out_specs=[inside] * 2,
-        out_shape=[shaped(*slabs), shaped(fields * NODES, elems)],
+        out_shape=[shaped(6 * elems, LANES), shaped(6 * elems, LANES)],
+        scratch_shapes=number_scratch + [dma((3,))],
+        compiler_params=limits(8),
+        name="scatter",
+    )(cross_slots, local_pairs, values, lifts)
+
+    totals, tiled = pl.pallas_call(
+        functools.partial(reduce_kernel, n_sub),
+        in_specs=[inside] * 7,
+        out_specs=[inside] * 2,
+        out_shape=[shaped(fields * NODES, row_cells), shaped(tiles, rows, LANES)],
         scratch_shapes=[
-            pltpu.VMEM((6 * elems, LANES), f32),
-            pltpu.VMEM((6 * elems, LANES), f32),
             pltpu.VMEM((tiles, fields, 6, FACE, LANES), f32),
             pltpu.VMEM((tiles, fields, 6, FACE, LANES), f32),
-        ]
-        + number_scratch
-        + [dma((3,))],
-        compiler_params=limits(32),
-        name="combine",
-    )(
-        cross_slots,
-        local_pairs,
-        values,
-        lifts,
-        volume,
-        right_side.reshape(slabs),
-        jnp.asarray(lift_table()),
-        modes,
-    )
-
-    totals = pl.pallas_call(
-        functools.partial(reduce_kernel, n_sub),
-        in_specs=[inside] * 2,
-        out_specs=inside,
-        out_shape=shaped(fields * NODES, row_cells),
-        scratch_shapes=[
+            pltpu.VMEM((fields * NODES, elems), f32),
             pltpu.VMEM((fields * NODES, row_cells), f32),
             pltpu.VMEM((n_sub - 1, fields * NODES, row_cells), f32),
             dma((n_sub - 1,)),
             dma((n_sub - 1,)),
         ],
-        compiler_params=limits(8, collective_id=1, has_side_effects=True),
+        compiler_params=limits(24, collective_id=1, has_side_effects=True),
         name="reduce",
-    )(coarse, cells)
+    )(value_table, lift_rows, rest, levels, jnp.asarray(lift_table()), modes, cells)
 
     chunk = min(elems, 256)
-    corrected = pl.pallas_call(
+    corrected, residual = pl.pallas_call(
         correct_kernel,
         grid=(elems // chunk,),
         in_specs=[
@@ -772,12 +815,17 @@
             pl.BlockSpec((1, chunk), lambda t: (0, t)),
             whole((2 * NODES, LANES)),
             pl.BlockSpec((fields, NODES, FACE, chunk), lambda t: (0, 0, 0, t)),
+            pl.BlockSpec(memory_space=pl.ANY),
         ],
-        out_specs=pl.BlockSpec((fields, NODES, FACE, chunk), lambda t: (0, 0, 0, t)),
-        out_shape=shaped(*slabs),
-        compiler_params=limits(32),
+        out_specs=[
+            pl.BlockSpec((fields, NODES, FACE, chunk), lambda t: (0, 0, 0, t)),
+            pl.BlockSpec(memory_space=pl.ANY),
+        ],
+        out_shape=[shaped(*slabs), shaped(rows, elems)],
+        scratch_shapes=[dma((tiles,))],
+        compiler_params=limits(16),
         name="correct",
-    )(totals, coarse_inverse, cells, modes, p)
+    )(totals, coarse_inverse, cells, modes, p, tiled)
     return residual.reshape(pressure.shape), corrected.reshape(pressure.shape)
 
 

time: 35 us -> 32.2 us (0.920)
  Pallas kernels: 34 us -> 31.2 us
    pallas_call x1, Pallas kernels: 6.62 us -> 2.75 us  [on_device(): pl.pallas_call(scatter_kernel, in_specs=[inside] * 4, out_specs=[inside]...]
    pallas_call x1, Pallas kernels: 1.81 us -> 2.49 us  [on_device(): pl.pallas_call(correct_kernel, grid=(elems // chunk,), in_specs=[whole((f...]
    pallas_call x1, Pallas kernels: 20 us -> 20.4 us  [on_device(): pl.pallas_call(functools.partial(front_kernel, n_blk, n_sub), in_specs=[o...]
where the time goes in v6:
time: 32.2 us; the launch traced here: 32 us
  Pallas kernels  31.2 us (97%)
  between operations  0.77 us (2%)
    pallas_call x1, Pallas kernels, on_device(): pl.pallas_call(functools.partial(front_kernel, n_blk, n_sub), in_specs=[o...  20.4 us
    pallas_call x1, Pallas kernels, on_device(): pl.pallas_call(functools.partial(reduce_kernel, n_sub), in_specs=[inside]...  5.58 us
    pallas_call x1, Pallas kernels, on_device(): pl.pallas_call(scatter_kernel, in_specs=[inside] * 4, out_specs=[inside]...  2.75 us
    pallas_call x1, Pallas kernels, on_device(): pl.pallas_call(correct_kernel, grid=(elems // chunk,), in_specs=[whole((f...  2.49 us

profile of v6, /device:TPU:0, one launch (start us, length us, event | category | flops | bytes accessed | tf_op | source)
XLA Modules:
  0.0 32.0 jit_solution(5669430610117073653)
XLA Ops:
  0.6 0.0 copy-start.2
  0.6 0.0 copy-start.3
  0.7 0.0 copy-start.4
  0.7 0.0 copy-start.5
  0.7 0.0 copy-start.6
  0.7 20.4 %front.1 = (f32[4,1024,128]{2,1,0:T(8,128)S(1)}, f32[4,256,128]{2,1,0:T(8,128)S(1)}, f32[1600,128]{1,0:T(8,128)S(1)}, f32[1600,128]{1,0:T(8,128)S(1)}) custom-call(s32[5,1,576]{2,1,0:T(1,128)} %slots.1, s32[5,512]{1,0:T(8,128)} %pairs.1, f32[1024,512]{1,0:T(8,128)} %bitcast.9, f32[6,64,512]{2,1,0:T(8,128)} %bitcast.15, f32[6,64,512]{2,1,0:T(8,128)} %bitcast.16, ...), custom_call_target="tpu_custom_call" | custom-call | tf_op jit(solution)/shard_map/front/pallas_call | solution.py:729
  21.1 0.0 copy-done.2
  21.1 0.0 copy-done.3
  21.1 2.8 %scatter.1 = (f32[3072,128]{1,0:T(8,128)S(1)}, f32[3072,128]{1,0:T(8,128)S(1)}) custom-call(s32[5,1,576]{2,1,0:T(1,128)S(1)} %copy-done.3, s32[5,512]{1,0:T(8,128)S(1)} %copy-done.2, f32[1600,128]{1,0:T(8,128)S(1)} %get-tuple-element.12.vb, f32[1600,128]{1,0:T(8,128)S(1)} %get-tuple-element.13.hb), custom_call_target="tpu_custom_call" | custom-call | tf_op jit(solution)/shard_map/scatter/pallas_call | solution.py:780
  23.9 0.0 copy-done.4
  23.9 0.0 copy-done.5
  23.9 0.0 copy-done.6
  23.9 0.0 copy-start
  23.9 0.0 copy-start.1
  23.9 5.6 %reduce.1 = (f32[16,256]{1,0:T(8,128)S(1)}, f32[4,1024,128]{2,1,0:T(8,128)S(1)}) custom-call(f32[3072,128]{1,0:T(8,128)S(1)} %get-tuple-element.14.vt, f32[3072,128]{1,0:T(8,128)S(1)} %get-tuple-element.15.lt, f32[4,1024,128]{2,1,0:T(8,128)S(1)} %get-tuple-element.16.rest, f32[4,256,128]{2,1,0:T(8,128)S(1)} %get-tuple-element.17.z, ...), custom_call_target="tpu_custom_call" | custom-call | tf_op jit(solution)/shard_map/reduce/pallas_call | solution.py:790
  29.5 0.0 copy-done
  29.5 0.0 copy-done.1
  29.5 2.5 %correct.1 = (f32[2,8,64,512]{3,2,1,0:T(8,128)}, f32[1024,512]{1,0:T(8,128)}) custom-call(f32[16,256]{1,0:T(8,128)S(1)} %get-tuple-element.18.total_ref, f32[8,8,256]{2,1,0:T(8,128)S(1)} %copy-done.1, s32[1,512]{1,0:T(1,128)S(1)} %bitcast.12, f32[16,128]{1,0:T(8,128)S(1)} %copy-done.5, f32[2,8,64,512]{3,2,1,0:T(8,128)S(1)} %bitcast.10, ...), custom_call_target="tpu_custom_call" | custom-call | tf_op jit(solution)/shard_map/correct/pallas_call | solution.py:809
Async XLA Ops:
  0.6 20.5 %copy-start.2 = (s32[5,512]{1,0:T(8,128)S(1)}, s32[5,512]{1,0:T(8,128)}, u32[]{:S(2)}) copy-start(s32[5,512]{1,0:T(8,128)} %pairs.1) | copy-start | bytes 30724
  0.6 20.5 %copy-start.3 = (s32[5,1,576]{2,1,0:T(1,128)S(1)}, s32[5,1,576]{2,1,0:T(1,128)}, u32[]{:S(2)}) copy-start(s32[5,1,576]{2,1,0:T(1,128)} %slots.1) | copy-start | bytes 34564
  0.7 23.2 %copy-start.4 = (bf16[64,192]{1,0:T(8,128)(2,1)S(1)}, bf16[64,192]{1,0:T(8,128)(2,1)}, u32[]{:S(2)}) copy-start(bf16[64,192]{1,0:T(8,128)(2,1)} %constant.11.clone.lift_ref) | copy-start | bytes 73732
  0.7 23.2 %copy-start.5 = (f32[16,128]{1,0:T(8,128)S(1)}, f32[16,128]{1,0:T(8,128)}, u32[]{:S(2)}) copy-start(f32[16,128]{1,0:T(8,128)} %constant.8.clone.modes.modes_ref) | copy-start | bytes 24580
  0.7 23.2 %copy-start.6 = (s32[512]{0:T(512)S(1)}, s32[512]{0:T(512)}, u32[]{:S(2)}) copy-start(s32[512]{0:T(512)} %param.20) | copy-start | bytes 6148
  23.9 5.6 %copy-start = (f32[2,8,8,8,512]{4,3,2,1,0:T(8,128)S(1)}, f32[2,8,8,8,512]{4,3,2,1,0:T(8,128)}, u32[]{:S(2)}) copy-start(f32[2,8,8,8,512]{4,3,2,1,0:T(8,128)} %param.13) | copy-start | bytes 6291460
  23.9 5.6 %copy-start.1 = (f32[8,8,256]{2,1,0:T(8,128)S(1)}, f32[8,8,256]{2,1,0:T(8,128)}, u32[]{:S(2)}) copy-start(f32[8,8,256]{2,1,0:T(8,128)} %inverse_ref.1) | copy-start | bytes 196612

commit v7 on v6

--- a/solution.py
+++ b/solution.py
@@ -274,7 +274,7 @@
             out[tiles[1], rows, :] = r23[:, LANES:]
         return carry
 
-    lax.fori_loop(0, NODES, middle, 0, unroll=4)
+    lax.fori_loop(0, NODES, middle, 0, unroll=8)
 
     def last(n, carry):
         f = n // NODES
@@ -367,8 +367,6 @@
         slope_tile(t, elems, p_s, fm_s, tg)
     for copy in numbers:
         copy.wait()
-    pl.semaphore_wait(barrier, len(others))
-    copies = []
     for k in others:
 
         def gather(n, carry, k=k):
@@ -381,6 +379,9 @@
             return carry
 
         lax.fori_loop(0, width // 16, gather, 0)
+    pl.semaphore_wait(barrier, len(others))
+    copies = []
+    for k in others:
         copies.append(
             pltpu.make_async_remote_copy(
                 src_ref=send.at[k],
@@ -433,22 +434,19 @@
         return carry
 
     lax.fori_loop(0, tiles // 2, volume, 0)
-    for copy in copies:
-        copy.wait()
-
-    def cross_flux(n, carry):
-        for shift in (0, 1, 5, 6):
-            k = 2 * n + shift
-            rows = aligned(k * width, FACE)
+    for first in range(0, len(others), 2):
+        for copy in copies[first : first + 2]:
+            copy.wait()
+        for k in others[first : first + 2]:
+            k = 8 - k
+            rows = slice(k * width, (k + 1) * width)
             turn = cb[rows, :]
             own = [send[k, j] for j in range(3)]
             value, lift = pair_flux(own, [recv[k, j] for j in range(3)], turn)
             live = turn >= 256
             vb[rows, :] = jnp.where(live, value, 0.0)
             hb[rows, :] = jnp.where(live, lift * spread_metric(own[0]), 0.0)
-        return carry
-
-    lax.fori_loop(0, 2, cross_flux, 0)
+
     vb[4 * width : 5 * width, :] = jnp.zeros((width, LANES), jnp.float32)
     hb[4 * width : 5 * width, :] = jnp.zeros((width, LANES), jnp.float32)
 

time: 32.2 us -> 31 us (0.963)
  Pallas kernels: 31.2 us -> 30.1 us
    pallas_call x1, Pallas kernels: 20.4 us -> 19.2 us  [on_device(): pl.pallas_call(functools.partial(front_kernel, n_blk, n_sub), in_specs=[o...]
where the time goes in v7:
time: 31 us; the launch traced here: 30.9 us
  Pallas kernels  30.1 us (97%)
  between operations  0.77 us (2%)
    pallas_call x1, Pallas kernels, on_device(): pl.pallas_call(functools.partial(front_kernel, n_blk, n_sub), in_specs=[o...  19.2 us
    pallas_call x1, Pallas kernels, on_device(): pl.pallas_call(functools.partial(reduce_kernel, n_sub), in_specs=[inside]...  5.58 us
    pallas_call x1, Pallas kernels, on_device(): pl.pallas_call(scatter_kernel, in_specs=[inside] * 4, out_specs=[inside]...  2.75 us
    pallas_call x1, Pallas kernels, on_device(): pl.pallas_call(correct_kernel, grid=(elems // chunk,), in_specs=[whole((f...  2.49 us

profile of v7, /device:TPU:0, one launch (start us, length us, event | category | flops | bytes accessed | tf_op | source)
XLA Modules:
  0.0 30.9 jit_solution(16471562098706148211)
XLA Ops:
  0.6 0.0 copy-start.2
  0.6 0.0 copy-start.3
  0.7 0.0 copy-start.4
  0.7 0.0 copy-start.5
  0.7 0.0 copy-start.6
  0.7 19.2 %front.1 = (f32[4,1024,128]{2,1,0:T(8,128)S(1)}, f32[4,256,128]{2,1,0:T(8,128)S(1)}, f32[1600,128]{1,0:T(8,128)S(1)}, f32[1600,128]{1,0:T(8,128)S(1)}) custom-call(s32[5,1,576]{2,1,0:T(1,128)} %slots.1, s32[5,512]{1,0:T(8,128)} %pairs.1, f32[1024,512]{1,0:T(8,128)} %bitcast.9, f32[6,64,512]{2,1,0:T(8,128)} %bitcast.15, f32[6,64,512]{2,1,0:T(8,128)} %bitcast.16, ...), custom_call_target="tpu_custom_call" | custom-call | tf_op jit(solution)/shard_map/front/pallas_call | solution.py:727
  19.9 0.0 copy-done.2
  20.0 0.0 copy-done.3
  20.0 2.8 %scatter.1 = (f32[3072,128]{1,0:T(8,128)S(1)}, f32[3072,128]{1,0:T(8,128)S(1)}) custom-call(s32[5,1,576]{2,1,0:T(1,128)S(1)} %copy-done.3, s32[5,512]{1,0:T(8,128)S(1)} %copy-done.2, f32[1600,128]{1,0:T(8,128)S(1)} %get-tuple-element.12.vb, f32[1600,128]{1,0:T(8,128)S(1)} %get-tuple-element.13.hb), custom_call_target="tpu_custom_call" | custom-call | tf_op jit(solution)/shard_map/scatter/pallas_call | solution.py:778
  22.7 0.0 copy-done.4
  22.7 0.0 copy-done.5
  22.7 0.0 copy-done.6
  22.8 0.0 copy-start
  22.8 0.0 copy-start.1
  22.8 5.6 %reduce.1 = (f32[16,256]{1,0:T(8,128)S(1)}, f32[4,1024,128]{2,1,0:T(8,128)S(1)}) custom-call(f32[3072,128]{1,0:T(8,128)S(1)} %get-tuple-element.14.vt, f32[3072,128]{1,0:T(8,128)S(1)} %get-tuple-element.15.lt, f32[4,1024,128]{2,1,0:T(8,128)S(1)} %get-tuple-element.16.rest, f32[4,256,128]{2,1,0:T(8,128)S(1)} %get-tuple-element.17.z, ...), custom_call_target="tpu_custom_call" | custom-call | tf_op jit(solution)/shard_map/reduce/pallas_call | solution.py:788
  28.4 0.0 copy-done
  28.4 0.0 copy-done.1
  28.4 2.5 %correct.1 = (f32[2,8,64,512]{3,2,1,0:T(8,128)}, f32[1024,512]{1,0:T(8,128)}) custom-call(f32[16,256]{1,0:T(8,128)S(1)} %get-tuple-element.18.total_ref, f32[8,8,256]{2,1,0:T(8,128)S(1)} %copy-done.1, s32[1,512]{1,0:T(1,128)S(1)} %bitcast.12, f32[16,128]{1,0:T(8,128)S(1)} %copy-done.5, f32[2,8,64,512]{3,2,1,0:T(8,128)S(1)} %bitcast.10, ...), custom_call_target="tpu_custom_call" | custom-call | tf_op jit(solution)/shard_map/correct/pallas_call | solution.py:807
Async XLA Ops:
  0.6 19.3 %copy-start.2 = (s32[5,512]{1,0:T(8,128)S(1)}, s32[5,512]{1,0:T(8,128)}, u32[]{:S(2)}) copy-start(s32[5,512]{1,0:T(8,128)} %pairs.1) | copy-start | bytes 30724
  0.6 19.3 %copy-start.3 = (s32[5,1,576]{2,1,0:T(1,128)S(1)}, s32[5,1,576]{2,1,0:T(1,128)}, u32[]{:S(2)}) copy-start(s32[5,1,576]{2,1,0:T(1,128)} %slots.1) | copy-start | bytes 34564
  0.7 22.1 %copy-start.4 = (bf16[64,192]{1,0:T(8,128)(2,1)S(1)}, bf16[64,192]{1,0:T(8,128)(2,1)}, u32[]{:S(2)}) copy-start(bf16[64,192]{1,0:T(8,128)(2,1)} %constant.11.clone.lift_ref) | copy-start | bytes 73732
  0.7 22.1 %copy-start.5 = (f32[16,128]{1,0:T(8,128)S(1)}, f32[16,128]{1,0:T(8,128)}, u32[]{:S(2)}) copy-start(f32[16,128]{1,0:T(8,128)} %constant.8.clone.modes.modes_ref) | copy-start | bytes 24580
  0.7 22.1 %copy-start.6 = (s32[512]{0:T(512)S(1)}, s32[512]{0:T(512)}, u32[]{:S(2)}) copy-start(s32[512]{0:T(512)} %param.20) | copy-start | bytes 6148
  22.8 5.6 %copy-start = (f32[2,8,8,8,512]{4,3,2,1,0:T(8,128)S(1)}, f32[2,8,8,8,512]{4,3,2,1,0:T(8,128)}, u32[]{:S(2)}) copy-start(f32[2,8,8,8,512]{4,3,2,1,0:T(8,128)} %param.13) | copy-start | bytes 6291460
  22.8 5.6 %copy-start.1 = (f32[8,8,256]{2,1,0:T(8,128)S(1)}, f32[8,8,256]{2,1,0:T(8,128)}, u32[]{:S(2)}) copy-start(f32[8,8,256]{2,1,0:T(8,128)} %inverse_ref.1) | copy-start | bytes 196612

commit v8 on v7

--- a/solution.py
+++ b/solution.py
@@ -612,21 +612,20 @@
 
 
 def correct_kernel(
-    total_ref, inverse_ref, cells_ref, modes_ref, p_ref, tiled, out_ref, res_hbm, res_sem
+    total_ref, inverse_ref, cells_ref, modes_ref, p_ref, tiled,
+    out_hbm, res_hbm,
+    out_s, res_sem, out_sem,
 ):
+    fields = p_ref.shape[0]
+    elems = p_ref.shape[-1]
+    row_cells = total_ref.shape[1]
+    half = 2 * LANES
     copies = [
         pltpu.make_async_copy(tiled.at[t], res_hbm.at[:, pl.ds(t * LANES, LANES)], res_sem.at[t])
         for t in range(tiled.shape[0])
     ]
-
-    @pl.when(pl.program_id(0) == 0)
-    def _():
-        for copy in copies:
-            copy.start()
-
-    fields = p_ref.shape[0]
-    elems = p_ref.shape[-1]
-    row_cells = total_ref.shape[1]
+    for copy in copies:
+        copy.start()
     rows = []
     for f in range(fields):
         level = None
@@ -637,40 +636,39 @@
     level = jnp.concatenate(rows, axis=0)
     high = level.astype(jnp.bfloat16)
     low = (level - high.astype(jnp.float32)).astype(jnp.bfloat16)
-    hot = lax.broadcasted_iota(jnp.int32, (row_cells, elems), 0) == cells_ref[...]
-    hot = hot.astype(jnp.float32).astype(jnp.bfloat16)
-    spread = lax.dot_general(
-        jnp.concatenate([high, low], axis=0),
-        hot,
-        (((1,), (0,)), ((), ())),
-        preferred_element_type=jnp.float32,
-    )
-    spread = spread[: level.shape[0]] + spread[level.shape[0] :]
+    both = jnp.concatenate([high, low], axis=0)
     columns = [modes_ref[c * NODES : (c + 1) * NODES, 0:1] for c in range(2)]
-    for f in range(fields):
-        planes = []
-        for a in range(2):
-            lines = []
-            for b in range(2):
-                start = f * NODES + 4 * a + 2 * b
-                lines.append(
-                    columns[0] * spread[start : start + 1] + columns[1] * spread[start + 1 : start + 2]
-                )
-            planes.append([weighted(MODES[j], lines) for j in range(NODES)])
-        for j in range(NODES):
-            part = slice(j * NODES, (j + 1) * NODES)
-            for i in range(NODES):
-                grown = weighted(MODES[i], [planes[0][j], planes[1][j]])
-                out_ref[f, i, part, :] = p_ref[f, i, part, :] + grown
-
-    @pl.when(pl.program_id(0) == pl.num_programs(0) - 1)
-    def _():
-        for copy in copies:
-            copy.wait()
-
-
-def whole(shape, space=VMEM):
-    return pl.BlockSpec(shape, lambda *_: (0,) * len(shape), memory_space=space)
+    for h in range(elems // half):
+        cols = slice(h * half, (h + 1) * half)
+        hot = lax.broadcasted_iota(jnp.int32, (row_cells, half), 0) == cells_ref[:, cols]
+        hot = hot.astype(jnp.float32).astype(jnp.bfloat16)
+        spread = lax.dot_general(
+            both, hot, (((1,), (0,)), ((), ())), preferred_element_type=jnp.float32
+        )
+        spread = spread[: level.shape[0]] + spread[level.shape[0] :]
+        for f in range(fields):
+            planes = []
+            for a in range(2):
+                lines = []
+                for b in range(2):
+                    start = f * NODES + 4 * a + 2 * b
+                    lines.append(
+                        columns[0] * spread[start : start + 1]
+                        + columns[1] * spread[start + 1 : start + 2]
+                    )
+                planes.append([weighted(MODES[j], lines) for j in range(NODES)])
+            for j in range(NODES):
+                part = slice(j * NODES, (j + 1) * NODES)
+                for i in range(NODES):
+                    grown = weighted(MODES[i], [planes[0][j], planes[1][j]])
+                    out_s[f, i, part, cols] = p_ref[f, i, part, cols] + grown
+            where = (f, slice(None), slice(None), pl.ds(h * half, half))
+            copies.append(
+                pltpu.make_async_copy(out_s.at[where], out_hbm.at[where], out_sem.at[h, f])
+            )
+            copies[-1].start()
+    for copy in copies:
+        copy.wait()
 
 
 def limits(mib, **extra):
@@ -803,24 +801,16 @@
         name="reduce",
     )(value_table, lift_rows, rest, levels, jnp.asarray(lift_table()), modes, cells)
 
-    chunk = min(elems, 256)
     corrected, residual = pl.pallas_call(
         correct_kernel,
-        grid=(elems // chunk,),
-        in_specs=[
-            whole((fields * NODES, row_cells)),
-            whole((NODES, NODES, row_cells)),
-            pl.BlockSpec((1, chunk), lambda t: (0, t)),
-            whole((2 * NODES, LANES)),
-            pl.BlockSpec((fields, NODES, FACE, chunk), lambda t: (0, 0, 0, t)),
-            pl.BlockSpec(memory_space=pl.ANY),
+        in_specs=[inside] * 5 + [pl.BlockSpec(memory_space=pl.ANY)],
+        out_specs=[outside] * 2,
+        out_shape=[shaped(*slabs), shaped(rows, elems)],
+        scratch_shapes=[
+            pltpu.VMEM(slabs, f32),
+            dma((tiles,)),
+            dma((elems // (2 * LANES), fields)),
         ],
-        out_specs=[
-            pl.BlockSpec((fields, NODES, FACE, chunk), lambda t: (0, 0, 0, t)),
-            pl.BlockSpec(memory_space=pl.ANY),
-        ],
-        out_shape=[shaped(*slabs), shaped(rows, elems)],
-        scratch_shapes=[dma((tiles,))],
         compiler_params=limits(16),
         name="correct",
     )(totals, coarse_inverse, cells, modes, p, tiled)

time: 31 us -> 30.9 us (level)
  no operation moved by 1% of the time
where the time goes in v8:
time: 30.9 us; the launch traced here: 30.8 us
  Pallas kernels  29.9 us (97%)
  between operations  0.77 us (2%)
    pallas_call x1, Pallas kernels, on_device(): pl.pallas_call(functools.partial(front_kernel, n_blk, n_sub), in_specs=[o...  19.2 us
    pallas_call x1, Pallas kernels, on_device(): pl.pallas_call(functools.partial(reduce_kernel, n_sub), in_specs=[inside]...  5.58 us
    pallas_call x1, Pallas kernels, on_device(): pl.pallas_call(scatter_kernel, in_specs=[inside] * 4, out_specs=[inside]...  2.75 us
    pallas_call x1, Pallas kernels, on_device(): pl.pallas_call(correct_kernel, in_specs=[inside] * 5 + [pl.BlockSpec(memo...  2.37 us

profile of v8, /device:TPU:0, one launch (start us, length us, event | category | flops | bytes accessed | tf_op | source)
XLA Modules:
  0.0 30.8 jit_solution(2627881007745819717)
XLA Ops:
  0.6 0.0 copy-start.2
  0.6 0.0 copy-start.3
  0.7 0.0 copy-start.4
  0.7 0.0 copy-start.5
  0.7 0.0 copy-start.6
  0.7 19.2 %front.1 = (f32[4,1024,128]{2,1,0:T(8,128)S(1)}, f32[4,256,128]{2,1,0:T(8,128)S(1)}, f32[1600,128]{1,0:T(8,128)S(1)}, f32[1600,128]{1,0:T(8,128)S(1)}) custom-call(s32[5,1,576]{2,1,0:T(1,128)} %slots.1, s32[5,512]{1,0:T(8,128)} %pairs.1, f32[1024,512]{1,0:T(8,128)} %bitcast.9, f32[6,64,512]{2,1,0:T(8,128)} %bitcast.15, f32[6,64,512]{2,1,0:T(8,128)} %bitcast.16, ...), custom_call_target="tpu_custom_call" | custom-call | tf_op jit(solution)/shard_map/front/pallas_call | solution.py:725
  19.9 0.0 copy-done.2
  20.0 0.0 copy-done.3
  20.0 2.8 %scatter.1 = (f32[3072,128]{1,0:T(8,128)S(1)}, f32[3072,128]{1,0:T(8,128)S(1)}) custom-call(s32[5,1,576]{2,1,0:T(1,128)S(1)} %copy-done.3, s32[5,512]{1,0:T(8,128)S(1)} %copy-done.2, f32[1600,128]{1,0:T(8,128)S(1)} %get-tuple-element.12.vb, f32[1600,128]{1,0:T(8,128)S(1)} %get-tuple-element.13.hb), custom_call_target="tpu_custom_call" | custom-call | tf_op jit(solution)/shard_map/scatter/pallas_call | solution.py:776
  22.7 0.0 copy-done.4
  22.7 0.0 copy-done.5
  22.7 0.0 copy-done.6
  22.8 0.0 copy-start
  22.8 0.0 copy-start.1
  22.8 5.6 %reduce.1 = (f32[16,256]{1,0:T(8,128)S(1)}, f32[4,1024,128]{2,1,0:T(8,128)S(1)}) custom-call(f32[3072,128]{1,0:T(8,128)S(1)} %get-tuple-element.14.vt, f32[3072,128]{1,0:T(8,128)S(1)} %get-tuple-element.15.lt, f32[4,1024,128]{2,1,0:T(8,128)S(1)} %get-tuple-element.16.rest, f32[4,256,128]{2,1,0:T(8,128)S(1)} %get-tuple-element.17.z, ...), custom_call_target="tpu_custom_call" | custom-call | tf_op jit(solution)/shard_map/reduce/pallas_call | solution.py:786
  28.4 0.0 copy-done
  28.4 0.0 copy-done.1
  28.4 2.4 %correct.1 = (f32[2,8,64,512]{3,2,1,0:T(8,128)}, f32[1024,512]{1,0:T(8,128)}) custom-call(f32[16,256]{1,0:T(8,128)S(1)} %get-tuple-element.18.total_ref, f32[8,8,256]{2,1,0:T(8,128)S(1)} %copy-done.1, s32[1,512]{1,0:T(1,128)S(1)} %bitcast.12, f32[16,128]{1,0:T(8,128)S(1)} %copy-done.5, f32[2,8,64,512]{3,2,1,0:T(8,128)S(1)} %bitcast.10, ...), custom_call_target="tpu_custom_call" | custom-call | tf_op jit(solution)/shard_map/correct/pallas_call | solution.py:804
Async XLA Ops:
  0.6 19.3 %copy-start.2 = (s32[5,512]{1,0:T(8,128)S(1)}, s32[5,512]{1,0:T(8,128)}, u32[]{:S(2)}) copy-start(s32[5,512]{1,0:T(8,128)} %pairs.1) | copy-start | bytes 30724
  0.6 19.3 %copy-start.3 = (s32[5,1,576]{2,1,0:T(1,128)S(1)}, s32[5,1,576]{2,1,0:T(1,128)}, u32[]{:S(2)}) copy-start(s32[5,1,576]{2,1,0:T(1,128)} %slots.1) | copy-start | bytes 34564
  0.7 22.1 %copy-start.4 = (bf16[64,192]{1,0:T(8,128)(2,1)S(1)}, bf16[64,192]{1,0:T(8,128)(2,1)}, u32[]{:S(2)}) copy-start(bf16[64,192]{1,0:T(8,128)(2,1)} %constant.11.clone.lift_ref) | copy-start | bytes 73732
  0.7 22.1 %copy-start.5 = (f32[16,128]{1,0:T(8,128)S(1)}, f32[16,128]{1,0:T(8,128)}, u32[]{:S(2)}) copy-start(f32[16,128]{1,0:T(8,128)} %constant.8.clone.modes.modes_ref) | copy-start | bytes 24580
  0.7 22.1 %copy-start.6 = (s32[512]{0:T(512)S(1)}, s32[512]{0:T(512)}, u32[]{:S(2)}) copy-start(s32[512]{0:T(512)} %param.20) | copy-start | bytes 6148
  22.8 5.6 %copy-start = (f32[2,8,8,8,512]{4,3,2,1,0:T(8,128)S(1)}, f32[2,8,8,8,512]{4,3,2,1,0:T(8,128)}, u32[]{:S(2)}) copy-start(f32[2,8,8,8,512]{4,3,2,1,0:T(8,128)} %param.13) | copy-start | bytes 6291460
  22.8 5.6 %copy-start.1 = (f32[8,8,256]{2,1,0:T(8,128)S(1)}, f32[8,8,256]{2,1,0:T(8,128)}, u32[]{:S(2)}) copy-start(f32[8,8,256]{2,1,0:T(8,128)} %inverse_ref.1) | copy-start | bytes 196612

commit v9 on v8

--- a/solution.py
+++ b/solution.py
@@ -393,8 +393,6 @@
             )
         )
         copies[-1].start()
-    code_rows(slots, pairs, pad, cb)
-
     for side, numbers in enumerate((rw1, rw2)):
 
         def gather_local(n, carry, side=side, numbers=numbers):
@@ -408,7 +406,8 @@
 
         lax.fori_loop(0, pair_total // 16, gather_local, 0)
 
-    group = min(pair_total, 2 * LANES)
+    code_rows(slots, pairs, pad, cb)
+    group = pair_total
 
     def local_flux(n, carry):
         one = aligned(n * group, group)
@@ -476,15 +475,15 @@
     ):
 
         def scatter(n, carry, start=start, numbers=numbers):
-            base = n * 16
-            rows = [numbers[0, base + u] for u in range(16)]
+            base = n * 32
+            rows = [numbers[0, base + u] for u in range(32)]
             for source, table in ((vb, vt), (hb, lt)):
-                found = [source[pl.ds(start + base + u, 1), :] for u in range(16)]
-                for u in range(16):
+                found = [source[pl.ds(start + base + u, 1), :] for u in range(32)]
+                for u in range(32):
                     table[pl.ds(rows[u], 1), :] = found[u]
             return carry
 
-        lax.fori_loop(0, count // 16, scatter, 0)
+        lax.fori_loop(0, count // 32, scatter, 0)
 
 
 def reduce_kernel(

time: 30.9 us -> 30.7 us (level)
  no operation moved by 1% of the time
where the time goes in v9:
time: 30.7 us; the launch traced here: 30.6 us
  Pallas kernels  29.8 us (97%)
  between operations  0.77 us (3%)
    pallas_call x1, Pallas kernels, on_device(): pl.pallas_call(functools.partial(front_kernel, n_blk, n_sub), in_specs=[o...  19.2 us
    pallas_call x1, Pallas kernels, on_device(): pl.pallas_call(functools.partial(reduce_kernel, n_sub), in_specs=[inside]...  5.58 us
    pallas_call x1, Pallas kernels, on_device(): pl.pallas_call(scatter_kernel, in_specs=[inside] * 4, out_specs=[inside]...  2.58 us
    pallas_call x1, Pallas kernels, on_device(): pl.pallas_call(correct_kernel, in_specs=[inside] * 5 + [pl.BlockSpec(memo...  2.37 us

profile of v9, /device:TPU:0, one launch (start us, length us, event | category | flops | bytes accessed | tf_op | source)
XLA Modules:
  0.0 30.6 jit_solution(5216266548548157891)
XLA Ops:
  0.6 0.0 copy-start.2
  0.6 0.0 copy-start.3
  0.7 0.0 copy-start.4
  0.7 0.0 copy-start.5
  0.7 0.0 copy-start.6
  0.7 19.2 %front.1 = (f32[4,1024,128]{2,1,0:T(8,128)S(1)}, f32[4,256,128]{2,1,0:T(8,128)S(1)}, f32[1600,128]{1,0:T(8,128)S(1)}, f32[1600,128]{1,0:T(8,128)S(1)}) custom-call(s32[5,1,576]{2,1,0:T(1,128)} %slots.1, s32[5,512]{1,0:T(8,128)} %pairs.1, f32[1024,512]{1,0:T(8,128)} %bitcast.9, f32[6,64,512]{2,1,0:T(8,128)} %bitcast.15, f32[6,64,512]{2,1,0:T(8,128)} %bitcast.16, ...), custom_call_target="tpu_custom_call" | custom-call | tf_op jit(solution)/shard_map/front/pallas_call | solution.py:724
  19.9 0.0 copy-done.2
  20.0 0.0 copy-done.3
  20.0 2.6 %scatter.1 = (f32[3072,128]{1,0:T(8,128)S(1)}, f32[3072,128]{1,0:T(8,128)S(1)}) custom-call(s32[5,1,576]{2,1,0:T(1,128)S(1)} %copy-done.3, s32[5,512]{1,0:T(8,128)S(1)} %copy-done.2, f32[1600,128]{1,0:T(8,128)S(1)} %get-tuple-element.12.vb, f32[1600,128]{1,0:T(8,128)S(1)} %get-tuple-element.13.hb), custom_call_target="tpu_custom_call" | custom-call | tf_op jit(solution)/shard_map/scatter/pallas_call | solution.py:775
  22.5 0.0 copy-done.4
  22.6 0.0 copy-done.5
  22.6 0.0 copy-done.6
  22.6 0.0 copy-start
  22.6 0.0 copy-start.1
  22.6 5.6 %reduce.1 = (f32[16,256]{1,0:T(8,128)S(1)}, f32[4,1024,128]{2,1,0:T(8,128)S(1)}) custom-call(f32[3072,128]{1,0:T(8,128)S(1)} %get-tuple-element.14.vt, f32[3072,128]{1,0:T(8,128)S(1)} %get-tuple-element.15.lt, f32[4,1024,128]{2,1,0:T(8,128)S(1)} %get-tuple-element.16.rest, f32[4,256,128]{2,1,0:T(8,128)S(1)} %get-tuple-element.17.z, ...), custom_call_target="tpu_custom_call" | custom-call | tf_op jit(solution)/shard_map/reduce/pallas_call | solution.py:785
  28.2 0.0 copy-done
  28.2 0.0 copy-done.1
  28.2 2.4 %correct.1 = (f32[2,8,64,512]{3,2,1,0:T(8,128)}, f32[1024,512]{1,0:T(8,128)}) custom-call(f32[16,256]{1,0:T(8,128)S(1)} %get-tuple-element.18.total_ref, f32[8,8,256]{2,1,0:T(8,128)S(1)} %copy-done.1, s32[1,512]{1,0:T(1,128)S(1)} %bitcast.12, f32[16,128]{1,0:T(8,128)S(1)} %copy-done.5, f32[2,8,64,512]{3,2,1,0:T(8,128)S(1)} %bitcast.10, ...), custom_call_target="tpu_custom_call" | custom-call | tf_op jit(solution)/shard_map/correct/pallas_call | solution.py:803
Async XLA Ops:
  0.6 19.3 %copy-start.2 = (s32[5,512]{1,0:T(8,128)S(1)}, s32[5,512]{1,0:T(8,128)}, u32[]{:S(2)}) copy-start(s32[5,512]{1,0:T(8,128)} %pairs.1) | copy-start | bytes 30724
  0.6 19.3 %copy-start.3 = (s32[5,1,576]{2,1,0:T(1,128)S(1)}, s32[5,1,576]{2,1,0:T(1,128)}, u32[]{:S(2)}) copy-start(s32[5,1,576]{2,1,0:T(1,128)} %slots.1) | copy-start | bytes 34564
  0.7 21.9 %copy-start.4 = (bf16[64,192]{1,0:T(8,128)(2,1)S(1)}, bf16[64,192]{1,0:T(8,128)(2,1)}, u32[]{:S(2)}) copy-start(bf16[64,192]{1,0:T(8,128)(2,1)} %constant.11.clone.lift_ref) | copy-start | bytes 73732
  0.7 21.9 %copy-start.5 = (f32[16,128]{1,0:T(8,128)S(1)}, f32[16,128]{1,0:T(8,128)}, u32[]{:S(2)}) copy-start(f32[16,128]{1,0:T(8,128)} %constant.8.clone.modes.modes_ref) | copy-start | bytes 24580
  0.7 21.9 %copy-start.6 = (s32[512]{0:T(512)S(1)}, s32[512]{0:T(512)}, u32[]{:S(2)}) copy-start(s32[512]{0:T(512)} %param.20) | copy-start | bytes 6148
  22.6 5.6 %copy-start = (f32[2,8,8,8,512]{4,3,2,1,0:T(8,128)S(1)}, f32[2,8,8,8,512]{4,3,2,1,0:T(8,128)}, u32[]{:S(2)}) copy-start(f32[2,8,8,8,512]{4,3,2,1,0:T(8,128)} %param.13) | copy-start | bytes 6291460
  22.6 5.6 %copy-start.1 = (f32[8,8,256]{2,1,0:T(8,128)S(1)}, f32[8,8,256]{2,1,0:T(8,128)}, u32[]{:S(2)}) copy-start(f32[8,8,256]{2,1,0:T(8,128)} %inverse_ref.1) | copy-start | bytes 196612
